TPU v7x, 512 devices: a whole 4x4x16 slice. The times are simulated.
512 devices in a mesh: dp: 32 (over x, y, core), tok: 16 (over z).
Axes of the slice: x: 4, y: 4, z: 16, core: 2. Of those that a mesh axis runs over, the one named last changes fastest.
Arguments:
- student_hidden: bfloat16 [64, 1024, 2048], P('dp', 'tok'), may hold values from -48 to 48
- teacher_values: bfloat16 [64, 1024, 4096], P('dp', 'tok'), may hold values from -48 to 48
- value_weight: bfloat16 [2048, 2048], P(None, 'tok'), may hold values from -0.09375 to 0.09375
- value_bias: bfloat16 [1, 2048], P(None, 'tok'), may hold values from -3 to 3
Outputs:
- hidden_grad: bfloat16 [64, 1024, 2048], P('dp', 'tok')
- bias_grad: float32 [2048], P('tok')
All inputs are finite; a program needn't handle non-finite values.
Results may differ from a plain program's by a relative error of at most 0.012.
The roundings to bfloat16 on the way count: a program that leaves them out, or rounds other values in their place, can miss the bound.
Values may be sent and summed in bfloat16 or wider, within the bound.
No kernel may reach another device: no remote copies, remote signals or barrier semaphores. Data moves between devices by JAX's collectives and lax.ppermute only.
A program may use at most 64 MiB of HBM per device.

v0:
```python
import math

import jax
import jax.numpy as jnp
from jax import lax
from jax.sharding import PartitionSpec as P

SH = 64
TH = 128


def pair_grads(student_head, teacher_head):
    length = student_head.shape[0]
    block = min(512, length)
    total = jnp.zeros(student_head.shape, jnp.float32)
    contract = (((1,), (1,)), ((), ()))
    for number in range(length // block):
        lower = number * block
        query_student = student_head[lower : lower + block]
        query_teacher = teacher_head[lower : lower + block]
        teacher_scores = lax.dot_general(
            query_teacher, teacher_head, contract, preferred_element_type=jnp.float32
        ) / jnp.sqrt(jnp.float32(TH))
        teacher_prob = jax.nn.softmax(teacher_scores, axis=-1)
        student_scores = lax.dot_general(
            query_student, student_head, contract, preferred_element_type=jnp.float32
        ) / jnp.sqrt(jnp.float32(SH))
        student_prob = jax.nn.softmax(student_scores, axis=-1)
        score_grad = (length * (student_prob - teacher_prob)).astype(jnp.bfloat16)
        total = total.at[lower : lower + block].add(
            jnp.dot(score_grad, student_head, preferred_element_type=jnp.float32)
        )
        total = total + lax.dot_general(
            score_grad, query_student, (((0,), (0,)), ((), ())), preferred_element_type=jnp.float32
        )
    return (total / jnp.sqrt(jnp.float32(SH))).astype(jnp.bfloat16)


def body(student_hidden, teacher_values, value_weight, value_bias):
    seq_count, local_len, width = student_hidden.shape
    local_cols = value_weight.shape[1]
    rows = student_hidden.reshape(seq_count * local_len, width)
    whole_weight, whole_bias = (
        lax.all_gather(value_weight, "tok", axis=1, tiled=True),
        lax.all_gather(value_bias, "tok", axis=1, tiled=True),
    )
    student_values = (
        jnp.dot(rows, whole_weight, preferred_element_type=jnp.float32)
        + whole_bias.astype(jnp.float32)
    ).astype(jnp.bfloat16)
    value_width = student_values.shape[1]
    student_values = student_values.reshape(seq_count, local_len, value_width)
    student_heads, teacher_heads = (
        lax.all_to_all(student_values, "tok", split_axis=2, concat_axis=1, tiled=True),
        lax.all_to_all(teacher_values, "tok", split_axis=2, concat_axis=1, tiled=True),
    )
    length = student_heads.shape[1]
    head_count = student_heads.shape[2] // SH
    student_items = (
        student_heads.reshape(seq_count, length, head_count, SH)
        .transpose(0, 2, 1, 3)
        .reshape(seq_count * head_count, length, SH)
    )
    teacher_items = (
        teacher_heads.reshape(seq_count, length, head_count, TH)
        .transpose(0, 2, 1, 3)
        .reshape(seq_count * head_count, length, TH)
    )
    grads = lax.map(lambda pair: pair_grads(pair[0], pair[1]), (student_items, teacher_items))
    head_grad = (
        grads.reshape(seq_count, head_count, length, SH)
        .transpose(0, 2, 1, 3)
        .reshape(seq_count, length, head_count * SH)
    )
    token_count = seq_count * length * lax.axis_size("dp")
    value_grad = lax.all_to_all(head_grad, "tok", split_axis=1, concat_axis=2, tiled=True)
    grad_rows = value_grad.reshape(seq_count * local_len, value_width)
    total_sum = lax.psum(jnp.sum(grad_rows.astype(jnp.float32), axis=0), ("dp", "tok"))
    bias_grad = lax.dynamic_slice_in_dim(
        total_sum, lax.axis_index("tok") * local_cols, local_cols
    ) / math.sqrt(token_count)
    hidden_grad = lax.dot_general(
        grad_rows, whole_weight, (((1,), (1,)), ((), ())), preferred_element_type=jnp.float32
    )
    hidden_grad = hidden_grad.astype(jnp.bfloat16).reshape(seq_count, local_len, width)
    return (hidden_grad, bias_grad)


def solution(mesh):
    placed = (P("dp", "tok", None), P("dp", "tok", None), P(None, "tok"), P(None, "tok"))
    return jax.shard_map(
        body,
        mesh=mesh,
        in_specs=placed,
        out_specs=(P("dp", "tok", None), P("tok")),
        check_vma=False,
    )
```

profile of v0, /device:TPU:1, one launch (start us, length us, event | category | flops | bytes accessed | tf_op | source)
XLA Modules:
  0.0 422.1 jit_solution(5664726289387013947)
XLA Ops:
  7.9 5.0 %copy.19 = bf16[2,64,4096]{1,0,2:T(2,128)(2,1)S(1)} copy(bf16[2,64,4096]{2,1,0:T(8,128)(2,1)} %param.11) | data formatting | bytes 2097152 | tf_op args[1]
  13.0 2.3 reshape.130
  15.3 15.7 %all-to-all-start.1 = ((bf16[16,2,16384]{2,1,0:T(2,128)(2,1)}), bf16[16,2,16384]{2,1,0:T(2,128)(2,1)S(1)}, u32[]{:S(2)}, u32[]{:S(2)}) async-start(bf16[16,2,16384]{2,1,0:T(2,128)(2,1)} %reshape.130), calls=%async_computation.1 | async-start | bytes 2097152 | tf_op jit(solution)/shard_map/all_to_all | solution.py:55
  31.1 76.6 %all_gather.7 = bf16[1,2048]{1,0:T(2,128)(2,1)S(1)} all-gather(bf16[1,128]{1,0:T(2,128)(2,1)S(1)} %copy-done.6), channel_id=1, replica_groups=mesh['dp'=32,'tok'=16] {'tok'}, dimensions={1}, use_global_device_ids=true | all-gather | bytes 4352 | tf_op jit(solution)/shard_map/all_gather | solution.py:45
  107.6 72.0 %all-gather.2.cloned.1.call-done = bf16[2048,2048]{1,0:T(8,128)(2,1)} async-done(((bf16[2048,128]{1,0:T(8,128)(2,1)}), bf16[2048,2048]{1,0:T(8,128)(2,1)}) %all-gather.2.cloned.1.call-update) | async-done | bytes 8388624 | tf_op jit(solution)/shard_map/all_gather | solution.py:44
  179.6 4.6 %fusion.29 = bf16[128,2048]{1,0:T(8,128)(2,1)S(1)} fusion(bf16[128,2048]{1,0:T(8,128)(2,1)S(1)} %bitcast.135, bf16[2048,2048]{1,0:T(8,128)(2,1)} %all-gather.2.cloned.1.call-done, f32[2048]{0:T(1024)S(1)} %bitcast.151), kind=kOutput, calls=%fused_computation.47 | convolution fusion | flops 1074266112 | bytes 9445376 | tf_op jit(solution)/shard_map/dot_general | solution.py:48
  185.0 1.5 reshape.128
  186.6 6.6 %all-to-all-start = ((bf16[16,2,8192]{2,1,0:T(2,128)(2,1)}), bf16[16,2,8192]{2,1,0:T(2,128)(2,1)}, u32[]{:S(2)}, u32[]{:S(2)}) async-start(bf16[16,2,8192]{2,1,0:T(2,128)(2,1)} %reshape.128), calls=%async_computation | async-start | bytes 1048576 | tf_op jit(solution)/shard_map/all_to_all | solution.py:54
  193.2 5.0 %reshape.131 = bf16[4096,2,64]{2,1,0:T(2,128)(2,1)S(1)} reshape(bf16[16,2,16384]{2,1,0:T(2,128)(2,1)} %copy-done.3) | data formatting | bytes 2097152
  198.2 3.5 copy.20
  203.1 6.8 %all-to-all-done = bf16[16,2,8192]{2,1,0:T(2,128)(2,1)} async-done(((bf16[16,2,8192]{2,1,0:T(2,128)(2,1)}), bf16[16,2,8192]{2,1,0:T(2,128)(2,1)}, u32[]{:S(2)}, u32[]{:S(2)}) %all-to-all-start) | async-done | bytes 524320 | tf_op jit(solution)/shard_map/all_to_all | solution.py:54
  209.9 3.0 reshape.129
  212.9 1.7 copy.37
  214.7 1.9 reshape.119
  216.6 42.4 %while.15 = (s32[]{:T(128)}, bf16[4,1024,64]{1,2,0:T(8,128)(2,1)}, bf16[4,1024,64]{1,2,0:T(8,128)(2,1)S(1)}, bf16[4,1024,128]{2,1,0:T(8,128)(2,1)S(1)}, s32[]{:T(128)}, /*index=5*/s32[]{:T(128)}, s32[]{}) while((s32[]{:T(128)}, bf16[4,1024,64]{1,2,0:T(8,128)(2,1)}, bf16[4,1024,64]{1,2,0:T(8,128)(2,1)S(1)}, ...), condition=%wide.region_9.10_spmd, body=%wide.region_0.9_spmd.sunk | while | flops 691269632 | bytes 47622872 | solution.py:69
  222.1 1.6 multiply_reduce_fusion.11
  232.7 1.6 multiply_reduce_fusion.11
  243.3 1.6 multiply_reduce_fusion.11
  253.9 1.6 multiply_reduce_fusion.11
  259.1 2.0 copy.23
  261.1 13.5 %all-to-all-start.2 = ((bf16[2,1024,128]{2,0,1:T(2,128)(2,1)}), bf16[2,1024,128]{2,0,1:T(2,128)(2,1)S(1)}, u32[]{:S(2)}, u32[]{:S(2)}) async-start(bf16[2,1024,128]{2,0,1:T(2,128)(2,1)} %copy.23), calls=%async_computation.2 | async-start | bytes 1048576 | tf_op jit(solution)/shard_map/all_to_all | solution.py:76
  274.6 20.6 %all-to-all-done.2 = bf16[2,1024,128]{2,0,1:T(2,128)(2,1)S(1)} async-done(((bf16[2,1024,128]{2,0,1:T(2,128)(2,1)}), bf16[2,1024,128]{2,0,1:T(2,128)(2,1)S(1)}, u32[]{:S(2)}, u32[]{:S(2)}) %all-to-all-start.2) | async-done | bytes 524320 | tf_op jit(solution)/shard_map/all_to_all | solution.py:76
  295.7 111.9 %psum.7 = f32[2048]{0:T(1024)S(1)} all-reduce(f32[2048]{0:T(1024)S(1)} %bitcast.152), channel_id=1, replica_groups=mesh['dp'=32,'tok'=16] {'dp','tok'}, use_global_device_ids=true, to_apply=%region_11.12 | all-reduce | flops 2048 | bytes 16384 | tf_op jit(solution)/shard_map/psum | solution.py:78
  408.2 7.1 %convolution_convert_fusion = bf16[128,2048]{1,0:T(8,128)(2,1)} fusion(bf16[2048,2048]{1,0:T(8,128)(2,1)} %all-gather.2.cloned.1.call-done, bf16[16,8,16,128]{3,2,1,0:T(8,128)(2,1)S(1)} %bitcast.148), kind=kOutput, calls=%fused_computation.46 | convolution fusion | flops 1074003968 | bytes 9437184 | tf_op jit(solution)/shard_map/dot_general | solution.py:82
  (110 shorter events, 39.9 us)
Async XLA Ops:
  7.2 172.5 %copy-start = (bf16[2,64,2048]{2,1,0:T(8,128)(2,1)S(1)}, bf16[2,64,2048]{2,1,0:T(8,128)(2,1)}, u32[]{:S(2)}) copy-start(bf16[2,64,2048]{2,1,0:T(8,128)(2,1)} %param.10) | copy-start | bytes 1572868
  7.2 172.4 %all-gather.2.cloned.1.call-start = ((), (), s32[]{:S(2)}) async-start(), calls=%async_computation.3 | async-start | bytes 8912896 | tf_op jit(solution)/shard_map/all_gather | solution.py:44
  13.0 18.1 %copy-start.6 = (bf16[1,128]{1,0:T(2,128)(2,1)S(1)}, bf16[1,128]{1,0:T(2,128)(2,1)}, u32[]{:S(2)}) copy-start(bf16[1,128]{1,0:T(2,128)(2,1)} %param.13) | copy-start | bytes 772
  15.3 171.2 %all-to-all-start.1 = ((bf16[16,2,16384]{2,1,0:T(2,128)(2,1)}), bf16[16,2,16384]{2,1,0:T(2,128)(2,1)S(1)}, u32[]{:S(2)}, u32[]{:S(2)}) async-start(bf16[16,2,16384]{2,1,0:T(2,128)(2,1)} %reshape.130), calls=%async_computation.1 | async-start | bytes 2097152 | tf_op jit(solution)/shard_map/all_to_all | solution.py:55
  186.5 6.6 %copy-start.3 = (bf16[16,2,16384]{2,1,0:T(2,128)(2,1)}, bf16[16,2,16384]{2,1,0:T(2,128)(2,1)S(1)}, u32[]{:S(2)}) copy-start(bf16[16,2,16384]{2,1,0:T(2,128)(2,1)S(1)} %all-to-all-done.1) | copy-start | bytes 3145732
  186.6 23.4 %all-to-all-start = ((bf16[16,2,8192]{2,1,0:T(2,128)(2,1)}), bf16[16,2,8192]{2,1,0:T(2,128)(2,1)}, u32[]{:S(2)}, u32[]{:S(2)}) async-start(bf16[16,2,8192]{2,1,0:T(2,128)(2,1)} %reshape.128), calls=%async_computation | async-start | bytes 1048576 | tf_op jit(solution)/shard_map/all_to_all | solution.py:54
  216.7 0.8 copy-start.4
  216.7 2.0 copy-start.1
  225.7 1.5 copy-start.2
  225.8 1.5 copy-start.5
  227.3 0.8 copy-start.4
  227.3 2.0 copy-start.1
  236.4 1.5 copy-start.2
  236.4 1.5 copy-start.5
  237.9 0.8 copy-start.4
  237.9 2.0 copy-start.1
  247.0 1.5 copy-start.2
  247.0 1.5 copy-start.5
  248.5 0.8 copy-start.4
  248.5 2.0 copy-start.1
  257.6 1.5 copy-start.2
  257.6 1.5 copy-start.5
  261.1 34.1 %all-to-all-start.2 = ((bf16[2,1024,128]{2,0,1:T(2,128)(2,1)}), bf16[2,1024,128]{2,0,1:T(2,128)(2,1)S(1)}, u32[]{:S(2)}, u32[]{:S(2)}) async-start(bf16[2,1024,128]{2,0,1:T(2,128)(2,1)} %copy.23), calls=%async_computation.2 | async-start | bytes 1048576 | tf_op jit(solution)/shard_map/all_to_all | solution.py:76
Sparse Core Ops, SparseCore 0:
  10.0 169.5 all-gather.1
where the time goes:
time: 423 us; the launch traced here: 422 us
  blocking collectives  188 us (44%)
  waiting for transfers between devices  100 us (24%)
  starting transfers between devices  35.9 us (8%)
  matrix products  33 us (8%)
  local copies, waits for them, and re-layouts  32.9 us (8%)
  other arithmetic  17.2 us (4%)
  between operations  14.2 us (3%)
    psum x1, blocking collectives, body(): lax.psum(jnp.sum(grad_rows.astype(jnp.float32), axis=0), ('dp', 'tok'))  112 us
    all_gather x1, blocking collectives, body(): lax.all_gather(value_bias, 'tok', axis=1, tiled=True)  76.6 us
    all_gather x1, waiting for transfers between devices, body(): lax.all_gather(value_weight, 'tok', axis=1, tiled=True)  72 us
    all_to_all x1, waiting for transfers between devices, body(): lax.all_to_all(head_grad, 'tok', split_axis=1, concat_axis=2, tiled=True)  20.6 us
    unnamed x11, local copies, waits for them, and re-layouts  16.9 us
    all_to_all x1, starting transfers between devices, body(): lax.all_to_all(teacher_values, 'tok', split_axis=2, concat_axis=1, tiled=...  15.7 us
    all_to_all x1, starting transfers between devices, body(): lax.all_to_all(head_grad, 'tok', split_axis=1, concat_axis=2, tiled=True)  13.5 us
    convert_element_type x8, other arithmetic, pair_grads(): score_grad = (length * (student_prob - teacher_prob)).astype(jnp.bfloat16)  8.92 us
  transfers between devices with their start and end apart: 4, of which 3 were waited for; matrix products, arithmetic and copies ran while one was open for 6% of the time, Pallas kernels for 0%

commit v1 on v0

v1 whole, which is shorter than its diff:
```python
import functools
import math

import jax
import jax.numpy as jnp
from jax import lax
from jax.experimental import pallas as pl
from jax.experimental.pallas import tpu as pltpu
from jax.sharding import PartitionSpec as P

SH = 64
TH = 128
LOG2E = 1.4426950408889634
NT = (((1,), (1,)), ((), ()))
TN = (((0,), (0,)), ((), ()))
NN = (((1,), (0,)), ((), ()))
F32 = jnp.float32
BF16 = jnp.bfloat16


def dot(a, b, dims):
    return lax.dot_general(a, b, dims, preferred_element_type=F32)


def params(mib):
    return pltpu.CompilerParams(vmem_limit_bytes=mib << 20)


def split_columns(x, parts):
    rows, width = x.shape
    cols = width // parts

    def kernel(x_ref, o_ref):
        o_ref[0] = x_ref[...]

    return pl.pallas_call(
        kernel,
        grid=(parts,),
        in_specs=[pl.BlockSpec((rows, cols), lambda t: (0, t))],
        out_specs=pl.BlockSpec((1, rows, cols), lambda t: (t, 0, 0)),
        out_shape=jax.ShapeDtypeStruct((parts, rows, cols), x.dtype),
        name="split_columns",
    )(x)


def project(hidden, weight, bias):
    seqs, toks, width = hidden.shape
    groups, blocks, depth, cols = weight.shape
    pair = 2

    def kernel(h_ref, w_ref, b_ref, *outs):
        h = h_ref[...].reshape(seqs * toks, width)
        w = jnp.concatenate(
            [w_ref[:, k].reshape(groups * depth, cols) for k in range(pair)], axis=1
        )
        r = dot(h, w, NN)
        for k in range(pair):
            v = (r[:, k * cols : (k + 1) * cols] + b_ref[k].astype(F32)).astype(BF16)
            for s in range(seqs):
                outs[s][k] = v[s * toks : (s + 1) * toks]

    return pl.pallas_call(
        kernel,
        grid=(blocks // pair,),
        in_specs=[
            pl.BlockSpec((seqs, toks, width), lambda t: (0, 0, 0)),
            pl.BlockSpec((groups, pair, depth, cols), lambda t: (0, t, 0, 0)),
            pl.BlockSpec((pair, 1, cols), lambda t: (t, 0, 0)),
        ],
        out_specs=[pl.BlockSpec((pair, toks, cols), lambda t: (t, 0, 0))] * seqs,
        out_shape=[jax.ShapeDtypeStruct((blocks, toks, cols), BF16)] * seqs,
        compiler_params=params(32),
        cost_estimate=pl.CostEstimate(
            flops=2 * seqs * toks * width * blocks * cols,
            bytes_accessed=2 * width * blocks * cols,
            transcendentals=0,
        ),
        name="project",
    )(hidden, weight, bias)


def soft(scores, scale, total):
    peak = jnp.max(scores, axis=1, keepdims=True)
    e = jnp.exp2((scores - peak) * scale)
    return e * (total / jnp.sum(e, axis=1, keepdims=True))


def teacher_probs(teacher, seqs):
    blocks, rows, width = teacher.shape
    toks = rows // seqs
    length = blocks * toks
    heads = width // TH
    step = 256
    t4 = teacher.reshape(blocks, seqs, toks, width)

    def kernel(t_ref, o_ref):
        i = pl.program_id(2)
        part = step // toks
        t = t_ref[...].reshape(length, TH)
        q = t_ref[pl.ds(i * part, part)].reshape(step, TH)
        o_ref[0, 0] = soft(dot(q, t, NT), LOG2E / math.sqrt(TH), float(length))

    return pl.pallas_call(
        kernel,
        grid=(seqs, heads, length // step),
        in_specs=[
            pl.BlockSpec((blocks, None, toks, TH), lambda s, h, i: (0, s, 0, h))
        ],
        out_specs=pl.BlockSpec((1, 1, step, length), lambda s, h, i: (s, h, i, 0)),
        out_shape=jax.ShapeDtypeStruct((seqs, heads, length, length), F32),
        compiler_params=params(40),
        cost_estimate=pl.CostEstimate(
            flops=2 * seqs * heads * length * length * TH,
            bytes_accessed=4 * seqs * heads * length * length,
            transcendentals=seqs * heads * length * length,
        ),
        name="teacher_probs",
    )(t4)


def head_grads(student, probs, seq):
    blocks, toks, cols = student.shape
    length = blocks * toks
    heads = cols // SH
    step = 256
    part = step // toks
    last = length // step - 1

    def kernel(s_ref, p_ref, o_ref, b_ref, rows, trans):
        i = pl.program_id(0)
        s = s_ref[...].reshape(length, cols)
        q = s_ref[pl.ds(i * part, part)].reshape(step, cols)
        lane = lax.broadcasted_iota(jnp.int32, (step, cols), 1) // SH
        here = jnp.zeros((step, cols), F32)
        across = jnp.zeros((cols, length), F32)
        for h in range(heads):
            qh = jnp.where(lane == h, q, jnp.zeros_like(q))
            p = soft(dot(qh, s, NT), LOG2E / math.sqrt(SH), float(length))
            g = (p - p_ref[0, h]).astype(BF16)
            here = jnp.where(lane == h, dot(g, s, NN), here)
            across = across + dot(qh, g, TN)
        rows[pl.ds(i * step, step)] = here

        @pl.when(i == 0)
        def _():
            trans[...] = across

        @pl.when(i > 0)
        def _():
            trans[...] += across

        @pl.when(i == last)
        def _():
            grad = ((rows[...] + trans[...].T) * (1.0 / math.sqrt(SH))).astype(BF16)
            o_ref[...] = grad.reshape(blocks, toks, cols)
            b_ref[...] = jnp.sum(grad.astype(F32), axis=0, keepdims=True)

    return pl.pallas_call(
        kernel,
        grid=(length // step,),
        in_specs=[
            pl.BlockSpec((blocks, toks, cols), lambda i: (0, 0, 0)),
            pl.BlockSpec((1, heads, step, length), lambda i: (seq, 0, i, 0)),
        ],
        out_specs=[
            pl.BlockSpec((blocks, toks, cols), lambda i: (0, 0, 0)),
            pl.BlockSpec((1, cols), lambda i: (0, 0)),
        ],
        out_shape=[
            jax.ShapeDtypeStruct((blocks, toks, cols), BF16),
            jax.ShapeDtypeStruct((1, cols), F32),
        ],
        scratch_shapes=[pltpu.VMEM((length, cols), F32), pltpu.VMEM((cols, length), F32)],
        compiler_params=params(48),
        cost_estimate=pl.CostEstimate(
            flops=6 * heads * length * length * cols,
            bytes_accessed=4 * heads * length * length,
            transcendentals=heads * length * length,
        ),
        name="head_grads",
    )(student, probs)


def hidden_grads(grads, weight):
    seqs = len(grads)
    blocks, toks, cols = grads[0].shape
    groups, _, depth, _ = weight.shape
    take = max(1, 256 // depth)

    def kernel(*refs):
        w_ref, o_ref = refs[seqs], refs[seqs + 1]
        acc = jnp.zeros((seqs * toks, take * depth), F32)
        for t in range(0, blocks, 2):
            g = jnp.concatenate(
                [
                    jnp.concatenate([refs[s][t + k] for k in range(2)], axis=1)
                    for s in range(seqs)
                ],
                axis=0,
            )
            w = jnp.concatenate(
                [w_ref[:, t + k].reshape(take * depth, cols) for k in range(2)], axis=1
            )
            acc = acc + dot(g, w, NT)
        o_ref[...] = acc.astype(BF16).reshape(seqs, toks, take * depth)

    return pl.pallas_call(
        kernel,
        grid=(groups // take,),
        in_specs=[pl.BlockSpec((blocks, toks, cols), lambda n: (0, 0, 0))] * seqs
        + [pl.BlockSpec((take, blocks, depth, cols), lambda n: (n, 0, 0, 0))],
        out_specs=pl.BlockSpec((seqs, toks, take * depth), lambda n: (0, 0, n)),
        out_shape=jax.ShapeDtypeStruct((seqs, toks, groups * depth), BF16),
        compiler_params=params(32),
        cost_estimate=pl.CostEstimate(
            flops=2 * seqs * toks * groups * depth * blocks * cols,
            bytes_accessed=2 * groups * depth * blocks * cols,
            transcendentals=0,
        ),
        name="hidden_grads",
    )(*grads, weight)


def sum_over(x, axis):
    size = lax.axis_size(axis)
    reach = 1
    while reach < size:
        x = x + lax.ppermute(x, axis, [(i, i ^ reach) for i in range(size)])
        reach *= 2
    return x


def exchange(x):
    return lax.all_to_all(x, "tok", split_axis=0, concat_axis=0, tiled=True)


def body(student_hidden, teacher_values, value_weight, value_bias):
    seqs, toks, width = student_hidden.shape
    groups, parts = lax.axis_size("dp"), lax.axis_size("tok")
    cols = value_weight.shape[1]
    depth = width // groups

    piece = lax.dynamic_slice_in_dim(value_weight, lax.axis_index("dp") * depth, depth)
    piece = jnp.concatenate([piece, jnp.broadcast_to(value_bias, (8, cols))], axis=0)
    pieces = exchange(jnp.broadcast_to(piece, (parts, depth + 8, cols)))
    weight = lax.all_gather(pieces[:, :depth], "dp", axis=0, tiled=False)
    bias = pieces[:, depth : depth + 1]

    teacher = exchange(
        split_columns(teacher_values.reshape(seqs * toks, -1), parts)
    )
    probs = teacher_probs(teacher, seqs)

    values = [exchange(v) for v in project(student_hidden, weight, bias)]
    grads, sums = [], []
    for s in range(seqs):
        grad, total = head_grads(values[s], probs, s)
        grads.append(exchange(grad))
        sums.append(total)
    hidden_grad = hidden_grads(grads, weight)
    tokens = seqs * toks * parts * groups
    bias_grad = sum_over(sum(sums[1:], sums[0]), "dp")[0] / math.sqrt(tokens)
    return (hidden_grad, bias_grad)


def solution(mesh):
    placed = (P("dp", "tok", None), P("dp", "tok", None), P(None, "tok"), P(None, "tok"))
    return jax.shard_map(
        body,
        mesh=mesh,
        in_specs=placed,
        out_specs=(P("dp", "tok", None), P("tok")),
        check_vma=False,
    )
```

time: 423 us -> 256 us (0.61)
  blocking collectives: 188 us -> 55.6 us
  Pallas kernels: 0 us -> 49 us
  waiting for transfers between devices: 100 us -> 60.1 us
  matrix products: 33 us -> 0 us
  starting transfers between devices: 35.9 us -> 62.2 us
  local copies, waits for them, and re-layouts: 32.9 us -> 10.2 us
  other arithmetic: 17.2 us -> 0.54 us
    psum x1 -> x0, blocking collectives: 112 us -> none  [body(): lax.psum(jnp.sum(grad_rows.astype(jnp.float32), axis=0), ('dp', 'tok'))]
    all_gather x1 -> x0, blocking collectives: 76.6 us -> none  [body(): lax.all_gather(value_bias, 'tok', axis=1, tiled=True)]
    all_to_all x0 -> x2, blocking collectives: none -> 55.6 us  [exchange(): return lax.all_to_all(x, 'tok', split_axis=0, concat_axis=0, tiled=True)]
    pallas_call x0 -> x6, Pallas kernels: none -> 49 us  [the longest x2 17.9 us: head_grads(): pl.pallas_call(kernel, grid=(length // step,), in_specs=[pl.BlockSpec((bl...]
    dot_general x34 -> x0, matrix products: 33 us -> none  [the longest x8 8.28 us: pair_grads(): lax.dot_general(query_teacher, teacher_head, contract, preferred_element_...]
    all_to_all x3 -> x4, waiting for transfers between devices: 27.4 us -> 3.8 us  [exchange(): return lax.all_to_all(x, 'tok', split_axis=0, concat_axis=0, tiled=True)]
    all_gather x1, waiting for transfers between devices: 72 us -> 49.4 us  [body(): weight = lax.all_gather(pieces[:, :depth], 'dp', axis=0, tiled=False)]
    ppermute x0 -> x5, starting transfers between devices: none -> 17.9 us  [sum_over(): x = x + lax.ppermute(x, axis, [(i, i ^ reach) for i in range(size)])]
  transfers between devices with their start and end apart: 4 -> 10, of which waited for: 3 -> 7; matrix products, arithmetic and copies ran while one was open for 6% -> 0% of each run, Pallas kernels for 0% -> 18%
where the time goes in v1:
time: 256 us; the launch traced here: 252 us
  starting transfers between devices  62.2 us (24%)
  waiting for transfers between devices  60.1 us (23%)
  blocking collectives  55.6 us (22%)
  Pallas kernels  49 us (19%)
  between operations  14.1 us (6%)
  local copies, waits for them, and re-layouts  10.2 us (4%)
    all_to_all x2, blocking collectives, exchange(): return lax.all_to_all(x, 'tok', split_axis=0, concat_axis=0, tiled=True)  55.6 us
    all_gather x1, waiting for transfers between devices, body(): weight = lax.all_gather(pieces[:, :depth], 'dp', axis=0, tiled=False)  49.4 us
    all_to_all x4, starting transfers between devices, exchange(): return lax.all_to_all(x, 'tok', split_axis=0, concat_axis=0, tiled=True)  44.2 us
    ppermute x5, starting transfers between devices, sum_over(): x = x + lax.ppermute(x, axis, [(i, i ^ reach) for i in range(size)])  17.9 us
    pallas_call x2, Pallas kernels, head_grads(): pl.pallas_call(kernel, grid=(length // step,), in_specs=[pl.BlockSpec((bl...  17.9 us
    pallas_call x1, Pallas kernels, teacher_probs(): pl.pallas_call(kernel, grid=(seqs, heads, length // step), in_specs=[pl.B...  13.1 us
    pallas_call x1, Pallas kernels, split_columns(): pl.pallas_call(kernel, grid=(parts,), in_specs=[pl.BlockSpec((rows, cols)...  8.84 us
    unnamed x8, local copies, waits for them, and re-layouts  8.79 us
  transfers between devices with their start and end apart: 10, of which 7 were waited for; matrix products, arithmetic and copies ran while one was open for 0% of the time, Pallas kernels for 18%

profile of v1, /device:TPU:1, one launch (start us, length us, event | category | flops | bytes accessed | tf_op | source)
XLA Modules:
  0.0 251.8 jit_solution(15447389197263052146)
XLA Ops:
  8.9 29.7 %all_to_all.30 = bf16[16,72,128]{2,1,0:T(8,128)(2,1)S(1)} all-to-all(bf16[16,72,128]{2,1,0:T(8,128)(2,1)S(1)} %broadcast_in_dim.12), channel_id=1, replica_groups=mesh['dp'=32,'tok'=16] {'tok'}, dimensions={0} | all-to-all | bytes 589824 | tf_op jit(solution)/shard_map/all_to_all | solution.py:234
  39.4 8.8 %split_columns.1 = bf16[16,128,256]{2,1,0:T(8,128)(2,1)} custom-call(bf16[128,4096]{1,0:T(8,128)(2,1)} %bitcast.9), custom_call_target="tpu_custom_call" | custom-call | tf_op jit(solution)/shard_map/split_columns/pallas_call | solution.py:36
  48.2 11.3 %all-to-all-start.2 = ((bf16[16,128,256]{2,1,0:T(8,128)(2,1)}), bf16[16,128,256]{2,1,0:T(8,128)(2,1)S(1)}, u32[]{:S(2)}, u32[]{:S(2)}) async-start(bf16[16,128,256]{2,1,0:T(8,128)(2,1)} %split_columns.1), calls=%async_computation.2 | async-start | bytes 2097152 | tf_op jit(solution)/shard_map/all_to_all | solution.py:234
  59.5 49.4 %all-gather.3.cloned.1.call-done = bf16[512,64,128]{2,1,0:T(8,128)(2,1)} async-done(((bf16[16,64,128]{2,1,0:T(8,128)(2,1)}), bf16[512,64,128]{2,1,0:T(8,128)(2,1)}) %all-gather.3.cloned.1.call-update) | async-done | bytes 8388624 | tf_op jit(solution)/shard_map/all_gather | solution.py:246
  108.9 3.4 %copy-done.1 = bf16[512,64,128]{2,1,0:T(8,128)(2,1)S(1)} copy-done((bf16[512,64,128]{2,1,0:T(8,128)(2,1)S(1)}, bf16[512,64,128]{2,1,0:T(8,128)(2,1)}, u32[]{:S(2)}) %copy-start.1) | copy-done | bytes 8388632
  113.3 4.3 %project.1 = (bf16[16,64,128]{2,1,0:T(8,128)(2,1)}, bf16[16,64,128]{2,1,0:T(8,128)(2,1)S(1)}) custom-call(bf16[2,64,2048]{2,1,0:T(8,128)(2,1)S(1)} %copy-done.3, bf16[32,16,64,128]{3,2,1,0:T(8,128)(2,1)S(1)} %bitcast.6, bf16[16,1,128]{2,1,0:T(2,128)(2,1)S(1)} %slice.9.b_ref), custom_call_target="tpu_custom_call" | custom-call | flops 1073741824 | bytes 8388608 | tf_op jit(solution)/shard_map/project/pallas_call | solution.py:62
  117.6 25.9 %all_to_all.31.s_ref = bf16[16,64,128]{2,1,0:T(8,128)(2,1)S(1)} all-to-all(bf16[16,64,128]{2,1,0:T(8,128)(2,1)S(1)} %get-tuple-element.10), channel_id=1, replica_groups=mesh['dp'=32,'tok'=16] {'tok'}, dimensions={0} | all-to-all | bytes 524288 | tf_op jit(solution)/shard_map/all_to_all | solution.py:234
  143.5 10.1 %all-to-all-start.1 = ((bf16[16,64,128]{2,1,0:T(8,128)(2,1)}), bf16[16,64,128]{2,1,0:T(8,128)(2,1)S(1)}, u32[]{:S(2)}, u32[]{:S(2)}) async-start(bf16[16,64,128]{2,1,0:T(8,128)(2,1)} %get-tuple-element.8), calls=%async_computation.1 | async-start | bytes 524288 | tf_op jit(solution)/shard_map/all_to_all | solution.py:234
  153.7 13.1 %teacher_probs.1.p_ref = f32[2,2,1024,1024]{3,2,1,0:T(8,128)} custom-call(bf16[16,2,64,256]{3,2,1,0:T(8,128)(2,1)S(1)} %bitcast.8), custom_call_target="tpu_custom_call" | custom-call | flops 1073741824 | bytes 16777216 | tf_op jit(solution)/shard_map/teacher_probs/pallas_call | solution.py:103
  166.8 8.9 %head_grads.3 = (bf16[16,64,128]{2,1,0:T(8,128)(2,1)}, f32[1,128]{1,0:T(1,128)S(1)}) custom-call(bf16[16,64,128]{2,1,0:T(8,128)(2,1)S(1)} %all_to_all.31.s_ref, f32[2,2,1024,1024]{3,2,1,0:T(8,128)} %teacher_probs.1.p_ref), custom_call_target="tpu_custom_call" | custom-call | flops 1610612736 | bytes 8388608 | tf_op jit(solution)/shard_map/head_grads/pallas_call | solution.py:158
  175.7 11.5 %all-to-all-start.5 = ((bf16[16,64,128]{2,1,0:T(8,128)(2,1)}), bf16[16,64,128]{2,1,0:T(8,128)(2,1)S(1)}, u32[]{:S(2)}, u32[]{:S(2)}) async-start(bf16[16,64,128]{2,1,0:T(8,128)(2,1)} %get-tuple-element.11), calls=%async_computation.5 | async-start | bytes 524288 | tf_op jit(solution)/shard_map/all_to_all | solution.py:234
  187.2 8.9 %head_grads.2 = (bf16[16,64,128]{2,1,0:T(8,128)(2,1)}, f32[1,128]{1,0:T(1,128)S(1)}) custom-call(bf16[16,64,128]{2,1,0:T(8,128)(2,1)S(1)} %all-to-all-done.1.s_ref, f32[2,2,1024,1024]{3,2,1,0:T(8,128)} %teacher_probs.1.p_ref), custom_call_target="tpu_custom_call" | custom-call | flops 1610612736 | bytes 8388608 | tf_op jit(solution)/shard_map/head_grads/pallas_call | solution.py:158
  196.1 3.8 %all-to-all-done.5.refs_1_ = bf16[16,64,128]{2,1,0:T(8,128)(2,1)S(1)} async-done(((bf16[16,64,128]{2,1,0:T(8,128)(2,1)}), bf16[16,64,128]{2,1,0:T(8,128)(2,1)S(1)}, u32[]{:S(2)}, u32[]{:S(2)}) %all-to-all-start.5) | async-done | bytes 262176 | tf_op jit(solution)/shard_map/all_to_all | solution.py:234
  199.9 11.4 %all-to-all-start.3 = ((bf16[16,64,128]{2,1,0:T(8,128)(2,1)}), bf16[16,64,128]{2,1,0:T(8,128)(2,1)S(1)}, u32[]{:S(2)}, u32[]{:S(2)}) async-start(bf16[16,64,128]{2,1,0:T(8,128)(2,1)} %get-tuple-element.9), calls=%async_computation.3 | async-start | bytes 524288 | tf_op jit(solution)/shard_map/all_to_all | solution.py:234
  211.3 2.9 %collective-permute-start = (f32[1,128]{1,0:T(1,128)S(1)}, f32[1,128]{1,0:T(1,128)S(1)}, u32[]{:S(2)}, u32[]{:S(2)}) collective-permute-start(f32[1,128]{1,0:T(1,128)S(1)} %add.22), channel_id=1, source_target_pairs={{0,16},{16,0},{32,48},{48,32},{64,80},{80,64},{96,112},{112,96},{1... | collective-permute-start | bytes 1544 | tf_op jit(solution)/shard_map/ppermute | solution.py:228
  215.1 2.9 %collective-permute-start.1 = (f32[1,128]{1,0:T(1,128)S(1)}, f32[1,128]{1,0:T(1,128)S(1)}, u32[]{:S(2)}, u32[]{:S(2)}) collective-permute-start(f32[1,128]{1,0:T(1,128)S(1)} %add.23), channel_id=1, source_target_pairs={{0,32},{16,48},{32,0},{48,16},{64,96},{80,112},{96,64},{112,80},{1... | collective-permute-start | bytes 1544 | tf_op jit(solution)/shard_map/ppermute | solution.py:228
  217.9 1.7 collective-permute-done.1
  219.7 4.4 %collective-permute-start.2 = (f32[1,128]{1,0:T(1,128)S(1)}, f32[1,128]{1,0:T(1,128)S(1)}, u32[]{:S(2)}, u32[]{:S(2)}) collective-permute-start(f32[1,128]{1,0:T(1,128)S(1)} %add.24), channel_id=1, source_target_pairs={{0,64},{16,80},{32,96},{48,112},{64,0},{80,16},{96,32},{112,48},{1... | collective-permute-start | bytes 1544 | tf_op jit(solution)/shard_map/ppermute | solution.py:228
  224.1 1.7 collective-permute-done.2
  225.8 3.1 %collective-permute-start.3 = (f32[1,128]{1,0:T(1,128)S(1)}, f32[1,128]{1,0:T(1,128)S(1)}, u32[]{:S(2)}, u32[]{:S(2)}) collective-permute-start(f32[1,128]{1,0:T(1,128)S(1)} %add.25), channel_id=1, source_target_pairs={{0,128},{16,144},{32,160},{48,176},{64,192},{80,208},{96,224},{112... | collective-permute-start | bytes 1544 | tf_op jit(solution)/shard_map/ppermute | solution.py:228
  228.9 1.5 collective-permute-done.3
  230.4 4.6 %collective-permute-start.4 = (f32[1,128]{1,0:T(1,128)S(1)}, f32[1,128]{1,0:T(1,128)S(1)}, u32[]{:S(2)}, u32[]{:S(2)}) collective-permute-start(f32[1,128]{1,0:T(1,128)S(1)} %add.26), channel_id=1, source_target_pairs={{0,256},{16,272},{32,288},{48,304},{64,320},{80,336},{96,352},{112... | collective-permute-start | bytes 1544 | tf_op jit(solution)/shard_map/ppermute | solution.py:228
  236.7 3.4 %copy-done.2 = bf16[512,64,128]{2,1,0:T(8,128)(2,1)S(1)} copy-done((bf16[512,64,128]{2,1,0:T(8,128)(2,1)S(1)}, bf16[512,64,128]{2,1,0:T(8,128)(2,1)}, u32[]{:S(2)}) %copy-start.2) | copy-done | bytes 8388632
  240.1 4.9 %hidden_grads.1 = bf16[2,64,2048]{2,1,0:T(8,128)(2,1)} custom-call(bf16[16,64,128]{2,1,0:T(8,128)(2,1)S(1)} %all-to-all-done.3.refs_0_, bf16[16,64,128]{2,1,0:T(8,128)(2,1)S(1)} %all-to-all-done.5.refs_1_, bf16[32,16,64,128]{3,2,1,0:T(8,128)(2,1)S(1)} %bitcast.7), custom_call_target="tpu_custom_call" | custom-call | flops 1073741824 | bytes 8388608 | tf_op jit(solution)/shard_map/hidden_grads/pallas_call | solution.py:207
  (25 shorter events, 6.1 us)
Async XLA Ops:
  7.2 1.0 copy-start
  7.2 101.7 %all-gather.3.cloned.1.call-start = ((), (), s32[]{:S(2)}) async-start(), calls=%async_computation.6 | async-start | bytes 8650752 | tf_op jit(solution)/shard_map/all_gather | solution.py:246
  48.2 69.4 %all-to-all-start.2 = ((bf16[16,128,256]{2,1,0:T(8,128)(2,1)}), bf16[16,128,256]{2,1,0:T(8,128)(2,1)S(1)}, u32[]{:S(2)}, u32[]{:S(2)}) async-start(bf16[16,128,256]{2,1,0:T(8,128)(2,1)} %split_columns.1), calls=%async_computation.2 | async-start | bytes 2097152 | tf_op jit(solution)/shard_map/all_to_all | solution.py:234
  108.9 3.4 %copy-start.1 = (bf16[512,64,128]{2,1,0:T(8,128)(2,1)S(1)}, bf16[512,64,128]{2,1,0:T(8,128)(2,1)}, u32[]{:S(2)}) copy-start(bf16[512,64,128]{2,1,0:T(8,128)(2,1)} %all-gather.3.cloned.1.call-done) | copy-start | bytes 25165828
  112.3 1.0 copy-start.3
  143.5 32.2 %all-to-all-start.1 = ((bf16[16,64,128]{2,1,0:T(8,128)(2,1)}), bf16[16,64,128]{2,1,0:T(8,128)(2,1)S(1)}, u32[]{:S(2)}, u32[]{:S(2)}) async-start(bf16[16,64,128]{2,1,0:T(8,128)(2,1)} %get-tuple-element.8), calls=%async_computation.1 | async-start | bytes 524288 | tf_op jit(solution)/shard_map/all_to_all | solution.py:234
  175.7 24.2 %all-to-all-start.5 = ((bf16[16,64,128]{2,1,0:T(8,128)(2,1)}), bf16[16,64,128]{2,1,0:T(8,128)(2,1)S(1)}, u32[]{:S(2)}, u32[]{:S(2)}) async-start(bf16[16,64,128]{2,1,0:T(8,128)(2,1)} %get-tuple-element.11), calls=%async_computation.5 | async-start | bytes 524288 | tf_op jit(solution)/shard_map/all_to_all | solution.py:234
  199.9 36.7 %all-to-all-start.3 = ((bf16[16,64,128]{2,1,0:T(8,128)(2,1)}), bf16[16,64,128]{2,1,0:T(8,128)(2,1)S(1)}, u32[]{:S(2)}, u32[]{:S(2)}) async-start(bf16[16,64,128]{2,1,0:T(8,128)(2,1)} %get-tuple-element.9), calls=%async_computation.3 | async-start | bytes 524288 | tf_op jit(solution)/shard_map/all_to_all | solution.py:234
  211.3 3.7 %collective-permute-start = (f32[1,128]{1,0:T(1,128)S(1)}, f32[1,128]{1,0:T(1,128)S(1)}, u32[]{:S(2)}, u32[]{:S(2)}) collective-permute-start(f32[1,128]{1,0:T(1,128)S(1)} %add.22), channel_id=1, source_target_pairs={{0,16},{16,0},{32,48},{48,32},{64,80},{80,64},{96,112},{112,96},{1... | collective-permute-start | bytes 1544 | tf_op jit(solution)/shard_map/ppermute | solution.py:228
  215.1 4.6 %collective-permute-start.1 = (f32[1,128]{1,0:T(1,128)S(1)}, f32[1,128]{1,0:T(1,128)S(1)}, u32[]{:S(2)}, u32[]{:S(2)}) collective-permute-start(f32[1,128]{1,0:T(1,128)S(1)} %add.23), channel_id=1, source_target_pairs={{0,32},{16,48},{32,0},{48,16},{64,96},{80,112},{96,64},{112,80},{1... | collective-permute-start | bytes 1544 | tf_op jit(solution)/shard_map/ppermute | solution.py:228
  219.7 6.1 %collective-permute-start.2 = (f32[1,128]{1,0:T(1,128)S(1)}, f32[1,128]{1,0:T(1,128)S(1)}, u32[]{:S(2)}, u32[]{:S(2)}) collective-permute-start(f32[1,128]{1,0:T(1,128)S(1)} %add.24), channel_id=1, source_target_pairs={{0,64},{16,80},{32,96},{48,112},{64,0},{80,16},{96,32},{112,48},{1... | collective-permute-start | bytes 1544 | tf_op jit(solution)/shard_map/ppermute | solution.py:228
  225.8 4.6 %collective-permute-start.3 = (f32[1,128]{1,0:T(1,128)S(1)}, f32[1,128]{1,0:T(1,128)S(1)}, u32[]{:S(2)}, u32[]{:S(2)}) collective-permute-start(f32[1,128]{1,0:T(1,128)S(1)} %add.25), channel_id=1, source_target_pairs={{0,128},{16,144},{32,160},{48,176},{64,192},{80,208},{96,224},{112... | collective-permute-start | bytes 1544 | tf_op jit(solution)/shard_map/ppermute | solution.py:228
  230.4 5.8 %collective-permute-start.4 = (f32[1,128]{1,0:T(1,128)S(1)}, f32[1,128]{1,0:T(1,128)S(1)}, u32[]{:S(2)}, u32[]{:S(2)}) collective-permute-start(f32[1,128]{1,0:T(1,128)S(1)} %add.26), channel_id=1, source_target_pairs={{0,256},{16,272},{32,288},{48,304},{64,320},{80,336},{96,352},{112... | collective-permute-start | bytes 1544 | tf_op jit(solution)/shard_map/ppermute | solution.py:228
  236.7 3.4 %copy-start.2 = (bf16[512,64,128]{2,1,0:T(8,128)(2,1)S(1)}, bf16[512,64,128]{2,1,0:T(8,128)(2,1)}, u32[]{:S(2)}) copy-start(bf16[512,64,128]{2,1,0:T(8,128)(2,1)} %all-gather.3.cloned.1.call-done) | copy-start | bytes 25165828
Sparse Core Ops, SparseCore 0:
  39.5 69.3 all-gather.2

commit v2 on v1

v2 whole, which is shorter than its diff:
```python
import math

import jax
import jax.numpy as jnp
from jax import lax
from jax.experimental import pallas as pl
from jax.experimental.pallas import tpu as pltpu
from jax.sharding import PartitionSpec as P


SH = 64
TH = 128
LOG2E = 1.4426950408889634
NT = (((1,), (1,)), ((), ()))
TN = (((0,), (0,)), ((), ()))
NN = (((1,), (0,)), ((), ()))
F32 = jnp.float32
BF16 = jnp.bfloat16


def dot(a, b, dims):
    return lax.dot_general(a, b, dims, preferred_element_type=F32)


def params(mib):
    return pltpu.CompilerParams(vmem_limit_bytes=mib << 20)


def split_columns(x, parts):
    rows, width = x.shape
    cols = width // parts

    def kernel(x_ref, o_ref):
        o_ref[0] = x_ref[...]

    return pl.pallas_call(
        kernel,
        grid=(parts,),
        in_specs=[pl.BlockSpec((rows, cols), lambda t: (0, t))],
        out_specs=pl.BlockSpec((1, rows, cols), lambda t: (t, 0, 0)),
        out_shape=jax.ShapeDtypeStruct((parts, rows, cols), x.dtype),
        name="split_columns",
    )(x)


SIDE = 4
LANE = 128


def ring_pairs(shift, first):
    def place(x, y, c):
        return ((x % SIDE) * SIDE + y % SIDE) * 2 + c

    pairs = []
    for x in range(SIDE):
        for y in range(SIDE):
            for c in range(2):
                dx, dy = (shift, 0) if (c == 0) == first else (0, shift)
                pairs.append((place(x, y, c), place(x + dx, y + dy, c)))
    return pairs


def gather_weight(piece):
    def send(v, shift, first):
        return lax.ppermute(v, "dp", ring_pairs(shift, first))

    near = [send(piece, k, True) for k in (1, -1, 2)]
    own = jnp.stack([piece, near[0], near[2], near[1]])
    down, up = send(own, 1, False), send(own, -1, False)
    half = SIDE // 2
    low, high = send(down[:half], 1, False), send(up[half:], -1, False)
    mine = [own, down, low, high, up]
    swap = [(d, d ^ 1) for d in range(2 * SIDE * SIDE)]
    theirs = [lax.ppermute(v, "dp", swap) for v in mine]
    return mine + theirs


def blocks_of():
    table = []
    for d in range(2 * SIDE * SIDE):
        x, y, c = d // (2 * SIDE), d // 2 % SIDE, d % 2
        table.append(
            [(x - j) % SIDE * SIDE + (y - b) % SIDE for j in range(SIDE) for b in range(SIDE)]
            + [c]
        )
    return lax.dynamic_index_in_dim(
        jnp.array(table, jnp.int32), lax.axis_index("dp"), keepdims=False
    )


def weight_block(refs, core, k):
    def pick(side, b, j):
        part = refs[5 * side : 5 * side + 5]
        if b == 2:
            half = SIDE // 2
            return part[2 + j // half][j % half, k]
        return part[{0: 0, 1: 1, 3: 4}[b]][j, k]

    rows = []
    for j in range(SIDE):
        for b in range(SIDE):
            rows.append(jnp.where(core == 0, pick(0, b, j), pick(1, b, j)))
            rows.append(jnp.where(core == 0, pick(1, j, b), pick(0, j, b)))
    return jnp.concatenate(rows, axis=0)


def weight_specs(weights, pair):
    return [
        pl.BlockSpec((w.shape[0], pair) + w.shape[2:], lambda t, place: (0, t, 0, 0))
        for w in weights
    ]


def project(hidden, weights, bias, place):
    rows, width = hidden.shape
    blocks, cols = weights[0].shape[1], weights[0].shape[3]
    pair = 2
    count = len(weights)

    def kernel(place_ref, h_ref, b_ref, *refs):
        w_refs, o_ref, h = refs[:count], refs[count], refs[count + 1]

        @pl.when(pl.program_id(0) == 0)
        def _():
            for m in range(width // LANE):
                at = pl.multiple_of(place_ref[m] * LANE, LANE)
                h[:, m * LANE : (m + 1) * LANE] = h_ref[:, pl.ds(at, LANE)]

        core = place_ref[width // LANE]
        w = jnp.concatenate(
            [weight_block(w_refs, core, k) for k in range(pair)], axis=1
        )
        r = dot(h[...], w, NN)
        for k in range(pair):
            o_ref[k] = (r[:, k * cols : (k + 1) * cols] + b_ref[k].astype(F32)).astype(BF16)

    return pl.pallas_call(
        kernel,
        grid_spec=pltpu.PrefetchScalarGridSpec(
            num_scalar_prefetch=1,
            grid=(blocks // pair,),
            in_specs=[
                pl.BlockSpec((rows, width), lambda t, place: (0, 0)),
                pl.BlockSpec((pair, 1, cols), lambda t, place: (t, 0, 0)),
            ]
            + weight_specs(weights, pair),
            out_specs=pl.BlockSpec((pair, rows, cols), lambda t, place: (t, 0, 0)),
            scratch_shapes=[pltpu.VMEM((rows, width), BF16)],
        ),
        out_shape=jax.ShapeDtypeStruct((blocks, rows, cols), BF16),
        compiler_params=params(32),
        cost_estimate=pl.CostEstimate(
            flops=2 * rows * width * blocks * cols,
            bytes_accessed=2 * width * blocks * cols,
            transcendentals=0,
        ),
        name="project",
    )(place, hidden, bias, *weights)


def soft(scores, scale, total):
    peak = jnp.max(scores, axis=1, keepdims=True)
    e = jnp.exp2((scores - peak) * scale)
    return e * (total / jnp.sum(e, axis=1, keepdims=True))


def teacher_probs(teacher, seqs):
    blocks, rows, width = teacher.shape
    toks = rows // seqs
    length = blocks * toks
    heads = width // TH
    step = 256
    t4 = teacher.reshape(blocks, seqs, toks, width)

    def kernel(t_ref, o_ref):
        i = pl.program_id(2)
        part = step // toks
        t = t_ref[...].reshape(length, TH)
        q = t_ref[pl.ds(i * part, part)].reshape(step, TH)
        o_ref[0, 0] = soft(dot(q, t, NT), LOG2E / math.sqrt(TH), float(length))

    return pl.pallas_call(
        kernel,
        grid=(seqs, heads, length // step),
        in_specs=[
            pl.BlockSpec((blocks, None, toks, TH), lambda s, h, i: (0, s, 0, h))
        ],
        out_specs=pl.BlockSpec((1, 1, step, length), lambda s, h, i: (s, h, i, 0)),
        out_shape=jax.ShapeDtypeStruct((seqs, heads, length, length), F32),
        compiler_params=params(40),
        cost_estimate=pl.CostEstimate(
            flops=2 * seqs * heads * length * length * TH,
            bytes_accessed=4 * seqs * heads * length * length,
            transcendentals=seqs * heads * length * length,
        ),
        name="teacher_probs",
    )(t4)


def head_grads(student, probs):
    seqs = probs.shape[0]
    blocks, both, cols = student.shape
    toks = both // seqs
    length = blocks * toks
    heads = cols // SH
    step = 256
    part = step // toks
    last = length // step - 1

    def kernel(s_ref, p_ref, o_ref, b_ref, rows, trans):
        i = pl.program_id(1)
        s = s_ref[...].reshape(length, cols)
        q = s_ref[pl.ds(i * part, part)].reshape(step, cols)
        lane = lax.broadcasted_iota(jnp.int32, (step, cols), 1) // SH
        here = jnp.zeros((step, cols), F32)
        across = jnp.zeros((cols, length), F32)
        for h in range(heads):
            qh = jnp.where(lane == h, q, jnp.zeros_like(q))
            p = soft(dot(qh, s, NT), LOG2E / math.sqrt(SH), float(length))
            g = (p - p_ref[0, h]).astype(BF16)
            here = jnp.where(lane == h, dot(g, s, NN), here)
            across = across + dot(qh, g, TN)
        rows[pl.ds(i * step, step)] = here

        @pl.when(i == 0)
        def _():
            trans[...] = across

        @pl.when(i > 0)
        def _():
            trans[...] += across

        @pl.when(i == last)
        def _():
            grad = ((rows[...] + trans[...].T) * (1.0 / math.sqrt(SH))).astype(BF16)
            o_ref[...] = grad.reshape(blocks, toks, cols)
            total = jnp.sum(grad.astype(F32), axis=0, keepdims=True)
            b_ref[...] = jnp.where(pl.program_id(0) == 0, total, b_ref[...] + total)

    grads, total = pl.pallas_call(
        kernel,
        grid=(seqs, length // step),
        in_specs=[
            pl.BlockSpec((blocks, None, toks, cols), lambda s, i: (0, s, 0, 0)),
            pl.BlockSpec((1, heads, step, length), lambda s, i: (s, 0, i, 0)),
        ],
        out_specs=[
            pl.BlockSpec((blocks, None, toks, cols), lambda s, i: (0, s, 0, 0)),
            pl.BlockSpec((1, cols), lambda s, i: (0, 0)),
        ],
        out_shape=[
            jax.ShapeDtypeStruct((blocks, seqs, toks, cols), BF16),
            jax.ShapeDtypeStruct((1, cols), F32),
        ],
        scratch_shapes=[pltpu.VMEM((length, cols), F32), pltpu.VMEM((cols, length), F32)],
        compiler_params=params(48),
        cost_estimate=pl.CostEstimate(
            flops=6 * seqs * heads * length * length * cols,
            bytes_accessed=4 * seqs * heads * length * length,
            transcendentals=seqs * heads * length * length,
        ),
        name="head_grads",
    )(student.reshape(blocks, seqs, toks, cols), probs)
    return grads.reshape(student.shape), total


def hidden_grads(grads, weights, place):
    blocks, rows, cols = grads.shape
    width = weights[0].shape[2] * 2 * SIDE * SIDE
    pair = 2
    count = len(weights)
    last = blocks // pair - 1

    def kernel(place_ref, g_ref, *refs):
        w_refs, o_ref, acc = refs[:count], refs[count], refs[count + 1]
        t = pl.program_id(0)
        core = place_ref[width // LANE]
        w = jnp.concatenate(
            [weight_block(w_refs, core, k) for k in range(pair)], axis=1
        )
        g = jnp.concatenate([g_ref[k] for k in range(pair)], axis=1)
        r = dot(g, w, NT)

        @pl.when(t == 0)
        def _():
            acc[...] = r

        @pl.when(t > 0)
        def _():
            acc[...] += r

        @pl.when(t == last)
        def _():
            for m in range(width // LANE):
                at = pl.multiple_of(place_ref[m] * LANE, LANE)
                o_ref[:, pl.ds(at, LANE)] = acc[:, m * LANE : (m + 1) * LANE].astype(BF16)

    return pl.pallas_call(
        kernel,
        grid_spec=pltpu.PrefetchScalarGridSpec(
            num_scalar_prefetch=1,
            grid=(blocks // pair,),
            in_specs=[pl.BlockSpec((pair, rows, cols), lambda t, place: (t, 0, 0))]
            + weight_specs(weights, pair),
            out_specs=pl.BlockSpec((rows, width), lambda t, place: (0, 0)),
            scratch_shapes=[pltpu.VMEM((rows, width), F32)],
        ),
        out_shape=jax.ShapeDtypeStruct((rows, width), BF16),
        compiler_params=params(32),
        cost_estimate=pl.CostEstimate(
            flops=2 * rows * width * blocks * cols,
            bytes_accessed=2 * width * blocks * cols,
            transcendentals=0,
        ),
        name="hidden_grads",
    )(place, grads, *weights)


def sum_over(x, axis):
    size = lax.axis_size(axis)
    reach = 1
    while reach < size:
        x = x + lax.ppermute(x, axis, [(i, i ^ reach) for i in range(size)])
        reach *= 2
    return x


def exchange(x):
    return lax.all_to_all(x, "tok", split_axis=0, concat_axis=0, tiled=True)


def body(student_hidden, teacher_values, value_weight, value_bias):
    seqs, toks, width = student_hidden.shape
    groups, parts = lax.axis_size("dp"), lax.axis_size("tok")
    cols = value_weight.shape[1]
    depth = width // groups

    piece = lax.dynamic_slice_in_dim(value_weight, lax.axis_index("dp") * depth, depth)
    piece = jnp.concatenate([piece, jnp.broadcast_to(value_bias, (8, cols))], axis=0)
    pieces = exchange(jnp.broadcast_to(piece, (parts, depth + 8, cols)))
    bias = pieces[:, depth : depth + 1]

    columns = split_columns(teacher_values.reshape(seqs * toks, -1), parts)
    teacher = exchange(columns)
    weights = gather_weight(pieces[:, :depth])
    probs = teacher_probs(teacher, seqs)

    place = blocks_of()
    rows = student_hidden.reshape(seqs * toks, width)
    values = project(rows, weights, bias, place)
    values = exchange(values)
    grads, total = head_grads(values, probs)
    grads = exchange(grads)
    hidden_grad = hidden_grads(grads, weights, place).reshape(student_hidden.shape)
    tokens = seqs * toks * parts * groups
    bias_grad = sum_over(total, "dp")[0] / math.sqrt(tokens)
    return (hidden_grad, bias_grad)


def solution(mesh):
    placed = (P("dp", "tok", None), P("dp", "tok", None), P(None, "tok"), P(None, "tok"))
    return jax.shard_map(
        body,
        mesh=mesh,
        in_specs=placed,
        out_specs=(P("dp", "tok", None), P("tok")),
        check_vma=False,
    )
```

time: 256 us -> 217 us (0.85)
  the two profiles are of different devices: /device:TPU:1 before, /device:TPU:6 now
where the time goes in v2:
time: 217 us; the launch traced here: 215 us
  starting transfers between devices  83.2 us (38%)
  waiting for transfers between devices  68 us (31%)
  Pallas kernels  55.4 us (26%)
  local copies, waits for them, and re-layouts  7 us (3%)
    all_to_all x4, starting transfers between devices, exchange(): return lax.all_to_all(x, 'tok', split_axis=0, concat_axis=0, tiled=True)  39.9 us
    all_to_all x4, waiting for transfers between devices, exchange(): return lax.all_to_all(x, 'tok', split_axis=0, concat_axis=0, tiled=True)  26.1 us
    ppermute x7, starting transfers between devices, send(): return lax.ppermute(v, 'dp', ring_pairs(shift, first))  23.6 us
    ppermute x7, waiting for transfers between devices, send(): return lax.ppermute(v, 'dp', ring_pairs(shift, first))  22.1 us
    ppermute x5, waiting for transfers between devices, sum_over(): x = x + lax.ppermute(x, axis, [(i, i ^ reach) for i in range(size)])  18.3 us
    pallas_call x1, Pallas kernels, head_grads(): pl.pallas_call(kernel, grid=(seqs, length // step), in_specs=[pl.BlockSpe...  15.3 us
    pallas_call x1, Pallas kernels, teacher_probs(): pl.pallas_call(kernel, grid=(seqs, heads, length // step), in_specs=[pl.B...  14.5 us
    ppermute x5, starting transfers between devices, gather_weight(): theirs = [lax.ppermute(v, 'dp', swap) for v in mine]  10.1 us
  transfers between devices with their start and end apart: 21, of which 14 were waited for; matrix products, arithmetic and copies ran while one was open for 1% of the time, Pallas kernels for 14%

profile of v2, /device:TPU:6, one launch (start us, length us, event | category | flops | bytes accessed | tf_op | source)
XLA Modules:
  0.0 215.2 jit_solution(2083817026825923130)
XLA Ops:
  3.1 15.2 %all-to-all-start = ((bf16[16,72,128]{2,1,0:T(8,128)(2,1)}), bf16[16,72,128]{2,1,0:T(8,128)(2,1)S(1)}, u32[]{:S(2)}, u32[]{:S(2)}) async-start(bf16[16,72,128]{2,1,0:T(8,128)(2,1)} %broadcast_in_dim.12), calls=%async_computation | async-start | bytes 589824 | tf_op jit(solution)/shard_map/all_to_all | solution.py:329
  18.3 8.8 %split_columns.1 = bf16[16,128,256]{2,1,0:T(8,128)(2,1)} custom-call(bf16[128,4096]{1,0:T(8,128)(2,1)} %bitcast.18), custom_call_target="tpu_custom_call" | custom-call | tf_op jit(solution)/shard_map/split_columns/pallas_call | solution.py:36
  27.1 10.6 %all-to-all-done = bf16[16,72,128]{2,1,0:T(8,128)(2,1)S(1)} async-done(((bf16[16,72,128]{2,1,0:T(8,128)(2,1)}), bf16[16,72,128]{2,1,0:T(8,128)(2,1)S(1)}, u32[]{:S(2)}, u32[]{:S(2)}) %all-to-all-start) | async-done | bytes 294944 | tf_op jit(solution)/shard_map/all_to_all | solution.py:329
  37.7 6.2 %all-to-all-start.2 = ((bf16[16,128,256]{2,1,0:T(8,128)(2,1)}), bf16[16,128,256]{2,1,0:T(8,128)(2,1)}, u32[]{:S(2)}, u32[]{:S(2)}) async-start(bf16[16,128,256]{2,1,0:T(8,128)(2,1)} %split_columns.1), calls=%async_computation.2 | async-start | bytes 2097152 | tf_op jit(solution)/shard_map/all_to_all | solution.py:329
  44.0 3.3 %collective-permute-start.1 = (bf16[16,64,128]{2,1,0:T(8,128)(2,1)S(1)}, bf16[16,64,128]{2,1,0:T(8,128)(2,1)S(1)}, u32[]{:S(2)}, u32[]{:S(2)}) collective-permute-start(bf16[16,64,128]{2,1,0:T(8,128)(2,1)S(1)} %get-tuple-element.7), channel_id=1, source_target_pairs={{0,256},{16,80},{32,288},{48,112},{64,320},{80,16},{96,352},{112,4... | collective-permute-start | bytes 786440 | tf_op jit(solution)/shard_map/ppermute | solution.py:65
  47.4 4.0 %collective-permute-start = (bf16[16,64,128]{2,1,0:T(8,128)(2,1)S(1)}, bf16[16,64,128]{2,1,0:T(8,128)(2,1)S(1)}, u32[]{:S(2)}, u32[]{:S(2)}) collective-permute-start(bf16[16,64,128]{2,1,0:T(8,128)(2,1)S(1)} %get-tuple-element.7), channel_id=1, source_target_pairs={{0,128},{16,48},{32,160},{48,80},{64,192},{80,112},{96,224},{112,1... | collective-permute-start | bytes 786440 | tf_op jit(solution)/shard_map/ppermute | solution.py:65
  55.6 5.2 %collective-permute-done.2 = bf16[16,64,128]{2,1,0:T(8,128)(2,1)S(1)} collective-permute-done((bf16[16,64,128]{2,1,0:T(8,128)(2,1)S(1)}, bf16[16,64,128]{2,1,0:T(8,128)(2,1)S(1)}, u32[]{:S(2)}, u32[]{:S(2)}) %collective-permute-start.2) | collective-permute-done | bytes 262176 | tf_op jit(solution)/shard_map/ppermute | solution.py:65
  61.0 4.9 %collective-permute-start.5 = (bf16[4,16,64,128]{3,2,1,0:T(8,128)(2,1)S(1)}, bf16[4,16,64,128]{3,2,1,0:T(8,128)(2,1)S(1)}, u32[]{:S(2)}, u32[]{:S(2)}) collective-permute-start(bf16[4,16,64,128]{3,2,1,0:T(8,128)(2,1)S(1)} %pad_maximum_fusion.refs_0_), channel_id=1, source_target_pairs={{0,96},{16,400},{32,0},{48,432},{64,32},{80,464},{96,64},{112,496}... | collective-permute-start | bytes 3145736 | tf_op jit(solution)/shard_map/ppermute | solution.py:65
  65.9 1.9 collective-permute-start.3
  69.8 8.4 %collective-permute-done.5.refs_4_ = bf16[4,16,64,128]{3,2,1,0:T(8,128)(2,1)S(1)} collective-permute-done((bf16[4,16,64,128]{3,2,1,0:T(8,128)(2,1)S(1)}, bf16[4,16,64,128]{3,2,1,0:T(8,128)(2,1)S(1)}, u32[]{:S(2)}, u32[]{:S(2)}) %collective-permute-start.5) | collective-permute-done | bytes 1048608 | tf_op jit(solution)/shard_map/ppermute | solution.py:65
  78.2 5.6 %collective-permute-start.6 = (bf16[2,16,64,128]{3,2,1,0:T(8,128)(2,1)S(1)}, bf16[2,16,64,128]{3,2,1,0:T(8,128)(2,1)S(1)}, u32[]{:S(2)}, u32[]{:S(2)}) collective-permute-start(bf16[2,16,64,128]{3,2,1,0:T(8,128)(2,1)S(1)} %slice.19), channel_id=1, source_target_pairs={{0,96},{16,400},{32,0},{48,432},{64,32},{80,464},{96,64},{112,496}... | collective-permute-start | bytes 1572872 | tf_op jit(solution)/shard_map/ppermute | solution.py:65
  88.8 2.4 %collective-permute-start.8 = (bf16[4,16,64,128]{3,2,1,0:T(8,128)(2,1)}, bf16[4,16,64,128]{3,2,1,0:T(8,128)(2,1)}, u32[]{:S(2)}, u32[]{:S(2)}) collective-permute-start(bf16[4,16,64,128]{3,2,1,0:T(8,128)(2,1)} %collective-permute-done.3.refs_1_), channel_id=1, source_target_pairs={{0,16},{16,0},{32,48},{48,32},{64,80},{80,64},{96,112},{112,96},{1... | collective-permute-start | bytes 3145736 | tf_op jit(solution)/shard_map/ppermute | solution.py:74
  93.2 6.1 %collective-permute-done.4.refs_2_ = bf16[2,16,64,128]{3,2,1,0:T(8,128)(2,1)} collective-permute-done((bf16[2,16,64,128]{3,2,1,0:T(8,128)(2,1)S(1)}, bf16[2,16,64,128]{3,2,1,0:T(8,128)(2,1)}, u32[]{:S(2)}, u32[]{:S(2)}) %collective-permute-start.4) | collective-permute-done | bytes 524320 | tf_op jit(solution)/shard_map/ppermute | solution.py:65
  104.4 7.4 %project.1 = bf16[16,128,128]{2,1,0:T(8,128)(2,1)S(1)} custom-call(s32[17]{0:T(128)S(1)} %dynamic-slice_bitcast_fusion.place_ref, bf16[128,2048]{1,0:T(8,128)(2,1)S(1)} %bitcast.16, bf16[16,1,128]{2,1,0:T(2,128)(2,1)S(1)} %slice.16.b_ref, bf16[4,16,64,128]{3,2,1,0:T(8,128)(2,1)S(1)} %pad_maximum_fusion.refs_0_, ...), custom_call_target="tpu_custom_call" | custom-call | flops 1073741824 | bytes 8388608 | tf_op jit(solution)/shard_map/project/pallas_call | solution.py:137
  112.7 12.0 %all-to-all-start.1 = ((bf16[16,128,128]{2,1,0:T(8,128)(2,1)}), bf16[16,128,128]{2,1,0:T(8,128)(2,1)}, u32[]{:S(2)}, u32[]{:S(2)}) async-start(bf16[16,128,128]{2,1,0:T(8,128)(2,1)} %copy-done.1), calls=%async_computation.1 | async-start | bytes 1048576 | tf_op jit(solution)/shard_map/all_to_all | solution.py:329
  124.7 14.5 %teacher_probs.1.p_ref = f32[2,2,1024,1024]{3,2,1,0:T(8,128)} custom-call(bf16[16,2,64,256]{3,2,1,0:T(8,128)(2,1)} %bitcast.9.t_ref), custom_call_target="tpu_custom_call" | custom-call | flops 1073741824 | bytes 16777216 | tf_op jit(solution)/shard_map/teacher_probs/pallas_call | solution.py:182
  139.2 14.8 %all-to-all-done.1 = bf16[16,128,128]{2,1,0:T(8,128)(2,1)} async-done(((bf16[16,128,128]{2,1,0:T(8,128)(2,1)}), bf16[16,128,128]{2,1,0:T(8,128)(2,1)}, u32[]{:S(2)}, u32[]{:S(2)}) %all-to-all-start.1) | async-done | bytes 524320 | tf_op jit(solution)/shard_map/all_to_all | solution.py:329
  154.0 15.3 %head_grads.1 = (bf16[16,2,64,128]{3,2,1,0:T(8,128)(2,1)S(1)}, f32[1,128]{1,0:T(1,128)S(1)}) custom-call(bf16[16,2,64,128]{3,2,1,0:T(8,128)(2,1)} %bitcast.7.s_ref, f32[2,2,1024,1024]{3,2,1,0:T(8,128)} %teacher_probs.1.p_ref), custom_call_target="tpu_custom_call" | custom-call | flops 3221225472 | bytes 16777216 | tf_op jit(solution)/shard_map/head_grads/pallas_call | solution.py:240
  170.1 6.5 %all-to-all-start.3 = ((bf16[16,128,128]{2,1,0:T(8,128)(2,1)}), bf16[16,128,128]{2,1,0:T(8,128)(2,1)}, u32[]{:S(2)}, u32[]{:S(2)}) async-start(bf16[16,128,128]{2,1,0:T(8,128)(2,1)} %bitcast.17), calls=%async_computation.3 | async-start | bytes 1048576 | tf_op jit(solution)/shard_map/all_to_all | solution.py:329
  181.6 3.5 %collective-permute-done.13 = f32[1,128]{1,0:T(1,128)S(1)} collective-permute-done((f32[1,128]{1,0:T(1,128)S(1)}, f32[1,128]{1,0:T(1,128)S(1)}, u32[]{:S(2)}, u32[]{:S(2)}) %collective-permute-start.13) | collective-permute-done | bytes 544 | tf_op jit(solution)/shard_map/ppermute | solution.py:323
  187.1 5.0 %collective-permute-done.14 = f32[1,128]{1,0:T(1,128)S(1)} collective-permute-done((f32[1,128]{1,0:T(1,128)S(1)}, f32[1,128]{1,0:T(1,128)S(1)}, u32[]{:S(2)}, u32[]{:S(2)}) %collective-permute-start.14) | collective-permute-done | bytes 544 | tf_op jit(solution)/shard_map/ppermute | solution.py:323
  194.0 3.5 %collective-permute-done.15 = f32[1,128]{1,0:T(1,128)S(1)} collective-permute-done((f32[1,128]{1,0:T(1,128)S(1)}, f32[1,128]{1,0:T(1,128)S(1)}, u32[]{:S(2)}, u32[]{:S(2)}) %collective-permute-start.15) | collective-permute-done | bytes 544 | tf_op jit(solution)/shard_map/ppermute | solution.py:323
  199.5 5.0 %collective-permute-done.16 = f32[1,128]{1,0:T(1,128)S(1)} collective-permute-done((f32[1,128]{1,0:T(1,128)S(1)}, f32[1,128]{1,0:T(1,128)S(1)}, u32[]{:S(2)}, u32[]{:S(2)}) %collective-permute-start.16) | collective-permute-done | bytes 544 | tf_op jit(solution)/shard_map/ppermute | solution.py:323
  205.8 9.4 %hidden_grads.1 = bf16[128,2048]{1,0:T(8,128)(2,1)} custom-call(s32[17]{0:T(128)S(1)} %dynamic-slice_bitcast_fusion.place_ref, bf16[16,128,128]{2,1,0:T(8,128)(2,1)} %all-to-all-done.3.g_ref, bf16[4,16,64,128]{3,2,1,0:T(8,128)(2,1)S(1)} %pad_maximum_fusion.refs_0_, bf16[4,16,64,128]{3,2,1,0:T(8,128)(2,1)} %collective-permute-done.3.refs_1_, ...), custom_call_target="tpu_custom_call" | custom-call | flops 1073741824 | bytes 8388608 | tf_op jit(solution)/shard_map/hidden_grads/pallas_call | solution.py:298
  (46 shorter events, 34.5 us)
Async XLA Ops:
  0.6 1.0 copy-start
  3.1 34.6 %all-to-all-start = ((bf16[16,72,128]{2,1,0:T(8,128)(2,1)}), bf16[16,72,128]{2,1,0:T(8,128)(2,1)S(1)}, u32[]{:S(2)}, u32[]{:S(2)}) async-start(bf16[16,72,128]{2,1,0:T(8,128)(2,1)} %broadcast_in_dim.12), calls=%async_computation | async-start | bytes 589824 | tf_op jit(solution)/shard_map/all_to_all | solution.py:329
  37.7 75.0 %all-to-all-start.2 = ((bf16[16,128,256]{2,1,0:T(8,128)(2,1)}), bf16[16,128,256]{2,1,0:T(8,128)(2,1)}, u32[]{:S(2)}, u32[]{:S(2)}) async-start(bf16[16,128,256]{2,1,0:T(8,128)(2,1)} %split_columns.1), calls=%async_computation.2 | async-start | bytes 2097152 | tf_op jit(solution)/shard_map/all_to_all | solution.py:329
  44.0 9.8 %collective-permute-start.1 = (bf16[16,64,128]{2,1,0:T(8,128)(2,1)S(1)}, bf16[16,64,128]{2,1,0:T(8,128)(2,1)S(1)}, u32[]{:S(2)}, u32[]{:S(2)}) collective-permute-start(bf16[16,64,128]{2,1,0:T(8,128)(2,1)S(1)} %get-tuple-element.7), channel_id=1, source_target_pairs={{0,256},{16,80},{32,288},{48,112},{64,320},{80,16},{96,352},{112,4... | collective-permute-start | bytes 786440 | tf_op jit(solution)/shard_map/ppermute | solution.py:65
  47.4 8.3 %collective-permute-start = (bf16[16,64,128]{2,1,0:T(8,128)(2,1)S(1)}, bf16[16,64,128]{2,1,0:T(8,128)(2,1)S(1)}, u32[]{:S(2)}, u32[]{:S(2)}) collective-permute-start(bf16[16,64,128]{2,1,0:T(8,128)(2,1)S(1)} %get-tuple-element.7), channel_id=1, source_target_pairs={{0,128},{16,48},{32,160},{48,80},{64,192},{80,112},{96,224},{112,1... | collective-permute-start | bytes 786440 | tf_op jit(solution)/shard_map/ppermute | solution.py:65
  51.4 9.5 %collective-permute-start.2 = (bf16[16,64,128]{2,1,0:T(8,128)(2,1)S(1)}, bf16[16,64,128]{2,1,0:T(8,128)(2,1)S(1)}, u32[]{:S(2)}, u32[]{:S(2)}) collective-permute-start(bf16[16,64,128]{2,1,0:T(8,128)(2,1)S(1)} %get-tuple-element.7), channel_id=1, source_target_pairs={{0,384},{16,112},{32,416},{48,16},{64,448},{80,48},{96,480},{112,8... | collective-permute-start | bytes 786440 | tf_op jit(solution)/shard_map/ppermute | solution.py:65
  61.0 17.2 %collective-permute-start.5 = (bf16[4,16,64,128]{3,2,1,0:T(8,128)(2,1)S(1)}, bf16[4,16,64,128]{3,2,1,0:T(8,128)(2,1)S(1)}, u32[]{:S(2)}, u32[]{:S(2)}) collective-permute-start(bf16[4,16,64,128]{3,2,1,0:T(8,128)(2,1)S(1)} %pad_maximum_fusion.refs_0_), channel_id=1, source_target_pairs={{0,96},{16,400},{32,0},{48,432},{64,32},{80,464},{96,64},{112,496}... | collective-permute-start | bytes 3145736 | tf_op jit(solution)/shard_map/ppermute | solution.py:65
  65.9 19.9 %collective-permute-start.3 = (bf16[4,16,64,128]{3,2,1,0:T(8,128)(2,1)S(1)}, bf16[4,16,64,128]{3,2,1,0:T(8,128)(2,1)}, u32[]{:S(2)}, u32[]{:S(2)}) collective-permute-start(bf16[4,16,64,128]{3,2,1,0:T(8,128)(2,1)S(1)} %pad_maximum_fusion.refs_0_), channel_id=1, source_target_pairs={{0,32},{16,144},{32,64},{48,176},{64,96},{80,208},{96,0},{112,240}... | collective-permute-start | bytes 3145736 | tf_op jit(solution)/shard_map/ppermute | solution.py:65
  67.8 34.1 %collective-permute-start.7 = (bf16[4,16,64,128]{3,2,1,0:T(8,128)(2,1)S(1)}, bf16[4,16,64,128]{3,2,1,0:T(8,128)(2,1)}, u32[]{:S(2)}, u32[]{:S(2)}) collective-permute-start(bf16[4,16,64,128]{3,2,1,0:T(8,128)(2,1)S(1)} %pad_maximum_fusion.refs_0_), channel_id=1, source_target_pairs={{0,16},{16,0},{32,48},{48,32},{64,80},{80,64},{96,112},{112,96},{1... | collective-permute-start | bytes 3145736 | tf_op jit(solution)/shard_map/ppermute | solution.py:74
  78.2 13.0 %collective-permute-start.6 = (bf16[2,16,64,128]{3,2,1,0:T(8,128)(2,1)S(1)}, bf16[2,16,64,128]{3,2,1,0:T(8,128)(2,1)S(1)}, u32[]{:S(2)}, u32[]{:S(2)}) collective-permute-start(bf16[2,16,64,128]{3,2,1,0:T(8,128)(2,1)S(1)} %slice.19), channel_id=1, source_target_pairs={{0,96},{16,400},{32,0},{48,432},{64,32},{80,464},{96,64},{112,496}... | collective-permute-start | bytes 1572872 | tf_op jit(solution)/shard_map/ppermute | solution.py:65
  83.9 18.1 %collective-permute-start.11 = (bf16[4,16,64,128]{3,2,1,0:T(8,128)(2,1)S(1)}, bf16[4,16,64,128]{3,2,1,0:T(8,128)(2,1)}, u32[]{:S(2)}, u32[]{:S(2)}) collective-permute-start(bf16[4,16,64,128]{3,2,1,0:T(8,128)(2,1)S(1)} %collective-permute-done.5.refs_4_), channel_id=1, source_target_pairs={{0,16},{16,0},{32,48},{48,32},{64,80},{80,64},{96,112},{112,96},{1... | collective-permute-start | bytes 3145736 | tf_op jit(solution)/shard_map/ppermute | solution.py:74
  86.9 12.4 %collective-permute-start.4 = (bf16[2,16,64,128]{3,2,1,0:T(8,128)(2,1)S(1)}, bf16[2,16,64,128]{3,2,1,0:T(8,128)(2,1)}, u32[]{:S(2)}, u32[]{:S(2)}) collective-permute-start(bf16[2,16,64,128]{3,2,1,0:T(8,128)(2,1)S(1)} %slice.18), channel_id=1, source_target_pairs={{0,32},{16,144},{32,64},{48,176},{64,96},{80,208},{96,0},{112,240}... | collective-permute-start | bytes 1572872 | tf_op jit(solution)/shard_map/ppermute | solution.py:65
  88.8 14.6 %collective-permute-start.8 = (bf16[4,16,64,128]{3,2,1,0:T(8,128)(2,1)}, bf16[4,16,64,128]{3,2,1,0:T(8,128)(2,1)}, u32[]{:S(2)}, u32[]{:S(2)}) collective-permute-start(bf16[4,16,64,128]{3,2,1,0:T(8,128)(2,1)} %collective-permute-done.3.refs_1_), channel_id=1, source_target_pairs={{0,16},{16,0},{32,48},{48,32},{64,80},{80,64},{96,112},{112,96},{1... | collective-permute-start | bytes 3145736 | tf_op jit(solution)/shard_map/ppermute | solution.py:74
  91.2 10.7 %collective-permute-start.10 = (bf16[2,16,64,128]{3,2,1,0:T(8,128)(2,1)S(1)}, bf16[2,16,64,128]{3,2,1,0:T(8,128)(2,1)}, u32[]{:S(2)}, u32[]{:S(2)}) collective-permute-start(bf16[2,16,64,128]{3,2,1,0:T(8,128)(2,1)S(1)} %collective-permute-done.6.refs_3_), channel_id=1, source_target_pairs={{0,16},{16,0},{32,48},{48,32},{64,80},{80,64},{96,112},{112,96},{1... | collective-permute-start | bytes 1572872 | tf_op jit(solution)/shard_map/ppermute | solution.py:74
  99.3 4.1 %collective-permute-start.9 = (bf16[2,16,64,128]{3,2,1,0:T(8,128)(2,1)}, bf16[2,16,64,128]{3,2,1,0:T(8,128)(2,1)}, u32[]{:S(2)}, u32[]{:S(2)}) collective-permute-start(bf16[2,16,64,128]{3,2,1,0:T(8,128)(2,1)} %collective-permute-done.4.refs_2_), channel_id=1, source_target_pairs={{0,16},{16,0},{32,48},{48,32},{64,80},{80,64},{96,112},{112,96},{1... | collective-permute-start | bytes 1572872 | tf_op jit(solution)/shard_map/ppermute | solution.py:74
  103.4 1.0 copy-start.2
  111.9 0.8 copy-start.1
  112.7 41.3 %all-to-all-start.1 = ((bf16[16,128,128]{2,1,0:T(8,128)(2,1)}), bf16[16,128,128]{2,1,0:T(8,128)(2,1)}, u32[]{:S(2)}, u32[]{:S(2)}) async-start(bf16[16,128,128]{2,1,0:T(8,128)(2,1)} %copy-done.1), calls=%async_computation.1 | async-start | bytes 1048576 | tf_op jit(solution)/shard_map/all_to_all | solution.py:329
  170.1 35.7 %all-to-all-start.3 = ((bf16[16,128,128]{2,1,0:T(8,128)(2,1)}), bf16[16,128,128]{2,1,0:T(8,128)(2,1)}, u32[]{:S(2)}, u32[]{:S(2)}) async-start(bf16[16,128,128]{2,1,0:T(8,128)(2,1)} %bitcast.17), calls=%async_computation.3 | async-start | bytes 1048576 | tf_op jit(solution)/shard_map/all_to_all | solution.py:329
  176.6 3.1 %collective-permute-start.12 = (f32[1,128]{1,0:T(1,128)S(1)}, f32[1,128]{1,0:T(1,128)S(1)}, u32[]{:S(2)}, u32[]{:S(2)}) collective-permute-start(f32[1,128]{1,0:T(1,128)S(1)} %get-tuple-element.5), channel_id=1, source_target_pairs={{0,16},{16,0},{32,48},{48,32},{64,80},{80,64},{96,112},{112,96},{1... | collective-permute-start | bytes 1544 | tf_op jit(solution)/shard_map/ppermute | solution.py:323
  179.7 5.5 %collective-permute-start.13 = (f32[1,128]{1,0:T(1,128)S(1)}, f32[1,128]{1,0:T(1,128)S(1)}, u32[]{:S(2)}, u32[]{:S(2)}) collective-permute-start(f32[1,128]{1,0:T(1,128)S(1)} %add.24), channel_id=1, source_target_pairs={{0,32},{16,48},{32,0},{48,16},{64,96},{80,112},{96,64},{112,80},{1... | collective-permute-start | bytes 1544 | tf_op jit(solution)/shard_map/ppermute | solution.py:323
  185.1 7.0 %collective-permute-start.14 = (f32[1,128]{1,0:T(1,128)S(1)}, f32[1,128]{1,0:T(1,128)S(1)}, u32[]{:S(2)}, u32[]{:S(2)}) collective-permute-start(f32[1,128]{1,0:T(1,128)S(1)} %add.25), channel_id=1, source_target_pairs={{0,64},{16,80},{32,96},{48,112},{64,0},{80,16},{96,32},{112,48},{1... | collective-permute-start | bytes 1544 | tf_op jit(solution)/shard_map/ppermute | solution.py:323
  192.1 5.5 %collective-permute-start.15 = (f32[1,128]{1,0:T(1,128)S(1)}, f32[1,128]{1,0:T(1,128)S(1)}, u32[]{:S(2)}, u32[]{:S(2)}) collective-permute-start(f32[1,128]{1,0:T(1,128)S(1)} %add.26), channel_id=1, source_target_pairs={{0,128},{16,144},{32,160},{48,176},{64,192},{80,208},{96,224},{112... | collective-permute-start | bytes 1544 | tf_op jit(solution)/shard_map/ppermute | solution.py:323
  197.5 7.0 %collective-permute-start.16 = (f32[1,128]{1,0:T(1,128)S(1)}, f32[1,128]{1,0:T(1,128)S(1)}, u32[]{:S(2)}, u32[]{:S(2)}) collective-permute-start(f32[1,128]{1,0:T(1,128)S(1)} %add.27), channel_id=1, source_target_pairs={{0,256},{16,272},{32,288},{48,304},{64,320},{80,336},{96,352},{112... | collective-permute-start | bytes 1544 | tf_op jit(solution)/shard_map/ppermute | solution.py:323
  (1 other events, 0.8 us)

commit v3 on v2

--- a/solution.py
+++ b/solution.py
@@ -64,14 +64,16 @@
     def send(v, shift, first):
         return lax.ppermute(v, "dp", ring_pairs(shift, first))
 
-    near = [send(piece, k, True) for k in (1, -1, 2)]
-    own = jnp.stack([piece, near[0], near[2], near[1]])
-    down, up = send(own, 1, False), send(own, -1, False)
-    half = SIDE // 2
-    low, high = send(down[:half], 1, False), send(up[half:], -1, False)
-    mine = [own, down, low, high, up]
+    below, above, far = [send(piece, k, True) for k in (1, -1, 2)]
+    own = [jnp.stack([piece, below]), jnp.stack([far, above])]
+    down0, up1 = send(own[0], 1, False), send(own[1], -1, False)
+    down1, up0 = send(own[1], 1, False), send(own[0], -1, False)
+    far0, far1 = send(down0, 1, False), send(up1, -1, False)
     swap = [(d, d ^ 1) for d in range(2 * SIDE * SIDE)]
-    theirs = [lax.ppermute(v, "dp", swap) for v in mine]
+    mine, theirs = [], []
+    for parts in (own, [down0, down1], [far0, far1], [up0, up1]):
+        theirs += [lax.ppermute(v, "dp", swap) for v in parts]
+        mine += parts
     return mine + theirs
 
 
@@ -89,19 +91,22 @@
 
 
 def weight_block(refs, core, k):
+    half = SIDE // 2
+    count = len(refs) // 2
+
     def pick(side, b, j):
-        part = refs[5 * side : 5 * side + 5]
-        if b == 2:
-            half = SIDE // 2
-            return part[2 + j // half][j % half, k]
-        return part[{0: 0, 1: 1, 3: 4}[b]][j, k]
+        return refs[(side ^ core) * count + 2 * b + j // half][j % half, k]
 
     rows = []
     for j in range(SIDE):
         for b in range(SIDE):
-            rows.append(jnp.where(core == 0, pick(0, b, j), pick(1, b, j)))
-            rows.append(jnp.where(core == 0, pick(1, j, b), pick(0, j, b)))
+            rows += [pick(0, b, j), pick(1, j, b)]
     return jnp.concatenate(rows, axis=0)
+
+
+def on_core(core, step):
+    for c in range(2):
+        pl.when(core == c)(lambda c=c: step(c))
 
 
 def weight_specs(weights, pair):
@@ -126,13 +131,16 @@
                 at = pl.multiple_of(place_ref[m] * LANE, LANE)
                 h[:, m * LANE : (m + 1) * LANE] = h_ref[:, pl.ds(at, LANE)]
 
-        core = place_ref[width // LANE]
-        w = jnp.concatenate(
-            [weight_block(w_refs, core, k) for k in range(pair)], axis=1
-        )
-        r = dot(h[...], w, NN)
-        for k in range(pair):
-            o_ref[k] = (r[:, k * cols : (k + 1) * cols] + b_ref[k].astype(F32)).astype(BF16)
+        def step(core):
+            w = jnp.concatenate(
+                [weight_block(w_refs, core, k) for k in range(pair)], axis=1
+            )
+            r = dot(h[...], w, NN)
+            for k in range(pair):
+                v = r[:, k * cols : (k + 1) * cols] + b_ref[k].astype(F32)
+                o_ref[k] = v.astype(BF16)
+
+        on_core(place_ref[width // LANE], step)
 
     return pl.pallas_call(
         kernel,
@@ -274,20 +282,19 @@
     def kernel(place_ref, g_ref, *refs):
         w_refs, o_ref, acc = refs[:count], refs[count], refs[count + 1]
         t = pl.program_id(0)
-        core = place_ref[width // LANE]
-        w = jnp.concatenate(
-            [weight_block(w_refs, core, k) for k in range(pair)], axis=1
-        )
-        g = jnp.concatenate([g_ref[k] for k in range(pair)], axis=1)
-        r = dot(g, w, NT)
 
         @pl.when(t == 0)
         def _():
-            acc[...] = r
-
-        @pl.when(t > 0)
-        def _():
-            acc[...] += r
+            acc[...] = jnp.zeros_like(acc)
+
+        def step(core):
+            w = jnp.concatenate(
+                [weight_block(w_refs, core, k) for k in range(pair)], axis=1
+            )
+            g = jnp.concatenate([g_ref[k] for k in range(pair)], axis=1)
+            acc[...] += dot(g, w, NT)
+
+        on_core(place_ref[width // LANE], step)
 
         @pl.when(t == last)
         def _():

time: 217 us -> 217 us (level)
  the two profiles are of different devices: /device:TPU:6 before, /device:TPU:16 now
where the time goes in v3:
time: 217 us; the launch traced here: 214 us
  starting transfers between devices  99.6 us (46%)
  Pallas kernels  53 us (24%)
  waiting for transfers between devices  47.2 us (22%)
  local copies, waits for them, and re-layouts  12.4 us (6%)
    all_to_all x4, starting transfers between devices, exchange(): return lax.all_to_all(x, 'tok', split_axis=0, concat_axis=0, tiled=True)  39.9 us
    ppermute x9, starting transfers between devices, send(): return lax.ppermute(v, 'dp', ring_pairs(shift, first))  28.8 us
    all_to_all x4, waiting for transfers between devices, exchange(): return lax.all_to_all(x, 'tok', split_axis=0, concat_axis=0, tiled=True)  27.5 us
    ppermute x8, starting transfers between devices, gather_weight(): theirs += [lax.ppermute(v, 'dp', swap) for v in parts]  18.9 us
    ppermute x5, waiting for transfers between devices, sum_over(): x = x + lax.ppermute(x, axis, [(i, i ^ reach) for i in range(size)])  15.8 us
    pallas_call x1, Pallas kernels, head_grads(): pl.pallas_call(kernel, grid=(seqs, length // step), in_specs=[pl.BlockSpe...  15.3 us
    pallas_call x1, Pallas kernels, teacher_probs(): pl.pallas_call(kernel, grid=(seqs, heads, length // step), in_specs=[pl.B...  13.1 us
    ppermute x5, starting transfers between devices, sum_over(): x = x + lax.ppermute(x, axis, [(i, i ^ reach) for i in range(size)])  12 us
  transfers between devices with their start and end apart: 26, of which 10 were waited for; matrix products, arithmetic and copies ran while one was open for 1% of the time, Pallas kernels for 14%

profile of v3, /device:TPU:16, one launch (start us, length us, event | category | flops | bytes accessed | tf_op | source)
XLA Modules:
  0.0 213.9 jit_solution(12328572936160994775)
XLA Ops:
  3.1 15.2 %all-to-all-start = ((bf16[16,72,128]{2,1,0:T(8,128)(2,1)}), bf16[16,72,128]{2,1,0:T(8,128)(2,1)S(1)}, u32[]{:S(2)}, u32[]{:S(2)}) async-start(bf16[16,72,128]{2,1,0:T(8,128)(2,1)} %broadcast_in_dim.12), calls=%async_computation | async-start | bytes 589824 | tf_op jit(solution)/shard_map/all_to_all | solution.py:336
  18.3 8.8 %split_columns.1 = bf16[16,128,256]{2,1,0:T(8,128)(2,1)} custom-call(bf16[128,4096]{1,0:T(8,128)(2,1)} %bitcast.19), custom_call_target="tpu_custom_call" | custom-call | tf_op jit(solution)/shard_map/split_columns/pallas_call | solution.py:36
  27.1 10.5 %all-to-all-done = bf16[16,72,128]{2,1,0:T(8,128)(2,1)S(1)} async-done(((bf16[16,72,128]{2,1,0:T(8,128)(2,1)}), bf16[16,72,128]{2,1,0:T(8,128)(2,1)S(1)}, u32[]{:S(2)}, u32[]{:S(2)}) %all-to-all-start) | async-done | bytes 294944 | tf_op jit(solution)/shard_map/all_to_all | solution.py:336
  37.7 6.2 %all-to-all-start.2 = ((bf16[16,128,256]{2,1,0:T(8,128)(2,1)}), bf16[16,128,256]{2,1,0:T(8,128)(2,1)S(1)}, u32[]{:S(2)}, u32[]{:S(2)}) async-start(bf16[16,128,256]{2,1,0:T(8,128)(2,1)} %split_columns.1), calls=%async_computation.2 | async-start | bytes 2097152 | tf_op jit(solution)/shard_map/all_to_all | solution.py:336
  43.9 4.9 %collective-permute-start.1 = (bf16[16,64,128]{2,1,0:T(8,128)(2,1)S(1)}, bf16[16,64,128]{2,1,0:T(8,128)(2,1)S(1)}, u32[]{:S(2)}, u32[]{:S(2)}) collective-permute-start(bf16[16,64,128]{2,1,0:T(8,128)(2,1)S(1)} %get-tuple-element.7), channel_id=1, source_target_pairs={{0,256},{16,80},{32,288},{48,112},{64,320},{80,16},{96,352},{112,4... | collective-permute-start | bytes 786440 | tf_op jit(solution)/shard_map/ppermute | solution.py:65
  48.9 3.0 %collective-permute-start.2 = (bf16[16,64,128]{2,1,0:T(8,128)(2,1)S(1)}, bf16[16,64,128]{2,1,0:T(8,128)(2,1)S(1)}, u32[]{:S(2)}, u32[]{:S(2)}) collective-permute-start(bf16[16,64,128]{2,1,0:T(8,128)(2,1)S(1)} %get-tuple-element.7), channel_id=1, source_target_pairs={{0,384},{16,112},{32,416},{48,16},{64,448},{80,48},{96,480},{112,8... | collective-permute-start | bytes 786440 | tf_op jit(solution)/shard_map/ppermute | solution.py:65
  51.9 2.8 %collective-permute-start = (bf16[16,64,128]{2,1,0:T(8,128)(2,1)S(1)}, bf16[16,64,128]{2,1,0:T(8,128)(2,1)S(1)}, u32[]{:S(2)}, u32[]{:S(2)}) collective-permute-start(bf16[16,64,128]{2,1,0:T(8,128)(2,1)S(1)} %get-tuple-element.7), channel_id=1, source_target_pairs={{0,128},{16,48},{32,160},{48,80},{64,192},{80,112},{96,224},{112,1... | collective-permute-start | bytes 786440 | tf_op jit(solution)/shard_map/ppermute | solution.py:65
  61.5 3.5 %collective-permute-start.4 = (bf16[2,16,64,128]{3,2,1,0:T(8,128)(2,1)S(1)}, bf16[2,16,64,128]{3,2,1,0:T(8,128)(2,1)}, u32[]{:S(2)}, u32[]{:S(2)}) collective-permute-start(bf16[2,16,64,128]{3,2,1,0:T(8,128)(2,1)S(1)} %pad_maximum_fusion.1.refs_1_), channel_id=1, source_target_pairs={{0,32},{16,144},{32,64},{48,176},{64,96},{80,208},{96,0},{112,240}... | collective-permute-start | bytes 1572872 | tf_op jit(solution)/shard_map/ppermute | solution.py:65
  65.1 4.4 %collective-permute-start.3 = (bf16[2,16,64,128]{3,2,1,0:T(8,128)(2,1)S(1)}, bf16[2,16,64,128]{3,2,1,0:T(8,128)(2,1)}, u32[]{:S(2)}, u32[]{:S(2)}) collective-permute-start(bf16[2,16,64,128]{3,2,1,0:T(8,128)(2,1)S(1)} %pad_maximum_fusion.refs_0_), channel_id=1, source_target_pairs={{0,32},{16,144},{32,64},{48,176},{64,96},{80,208},{96,0},{112,240}... | collective-permute-start | bytes 1572872 | tf_op jit(solution)/shard_map/ppermute | solution.py:65
  73.3 4.5 %collective-permute-start.16 = (bf16[2,16,64,128]{3,2,1,0:T(8,128)(2,1)S(1)}, bf16[2,16,64,128]{3,2,1,0:T(8,128)(2,1)S(1)}, u32[]{:S(2)}, u32[]{:S(2)}) collective-permute-start(bf16[2,16,64,128]{3,2,1,0:T(8,128)(2,1)S(1)} %collective-permute-done.6.refs_7_), channel_id=1, source_target_pairs={{0,16},{16,0},{32,48},{48,32},{64,80},{80,64},{96,112},{112,96},{1... | collective-permute-start | bytes 1572872 | tf_op jit(solution)/shard_map/ppermute | solution.py:75
  80.6 3.9 %collective-permute-start.5 = (bf16[2,16,64,128]{3,2,1,0:T(8,128)(2,1)}, bf16[2,16,64,128]{3,2,1,0:T(8,128)(2,1)}, u32[]{:S(2)}, u32[]{:S(2)}) collective-permute-start(bf16[2,16,64,128]{3,2,1,0:T(8,128)(2,1)} %collective-permute-done.3.refs_2_), channel_id=1, source_target_pairs={{0,32},{16,144},{32,64},{48,176},{64,96},{80,208},{96,0},{112,240}... | collective-permute-start | bytes 1572872 | tf_op jit(solution)/shard_map/ppermute | solution.py:65
  87.2 2.4 %collective-permute-start.12 = (bf16[2,16,64,128]{3,2,1,0:T(8,128)(2,1)}, bf16[2,16,64,128]{3,2,1,0:T(8,128)(2,1)}, u32[]{:S(2)}, u32[]{:S(2)}) collective-permute-start(bf16[2,16,64,128]{3,2,1,0:T(8,128)(2,1)} %collective-permute-done.4.refs_3_), channel_id=1, source_target_pairs={{0,16},{16,0},{32,48},{48,32},{64,80},{80,64},{96,112},{112,96},{1... | collective-permute-start | bytes 1572872 | tf_op jit(solution)/shard_map/ppermute | solution.py:75
  103.1 7.1 %project.1 = bf16[16,128,128]{2,1,0:T(8,128)(2,1)S(1)} custom-call(s32[17]{0:T(128)S(1)} %dynamic-slice_bitcast_fusion.place_ref, bf16[128,2048]{1,0:T(8,128)(2,1)S(1)} %bitcast.17, bf16[16,1,128]{2,1,0:T(2,128)(2,1)S(1)} %slice.8.b_ref, bf16[2,16,64,128]{3,2,1,0:T(8,128)(2,1)S(1)} %pad_maximum_fusion.refs_0_, ...), custom_call_target="tpu_custom_call" | custom-call | flops 1073741824 | bytes 8388608 | tf_op jit(solution)/shard_map/project/pallas_call | solution.py:145
  111.0 12.1 %all-to-all-start.1 = ((bf16[16,128,128]{2,1,0:T(8,128)(2,1)}), bf16[16,128,128]{2,1,0:T(8,128)(2,1)}, u32[]{:S(2)}, u32[]{:S(2)}) async-start(bf16[16,128,128]{2,1,0:T(8,128)(2,1)} %copy-done.10), calls=%async_computation.1 | async-start | bytes 1048576 | tf_op jit(solution)/shard_map/all_to_all | solution.py:336
  123.1 13.1 %teacher_probs.1.p_ref = f32[2,2,1024,1024]{3,2,1,0:T(8,128)} custom-call(bf16[16,2,64,256]{3,2,1,0:T(8,128)(2,1)S(1)} %bitcast.16), custom_call_target="tpu_custom_call" | custom-call | flops 1073741824 | bytes 16777216 | tf_op jit(solution)/shard_map/teacher_probs/pallas_call | solution.py:190
  136.2 16.2 %all-to-all-done.1 = bf16[16,128,128]{2,1,0:T(8,128)(2,1)} async-done(((bf16[16,128,128]{2,1,0:T(8,128)(2,1)}), bf16[16,128,128]{2,1,0:T(8,128)(2,1)}, u32[]{:S(2)}, u32[]{:S(2)}) %all-to-all-start.1) | async-done | bytes 524320 | tf_op jit(solution)/shard_map/all_to_all | solution.py:336
  152.3 15.3 %head_grads.1 = (bf16[16,2,64,128]{3,2,1,0:T(8,128)(2,1)S(1)}, f32[1,128]{1,0:T(1,128)S(1)}) custom-call(bf16[16,2,64,128]{3,2,1,0:T(8,128)(2,1)} %bitcast.7.s_ref, f32[2,2,1024,1024]{3,2,1,0:T(8,128)} %teacher_probs.1.p_ref), custom_call_target="tpu_custom_call" | custom-call | flops 3221225472 | bytes 16777216 | tf_op jit(solution)/shard_map/head_grads/pallas_call | solution.py:248
  168.4 6.5 %all-to-all-start.3 = ((bf16[16,128,128]{2,1,0:T(8,128)(2,1)}), bf16[16,128,128]{2,1,0:T(8,128)(2,1)}, u32[]{:S(2)}, u32[]{:S(2)}) async-start(bf16[16,128,128]{2,1,0:T(8,128)(2,1)} %bitcast.18), calls=%async_computation.3 | async-start | bytes 1048576 | tf_op jit(solution)/shard_map/all_to_all | solution.py:336
  178.0 3.1 %collective-permute-start.18 = (f32[1,128]{1,0:T(1,128)S(1)}, f32[1,128]{1,0:T(1,128)S(1)}, u32[]{:S(2)}, u32[]{:S(2)}) collective-permute-start(f32[1,128]{1,0:T(1,128)S(1)} %add.24), channel_id=1, source_target_pairs={{0,32},{16,48},{32,0},{48,16},{64,96},{80,112},{96,64},{112,80},{1... | collective-permute-start | bytes 1544 | tf_op jit(solution)/shard_map/ppermute | solution.py:330
  185.8 4.6 %collective-permute-done.19 = f32[1,128]{1,0:T(1,128)S(1)} collective-permute-done((f32[1,128]{1,0:T(1,128)S(1)}, f32[1,128]{1,0:T(1,128)S(1)}, u32[]{:S(2)}, u32[]{:S(2)}) %collective-permute-start.19) | collective-permute-done | bytes 544 | tf_op jit(solution)/shard_map/ppermute | solution.py:330
  192.3 3.5 %collective-permute-done.20 = f32[1,128]{1,0:T(1,128)S(1)} collective-permute-done((f32[1,128]{1,0:T(1,128)S(1)}, f32[1,128]{1,0:T(1,128)S(1)}, u32[]{:S(2)}, u32[]{:S(2)}) %collective-permute-start.20) | collective-permute-done | bytes 544 | tf_op jit(solution)/shard_map/ppermute | solution.py:330
  195.9 2.7 %collective-permute-start.21 = (f32[1,128]{1,0:T(1,128)S(1)}, f32[1,128]{1,0:T(1,128)S(1)}, u32[]{:S(2)}, u32[]{:S(2)}) collective-permute-start(f32[1,128]{1,0:T(1,128)S(1)} %add.27), channel_id=1, source_target_pairs={{0,256},{16,272},{32,288},{48,304},{64,320},{80,336},{96,352},{112... | collective-permute-start | bytes 1544 | tf_op jit(solution)/shard_map/ppermute | solution.py:330
  198.6 4.2 %collective-permute-done.21 = f32[1,128]{1,0:T(1,128)S(1)} collective-permute-done((f32[1,128]{1,0:T(1,128)S(1)}, f32[1,128]{1,0:T(1,128)S(1)}, u32[]{:S(2)}, u32[]{:S(2)}) %collective-permute-start.21) | collective-permute-done | bytes 544 | tf_op jit(solution)/shard_map/ppermute | solution.py:330
  205.2 8.8 %hidden_grads.1 = bf16[128,2048]{1,0:T(8,128)(2,1)} custom-call(s32[17]{0:T(128)S(1)} %dynamic-slice_bitcast_fusion.place_ref, bf16[16,128,128]{2,1,0:T(8,128)(2,1)} %all-to-all-done.3.g_ref, bf16[2,16,64,128]{3,2,1,0:T(8,128)(2,1)S(1)} %pad_maximum_fusion.refs_0_, bf16[2,16,64,128]{3,2,1,0:T(8,128)(2,1)S(1)} %pad_maximum_fusion.1.refs_1_, ...), custom_call_target="tpu_custom_call" | custom-call | flops 1073741824 | bytes 8388608 | tf_op jit(solution)/shard_map/hidden_grads/pallas_call | solution.py:305
  (73 shorter events, 45.5 us)
Async XLA Ops:
  3.1 34.6 %all-to-all-start = ((bf16[16,72,128]{2,1,0:T(8,128)(2,1)}), bf16[16,72,128]{2,1,0:T(8,128)(2,1)S(1)}, u32[]{:S(2)}, u32[]{:S(2)}) async-start(bf16[16,72,128]{2,1,0:T(8,128)(2,1)} %broadcast_in_dim.12), calls=%async_computation | async-start | bytes 589824 | tf_op jit(solution)/shard_map/all_to_all | solution.py:336
  37.7 73.3 %all-to-all-start.2 = ((bf16[16,128,256]{2,1,0:T(8,128)(2,1)}), bf16[16,128,256]{2,1,0:T(8,128)(2,1)S(1)}, u32[]{:S(2)}, u32[]{:S(2)}) async-start(bf16[16,128,256]{2,1,0:T(8,128)(2,1)} %split_columns.1), calls=%async_computation.2 | async-start | bytes 2097152 | tf_op jit(solution)/shard_map/all_to_all | solution.py:336
  43.9 10.8 %collective-permute-start.1 = (bf16[16,64,128]{2,1,0:T(8,128)(2,1)S(1)}, bf16[16,64,128]{2,1,0:T(8,128)(2,1)S(1)}, u32[]{:S(2)}, u32[]{:S(2)}) collective-permute-start(bf16[16,64,128]{2,1,0:T(8,128)(2,1)S(1)} %get-tuple-element.7), channel_id=1, source_target_pairs={{0,256},{16,80},{32,288},{48,112},{64,320},{80,16},{96,352},{112,4... | collective-permute-start | bytes 786440 | tf_op jit(solution)/shard_map/ppermute | solution.py:65
  48.9 8.3 %collective-permute-start.2 = (bf16[16,64,128]{2,1,0:T(8,128)(2,1)S(1)}, bf16[16,64,128]{2,1,0:T(8,128)(2,1)S(1)}, u32[]{:S(2)}, u32[]{:S(2)}) collective-permute-start(bf16[16,64,128]{2,1,0:T(8,128)(2,1)S(1)} %get-tuple-element.7), channel_id=1, source_target_pairs={{0,384},{16,112},{32,416},{48,16},{64,448},{80,48},{96,480},{112,8... | collective-permute-start | bytes 786440 | tf_op jit(solution)/shard_map/ppermute | solution.py:65
  51.9 13.1 %collective-permute-start = (bf16[16,64,128]{2,1,0:T(8,128)(2,1)S(1)}, bf16[16,64,128]{2,1,0:T(8,128)(2,1)S(1)}, u32[]{:S(2)}, u32[]{:S(2)}) collective-permute-start(bf16[16,64,128]{2,1,0:T(8,128)(2,1)S(1)} %get-tuple-element.7), channel_id=1, source_target_pairs={{0,128},{16,48},{32,160},{48,80},{64,192},{80,112},{96,224},{112,1... | collective-permute-start | bytes 786440 | tf_op jit(solution)/shard_map/ppermute | solution.py:65
  57.2 14.2 %collective-permute-start.10 = (bf16[2,16,64,128]{3,2,1,0:T(8,128)(2,1)S(1)}, bf16[2,16,64,128]{3,2,1,0:T(8,128)(2,1)S(1)}, u32[]{:S(2)}, u32[]{:S(2)}) collective-permute-start(bf16[2,16,64,128]{3,2,1,0:T(8,128)(2,1)S(1)} %pad_maximum_fusion.1.refs_1_), channel_id=1, source_target_pairs={{0,16},{16,0},{32,48},{48,32},{64,80},{80,64},{96,112},{112,96},{1... | collective-permute-start | bytes 1572872 | tf_op jit(solution)/shard_map/ppermute | solution.py:75
  59.1 14.2 %collective-permute-start.6 = (bf16[2,16,64,128]{3,2,1,0:T(8,128)(2,1)S(1)}, bf16[2,16,64,128]{3,2,1,0:T(8,128)(2,1)S(1)}, u32[]{:S(2)}, u32[]{:S(2)}) collective-permute-start(bf16[2,16,64,128]{3,2,1,0:T(8,128)(2,1)S(1)} %pad_maximum_fusion.1.refs_1_), channel_id=1, source_target_pairs={{0,96},{16,400},{32,0},{48,432},{64,32},{80,464},{96,64},{112,496}... | collective-permute-start | bytes 1572872 | tf_op jit(solution)/shard_map/ppermute | solution.py:65
  61.5 16.3 %collective-permute-start.4 = (bf16[2,16,64,128]{3,2,1,0:T(8,128)(2,1)S(1)}, bf16[2,16,64,128]{3,2,1,0:T(8,128)(2,1)}, u32[]{:S(2)}, u32[]{:S(2)}) collective-permute-start(bf16[2,16,64,128]{3,2,1,0:T(8,128)(2,1)S(1)} %pad_maximum_fusion.1.refs_1_), channel_id=1, source_target_pairs={{0,32},{16,144},{32,64},{48,176},{64,96},{80,208},{96,0},{112,240}... | collective-permute-start | bytes 1572872 | tf_op jit(solution)/shard_map/ppermute | solution.py:65
  65.1 15.5 %collective-permute-start.3 = (bf16[2,16,64,128]{3,2,1,0:T(8,128)(2,1)S(1)}, bf16[2,16,64,128]{3,2,1,0:T(8,128)(2,1)}, u32[]{:S(2)}, u32[]{:S(2)}) collective-permute-start(bf16[2,16,64,128]{3,2,1,0:T(8,128)(2,1)S(1)} %pad_maximum_fusion.refs_0_), channel_id=1, source_target_pairs={{0,32},{16,144},{32,64},{48,176},{64,96},{80,208},{96,0},{112,240}... | collective-permute-start | bytes 1572872 | tf_op jit(solution)/shard_map/ppermute | solution.py:65
  69.5 15.0 %collective-permute-start.9 = (bf16[2,16,64,128]{3,2,1,0:T(8,128)(2,1)S(1)}, bf16[2,16,64,128]{3,2,1,0:T(8,128)(2,1)S(1)}, u32[]{:S(2)}, u32[]{:S(2)}) collective-permute-start(bf16[2,16,64,128]{3,2,1,0:T(8,128)(2,1)S(1)} %pad_maximum_fusion.refs_0_), channel_id=1, source_target_pairs={{0,16},{16,0},{32,48},{48,32},{64,80},{80,64},{96,112},{112,96},{1... | collective-permute-start | bytes 1572872 | tf_op jit(solution)/shard_map/ppermute | solution.py:75
  71.4 15.8 %collective-permute-start.8 = (bf16[2,16,64,128]{3,2,1,0:T(8,128)(2,1)S(1)}, bf16[2,16,64,128]{3,2,1,0:T(8,128)(2,1)}, u32[]{:S(2)}, u32[]{:S(2)}) collective-permute-start(bf16[2,16,64,128]{3,2,1,0:T(8,128)(2,1)S(1)} %pad_maximum_fusion.refs_0_), channel_id=1, source_target_pairs={{0,96},{16,400},{32,0},{48,432},{64,32},{80,464},{96,64},{112,496}... | collective-permute-start | bytes 1572872 | tf_op jit(solution)/shard_map/ppermute | solution.py:65
  73.3 16.3 %collective-permute-start.16 = (bf16[2,16,64,128]{3,2,1,0:T(8,128)(2,1)S(1)}, bf16[2,16,64,128]{3,2,1,0:T(8,128)(2,1)S(1)}, u32[]{:S(2)}, u32[]{:S(2)}) collective-permute-start(bf16[2,16,64,128]{3,2,1,0:T(8,128)(2,1)S(1)} %collective-permute-done.6.refs_7_), channel_id=1, source_target_pairs={{0,16},{16,0},{32,48},{48,32},{64,80},{80,64},{96,112},{112,96},{1... | collective-permute-start | bytes 1572872 | tf_op jit(solution)/shard_map/ppermute | solution.py:75
  77.8 14.5 %collective-permute-start.7 = (bf16[2,16,64,128]{3,2,1,0:T(8,128)(2,1)S(1)}, bf16[2,16,64,128]{3,2,1,0:T(8,128)(2,1)}, u32[]{:S(2)}, u32[]{:S(2)}) collective-permute-start(bf16[2,16,64,128]{3,2,1,0:T(8,128)(2,1)S(1)} %collective-permute-done.6.refs_7_), channel_id=1, source_target_pairs={{0,96},{16,400},{32,0},{48,432},{64,32},{80,464},{96,64},{112,496}... | collective-permute-start | bytes 1572872 | tf_op jit(solution)/shard_map/ppermute | solution.py:65
  80.6 14.2 %collective-permute-start.5 = (bf16[2,16,64,128]{3,2,1,0:T(8,128)(2,1)}, bf16[2,16,64,128]{3,2,1,0:T(8,128)(2,1)}, u32[]{:S(2)}, u32[]{:S(2)}) collective-permute-start(bf16[2,16,64,128]{3,2,1,0:T(8,128)(2,1)} %collective-permute-done.3.refs_2_), channel_id=1, source_target_pairs={{0,32},{16,144},{32,64},{48,176},{64,96},{80,208},{96,0},{112,240}... | collective-permute-start | bytes 1572872 | tf_op jit(solution)/shard_map/ppermute | solution.py:65
  85.3 12.2 %collective-permute-start.11 = (bf16[2,16,64,128]{3,2,1,0:T(8,128)(2,1)}, bf16[2,16,64,128]{3,2,1,0:T(8,128)(2,1)}, u32[]{:S(2)}, u32[]{:S(2)}) collective-permute-start(bf16[2,16,64,128]{3,2,1,0:T(8,128)(2,1)} %collective-permute-done.3.refs_2_), channel_id=1, source_target_pairs={{0,16},{16,0},{32,48},{48,32},{64,80},{80,64},{96,112},{112,96},{1... | collective-permute-start | bytes 1572872 | tf_op jit(solution)/shard_map/ppermute | solution.py:75
  87.2 10.2 %collective-permute-start.12 = (bf16[2,16,64,128]{3,2,1,0:T(8,128)(2,1)}, bf16[2,16,64,128]{3,2,1,0:T(8,128)(2,1)}, u32[]{:S(2)}, u32[]{:S(2)}) collective-permute-start(bf16[2,16,64,128]{3,2,1,0:T(8,128)(2,1)} %collective-permute-done.4.refs_3_), channel_id=1, source_target_pairs={{0,16},{16,0},{32,48},{48,32},{64,80},{80,64},{96,112},{112,96},{1... | collective-permute-start | bytes 1572872 | tf_op jit(solution)/shard_map/ppermute | solution.py:75
  90.4 7.0 %collective-permute-start.15 = (bf16[2,16,64,128]{3,2,1,0:T(8,128)(2,1)}, bf16[2,16,64,128]{3,2,1,0:T(8,128)(2,1)}, u32[]{:S(2)}, u32[]{:S(2)}) collective-permute-start(bf16[2,16,64,128]{3,2,1,0:T(8,128)(2,1)} %collective-permute-done.8.refs_6_), channel_id=1, source_target_pairs={{0,16},{16,0},{32,48},{48,32},{64,80},{80,64},{96,112},{112,96},{1... | collective-permute-start | bytes 1572872 | tf_op jit(solution)/shard_map/ppermute | solution.py:75
  92.4 5.1 %collective-permute-start.14 = (bf16[2,16,64,128]{3,2,1,0:T(8,128)(2,1)}, bf16[2,16,64,128]{3,2,1,0:T(8,128)(2,1)}, u32[]{:S(2)}, u32[]{:S(2)}) collective-permute-start(bf16[2,16,64,128]{3,2,1,0:T(8,128)(2,1)} %collective-permute-done.7.refs_5_), channel_id=1, source_target_pairs={{0,16},{16,0},{32,48},{48,32},{64,80},{80,64},{96,112},{112,96},{1... | collective-permute-start | bytes 1572872 | tf_op jit(solution)/shard_map/ppermute | solution.py:75
  111.0 41.3 %all-to-all-start.1 = ((bf16[16,128,128]{2,1,0:T(8,128)(2,1)}), bf16[16,128,128]{2,1,0:T(8,128)(2,1)}, u32[]{:S(2)}, u32[]{:S(2)}) async-start(bf16[16,128,128]{2,1,0:T(8,128)(2,1)} %copy-done.10), calls=%async_computation.1 | async-start | bytes 1048576 | tf_op jit(solution)/shard_map/all_to_all | solution.py:336
  168.4 35.7 %all-to-all-start.3 = ((bf16[16,128,128]{2,1,0:T(8,128)(2,1)}), bf16[16,128,128]{2,1,0:T(8,128)(2,1)}, u32[]{:S(2)}, u32[]{:S(2)}) async-start(bf16[16,128,128]{2,1,0:T(8,128)(2,1)} %bitcast.18), calls=%async_computation.3 | async-start | bytes 1048576 | tf_op jit(solution)/shard_map/all_to_all | solution.py:336
  178.0 5.5 %collective-permute-start.18 = (f32[1,128]{1,0:T(1,128)S(1)}, f32[1,128]{1,0:T(1,128)S(1)}, u32[]{:S(2)}, u32[]{:S(2)}) collective-permute-start(f32[1,128]{1,0:T(1,128)S(1)} %add.24), channel_id=1, source_target_pairs={{0,32},{16,48},{32,0},{48,16},{64,96},{80,112},{96,64},{112,80},{1... | collective-permute-start | bytes 1544 | tf_op jit(solution)/shard_map/ppermute | solution.py:330
  183.5 7.0 %collective-permute-start.19 = (f32[1,128]{1,0:T(1,128)S(1)}, f32[1,128]{1,0:T(1,128)S(1)}, u32[]{:S(2)}, u32[]{:S(2)}) collective-permute-start(f32[1,128]{1,0:T(1,128)S(1)} %add.25), channel_id=1, source_target_pairs={{0,64},{16,80},{32,96},{48,112},{64,0},{80,16},{96,32},{112,48},{1... | collective-permute-start | bytes 1544 | tf_op jit(solution)/shard_map/ppermute | solution.py:330
  190.4 5.5 %collective-permute-start.20 = (f32[1,128]{1,0:T(1,128)S(1)}, f32[1,128]{1,0:T(1,128)S(1)}, u32[]{:S(2)}, u32[]{:S(2)}) collective-permute-start(f32[1,128]{1,0:T(1,128)S(1)} %add.26), channel_id=1, source_target_pairs={{0,128},{16,144},{32,160},{48,176},{64,192},{80,208},{96,224},{112... | collective-permute-start | bytes 1544 | tf_op jit(solution)/shard_map/ppermute | solution.py:330
  195.9 7.0 %collective-permute-start.21 = (f32[1,128]{1,0:T(1,128)S(1)}, f32[1,128]{1,0:T(1,128)S(1)}, u32[]{:S(2)}, u32[]{:S(2)}) collective-permute-start(f32[1,128]{1,0:T(1,128)S(1)} %add.27), channel_id=1, source_target_pairs={{0,256},{16,272},{32,288},{48,304},{64,320},{80,336},{96,352},{112... | collective-permute-start | bytes 1544 | tf_op jit(solution)/shard_map/ppermute | solution.py:330
  (15 other events, 153.4 us)

commit v4 on v3

--- a/solution.py
+++ b/solution.py
@@ -43,8 +43,36 @@
     )(x)
 
 
+def copies_of_piece(weight, bias, group, depth, copies):
+    cols = weight.shape[1]
+
+    def kernel(g_ref, b_ref, w_ref, o_ref, held, ready):
+        at = pl.multiple_of(g_ref[0] * depth, depth)
+        copy = pltpu.make_async_copy(w_ref.at[pl.ds(at, depth)], held, ready)
+        copy.start()
+        copy.wait()
+        tail = jnp.broadcast_to(b_ref[...], (8, cols))
+        for t in range(copies):
+            o_ref[t, :depth] = held[...]
+            o_ref[t, depth:] = tail
+
+    return pl.pallas_call(
+        kernel,
+        in_specs=[
+            pl.BlockSpec(memory_space=pltpu.SMEM),
+            pl.BlockSpec(memory_space=pltpu.VMEM),
+            pl.BlockSpec(memory_space=pltpu.HBM),
+        ],
+        out_specs=pl.BlockSpec(memory_space=pltpu.VMEM),
+        out_shape=jax.ShapeDtypeStruct((copies, depth + 8, cols), BF16),
+        scratch_shapes=[pltpu.VMEM((depth, cols), BF16), pltpu.SemaphoreType.DMA],
+        name="copies_of_piece",
+    )(group, bias, weight)
+
+
 SIDE = 4
 LANE = 128
+TAKE = 8
 
 
 def ring_pairs(shift, first):
@@ -90,12 +118,11 @@
     )
 
 
-def weight_block(refs, core, k):
+def weight_block(held, t):
     half = SIDE // 2
-    count = len(refs) // 2
 
     def pick(side, b, j):
-        return refs[(side ^ core) * count + 2 * b + j // half][j % half, k]
+        return held[side, 2 * b + j // half, j % half, t]
 
     rows = []
     for j in range(SIDE):
@@ -104,57 +131,72 @@
     return jnp.concatenate(rows, axis=0)
 
 
-def on_core(core, step):
-    for c in range(2):
-        pl.when(core == c)(lambda c=c: step(c))
-
-
-def weight_specs(weights, pair):
-    return [
-        pl.BlockSpec((w.shape[0], pair) + w.shape[2:], lambda t, place: (0, t, 0, 0))
-        for w in weights
-    ]
+class Stream:
+    def __init__(self, refs, held, sems, core, take):
+        self.refs, self.held, self.sems = refs, held, sems
+        self.core, self.take = core, take
+
+    def start(self):
+        count = len(self.refs) // 2
+        blocks = self.held.shape[3]
+        for n in range(blocks // self.take):
+            span = pl.ds(n * self.take, self.take)
+            for a, ref in enumerate(self.refs):
+                side = self.core if a < count else 1 - self.core
+                pltpu.make_async_copy(
+                    ref.at[:, span], self.held.at[side, a % count, :, span], self.sems.at[n]
+                ).start()
+
+    def wait(self, n):
+        span = pl.ds(n * self.take, self.take)
+        part = self.held.at[:, :, :, span]
+        pltpu.make_async_copy(part, part, self.sems.at[n]).wait()
 
 
 def project(hidden, weights, bias, place):
     rows, width = hidden.shape
-    blocks, cols = weights[0].shape[1], weights[0].shape[3]
+    half, blocks, depth, cols = weights[0].shape
     pair = 2
     count = len(weights)
+    chips = width // LANE
 
     def kernel(place_ref, h_ref, b_ref, *refs):
-        w_refs, o_ref, h = refs[:count], refs[count], refs[count + 1]
-
-        @pl.when(pl.program_id(0) == 0)
-        def _():
-            for m in range(width // LANE):
-                at = pl.multiple_of(place_ref[m] * LANE, LANE)
-                h[:, m * LANE : (m + 1) * LANE] = h_ref[:, pl.ds(at, LANE)]
-
-        def step(core):
+        w_refs, o_ref, raw, h, held, ready, sems = refs[:count], *refs[count:]
+        copy = pltpu.make_async_copy(h_ref, raw, ready)
+        copy.start()
+        stream = Stream(w_refs, held, sems, place_ref[chips], TAKE)
+        stream.start()
+        copy.wait()
+        for m in range(chips):
+            at = pl.multiple_of(place_ref[m] * LANE, LANE)
+            h[:, m * LANE : (m + 1) * LANE] = raw[:, pl.ds(at, LANE)]
+        for n in range(blocks // pair):
+            if n * pair % TAKE == 0:
+                stream.wait(n * pair // TAKE)
             w = jnp.concatenate(
-                [weight_block(w_refs, core, k) for k in range(pair)], axis=1
+                [weight_block(held, n * pair + k) for k in range(pair)], axis=1
             )
             r = dot(h[...], w, NN)
             for k in range(pair):
-                v = r[:, k * cols : (k + 1) * cols] + b_ref[k].astype(F32)
-                o_ref[k] = v.astype(BF16)
-
-        on_core(place_ref[width // LANE], step)
+                v = r[:, k * cols : (k + 1) * cols] + b_ref[n * pair + k].astype(F32)
+                o_ref[n * pair + k] = v.astype(BF16)
 
     return pl.pallas_call(
         kernel,
-        grid_spec=pltpu.PrefetchScalarGridSpec(
-            num_scalar_prefetch=1,
-            grid=(blocks // pair,),
-            in_specs=[
-                pl.BlockSpec((rows, width), lambda t, place: (0, 0)),
-                pl.BlockSpec((pair, 1, cols), lambda t, place: (t, 0, 0)),
-            ]
-            + weight_specs(weights, pair),
-            out_specs=pl.BlockSpec((pair, rows, cols), lambda t, place: (t, 0, 0)),
-            scratch_shapes=[pltpu.VMEM((rows, width), BF16)],
-        ),
+        in_specs=[
+            pl.BlockSpec(memory_space=pltpu.SMEM),
+            pl.BlockSpec(memory_space=pltpu.HBM),
+            pl.BlockSpec(memory_space=pltpu.VMEM),
+        ]
+        + [pl.BlockSpec(memory_space=pl.ANY)] * count,
+        out_specs=pl.BlockSpec(memory_space=pltpu.VMEM),
+        scratch_shapes=[
+            pltpu.VMEM((rows, width), BF16),
+            pltpu.VMEM((rows, width), BF16),
+            pltpu.VMEM((2, count // 2, half, blocks, depth, cols), BF16),
+            pltpu.SemaphoreType.DMA,
+            pltpu.SemaphoreType.DMA((blocks // TAKE,)),
+        ],
         out_shape=jax.ShapeDtypeStruct((blocks, rows, cols), BF16),
         compiler_params=params(32),
         cost_estimate=pl.CostEstimate(
@@ -211,7 +253,7 @@
     toks = both // seqs
     length = blocks * toks
     heads = cols // SH
-    step = 256
+    step = 512
     part = step // toks
     last = length // step - 1
 
@@ -274,44 +316,45 @@
 
 def hidden_grads(grads, weights, place):
     blocks, rows, cols = grads.shape
-    width = weights[0].shape[2] * 2 * SIDE * SIDE
+    half, _, depth, _ = weights[0].shape
+    count = len(weights)
+    width = count * half * depth
     pair = 2
-    count = len(weights)
-    last = blocks // pair - 1
+    chips = width // LANE
 
     def kernel(place_ref, g_ref, *refs):
-        w_refs, o_ref, acc = refs[:count], refs[count], refs[count + 1]
-        t = pl.program_id(0)
-
-        @pl.when(t == 0)
-        def _():
-            acc[...] = jnp.zeros_like(acc)
-
-        def step(core):
+        w_refs, o_ref, acc, held, sems = refs[:count], *refs[count:]
+        stream = Stream(w_refs, held, sems, place_ref[chips], TAKE)
+        stream.start()
+        for n in range(blocks // pair):
+            if n * pair % TAKE == 0:
+                stream.wait(n * pair // TAKE)
             w = jnp.concatenate(
-                [weight_block(w_refs, core, k) for k in range(pair)], axis=1
+                [weight_block(held, n * pair + k) for k in range(pair)], axis=1
             )
-            g = jnp.concatenate([g_ref[k] for k in range(pair)], axis=1)
-            acc[...] += dot(g, w, NT)
-
-        on_core(place_ref[width // LANE], step)
-
-        @pl.when(t == last)
-        def _():
-            for m in range(width // LANE):
-                at = pl.multiple_of(place_ref[m] * LANE, LANE)
-                o_ref[:, pl.ds(at, LANE)] = acc[:, m * LANE : (m + 1) * LANE].astype(BF16)
+            g = jnp.concatenate([g_ref[n * pair + k] for k in range(pair)], axis=1)
+            r = dot(g, w, NT)
+            if n == 0:
+                acc[...] = r
+            else:
+                acc[...] += r
+        for m in range(chips):
+            at = pl.multiple_of(place_ref[m] * LANE, LANE)
+            o_ref[:, pl.ds(at, LANE)] = acc[:, m * LANE : (m + 1) * LANE].astype(BF16)
 
     return pl.pallas_call(
         kernel,
-        grid_spec=pltpu.PrefetchScalarGridSpec(
-            num_scalar_prefetch=1,
-            grid=(blocks // pair,),
-            in_specs=[pl.BlockSpec((pair, rows, cols), lambda t, place: (t, 0, 0))]
-            + weight_specs(weights, pair),
-            out_specs=pl.BlockSpec((rows, width), lambda t, place: (0, 0)),
-            scratch_shapes=[pltpu.VMEM((rows, width), F32)],
-        ),
+        in_specs=[
+            pl.BlockSpec(memory_space=pltpu.SMEM),
+            pl.BlockSpec(memory_space=pltpu.VMEM),
+        ]
+        + [pl.BlockSpec(memory_space=pl.ANY)] * count,
+        out_specs=pl.BlockSpec(memory_space=pltpu.VMEM),
+        scratch_shapes=[
+            pltpu.VMEM((rows, width), F32),
+            pltpu.VMEM((2, count // 2, half, blocks, depth, cols), BF16),
+            pltpu.SemaphoreType.DMA((blocks // TAKE,)),
+        ],
         out_shape=jax.ShapeDtypeStruct((rows, width), BF16),
         compiler_params=params(32),
         cost_estimate=pl.CostEstimate(
@@ -339,12 +382,11 @@
 def body(student_hidden, teacher_values, value_weight, value_bias):
     seqs, toks, width = student_hidden.shape
     groups, parts = lax.axis_size("dp"), lax.axis_size("tok")
-    cols = value_weight.shape[1]
     depth = width // groups
 
-    piece = lax.dynamic_slice_in_dim(value_weight, lax.axis_index("dp") * depth, depth)
-    piece = jnp.concatenate([piece, jnp.broadcast_to(value_bias, (8, cols))], axis=0)
-    pieces = exchange(jnp.broadcast_to(piece, (parts, depth + 8, cols)))
+    group = lax.axis_index("dp").astype(jnp.int32)[None]
+    piece = copies_of_piece(value_weight, value_bias, group, depth, parts)
+    pieces = exchange(piece)
     bias = pieces[:, depth : depth + 1]
 
     columns = split_columns(teacher_values.reshape(seqs * toks, -1), parts)

time: 217 us -> 204 us (0.940)
  the two profiles are of different devices: /device:TPU:16 before, /device:TPU:24 now
where the time goes in v4:
time: 204 us; the launch traced here: 202 us
  starting transfers between devices  101 us (50%)
  waiting for transfers between devices  46.5 us (23%)
  Pallas kernels  46.1 us (23%)
  local copies, waits for them, and re-layouts  7.07 us (3%)
    all_to_all x4, starting transfers between devices, exchange(): return lax.all_to_all(x, 'tok', split_axis=0, concat_axis=0, tiled=True)  40 us
    ppermute x9, starting transfers between devices, send(): return lax.ppermute(v, 'dp', ring_pairs(shift, first))  31.3 us
    all_to_all x4, waiting for transfers between devices, exchange(): return lax.all_to_all(x, 'tok', split_axis=0, concat_axis=0, tiled=True)  27.4 us
    ppermute x8, starting transfers between devices, gather_weight(): theirs += [lax.ppermute(v, 'dp', swap) for v in parts]  16.9 us
    ppermute x5, waiting for transfers between devices, sum_over(): x = x + lax.ppermute(x, axis, [(i, i ^ reach) for i in range(size)])  15.1 us
    pallas_call x1, Pallas kernels, teacher_probs(): pl.pallas_call(kernel, grid=(seqs, heads, length // step), in_specs=[pl.B...  13.2 us
    ppermute x5, starting transfers between devices, sum_over(): x = x + lax.ppermute(x, axis, [(i, i ^ reach) for i in range(size)])  12.7 us
    pallas_call x1, Pallas kernels, head_grads(): pl.pallas_call(kernel, grid=(seqs, length // step), in_specs=[pl.BlockSpe...  11.6 us
  transfers between devices with their start and end apart: 26, of which 10 were waited for; matrix products, arithmetic and copies ran while one was open for 1% of the time, Pallas kernels for 13%

profile of v4, /device:TPU:24, one launch (start us, length us, event | category | flops | bytes accessed | tf_op | source)
XLA Modules:
  0.0 202.1 jit_solution(8521234595895400831)
XLA Ops:
  2.8 15.2 %all-to-all-start = ((bf16[16,72,128]{2,1,0:T(8,128)(2,1)}), bf16[16,72,128]{2,1,0:T(8,128)(2,1)S(1)}, u32[]{:S(2)}, u32[]{:S(2)}) async-start(bf16[16,72,128]{2,1,0:T(8,128)(2,1)} %copies_of_piece.1), calls=%async_computation | async-start | bytes 589824 | tf_op jit(solution)/shard_map/all_to_all | solution.py:379
  18.0 8.8 %split_columns.1 = bf16[16,128,256]{2,1,0:T(8,128)(2,1)} custom-call(bf16[128,4096]{1,0:T(8,128)(2,1)} %bitcast.19), custom_call_target="tpu_custom_call" | custom-call | tf_op jit(solution)/shard_map/split_columns/pallas_call | solution.py:36
  26.8 10.6 %all-to-all-done = bf16[16,72,128]{2,1,0:T(8,128)(2,1)S(1)} async-done(((bf16[16,72,128]{2,1,0:T(8,128)(2,1)}), bf16[16,72,128]{2,1,0:T(8,128)(2,1)S(1)}, u32[]{:S(2)}, u32[]{:S(2)}) %all-to-all-start) | async-done | bytes 294944 | tf_op jit(solution)/shard_map/all_to_all | solution.py:379
  37.4 6.2 %all-to-all-start.2 = ((bf16[16,128,256]{2,1,0:T(8,128)(2,1)}), bf16[16,128,256]{2,1,0:T(8,128)(2,1)S(1)}, u32[]{:S(2)}, u32[]{:S(2)}) async-start(bf16[16,128,256]{2,1,0:T(8,128)(2,1)} %split_columns.1), calls=%async_computation.2 | async-start | bytes 2097152 | tf_op jit(solution)/shard_map/all_to_all | solution.py:379
  43.6 4.9 %collective-permute-start.1 = (bf16[16,64,128]{2,1,0:T(8,128)(2,1)S(1)}, bf16[16,64,128]{2,1,0:T(8,128)(2,1)S(1)}, u32[]{:S(2)}, u32[]{:S(2)}) collective-permute-start(bf16[16,64,128]{2,1,0:T(8,128)(2,1)S(1)} %get-tuple-element.7), channel_id=1, source_target_pairs={{0,256},{16,80},{32,288},{48,112},{64,320},{80,16},{96,352},{112,4... | collective-permute-start | bytes 786440 | tf_op jit(solution)/shard_map/ppermute | solution.py:93
  48.6 3.0 %collective-permute-start.2 = (bf16[16,64,128]{2,1,0:T(8,128)(2,1)S(1)}, bf16[16,64,128]{2,1,0:T(8,128)(2,1)S(1)}, u32[]{:S(2)}, u32[]{:S(2)}) collective-permute-start(bf16[16,64,128]{2,1,0:T(8,128)(2,1)S(1)} %get-tuple-element.7), channel_id=1, source_target_pairs={{0,384},{16,112},{32,416},{48,16},{64,448},{80,48},{96,480},{112,8... | collective-permute-start | bytes 786440 | tf_op jit(solution)/shard_map/ppermute | solution.py:93
  51.6 2.8 %collective-permute-start = (bf16[16,64,128]{2,1,0:T(8,128)(2,1)S(1)}, bf16[16,64,128]{2,1,0:T(8,128)(2,1)S(1)}, u32[]{:S(2)}, u32[]{:S(2)}) collective-permute-start(bf16[16,64,128]{2,1,0:T(8,128)(2,1)S(1)} %get-tuple-element.7), channel_id=1, source_target_pairs={{0,128},{16,48},{32,160},{48,80},{64,192},{80,112},{96,224},{112,1... | collective-permute-start | bytes 786440 | tf_op jit(solution)/shard_map/ppermute | solution.py:93
  61.5 4.4 %collective-permute-start.4 = (bf16[2,16,64,128]{3,2,1,0:T(8,128)(2,1)S(1)}, bf16[2,16,64,128]{3,2,1,0:T(8,128)(2,1)}, u32[]{:S(2)}, u32[]{:S(2)}) collective-permute-start(bf16[2,16,64,128]{3,2,1,0:T(8,128)(2,1)S(1)} %pad_maximum_fusion.1.refs_1_), channel_id=1, source_target_pairs={{0,32},{16,144},{32,64},{48,176},{64,96},{80,208},{96,0},{112,240}... | collective-permute-start | bytes 1572872 | tf_op jit(solution)/shard_map/ppermute | solution.py:93
  69.8 3.9 %collective-permute-start.8 = (bf16[2,16,64,128]{3,2,1,0:T(8,128)(2,1)S(1)}, bf16[2,16,64,128]{3,2,1,0:T(8,128)(2,1)}, u32[]{:S(2)}, u32[]{:S(2)}) collective-permute-start(bf16[2,16,64,128]{3,2,1,0:T(8,128)(2,1)S(1)} %pad_maximum_fusion.refs_0_), channel_id=1, source_target_pairs={{0,96},{16,400},{32,0},{48,432},{64,32},{80,464},{96,64},{112,496}... | collective-permute-start | bytes 1572872 | tf_op jit(solution)/shard_map/ppermute | solution.py:93
  76.2 3.9 %collective-permute-start.7 = (bf16[2,16,64,128]{3,2,1,0:T(8,128)(2,1)S(1)}, bf16[2,16,64,128]{3,2,1,0:T(8,128)(2,1)}, u32[]{:S(2)}, u32[]{:S(2)}) collective-permute-start(bf16[2,16,64,128]{3,2,1,0:T(8,128)(2,1)S(1)} %collective-permute-done.6.refs_7_), channel_id=1, source_target_pairs={{0,96},{16,400},{32,0},{48,432},{64,32},{80,464},{96,64},{112,496}... | collective-permute-start | bytes 1572872 | tf_op jit(solution)/shard_map/ppermute | solution.py:93
  80.2 3.7 %collective-permute-start.5 = (bf16[2,16,64,128]{3,2,1,0:T(8,128)(2,1)}, bf16[2,16,64,128]{3,2,1,0:T(8,128)(2,1)}, u32[]{:S(2)}, u32[]{:S(2)}) collective-permute-start(bf16[2,16,64,128]{3,2,1,0:T(8,128)(2,1)} %collective-permute-done.3.refs_2_), channel_id=1, source_target_pairs={{0,32},{16,144},{32,64},{48,176},{64,96},{80,208},{96,0},{112,240}... | collective-permute-start | bytes 1572872 | tf_op jit(solution)/shard_map/ppermute | solution.py:93
  101.5 3.9 %project.1 = bf16[16,128,128]{2,1,0:T(8,128)(2,1)S(1)} custom-call(s32[17]{0:T(128)S(1)} %dynamic-slice_bitcast_fusion.place_ref, bf16[128,2048]{1,0:T(8,128)(2,1)S(1)} %bitcast.17, bf16[16,1,128]{2,1,0:T(2,128)(2,1)S(1)} %slice.8.b_ref, bf16[2,16,64,128]{3,2,1,0:T(8,128)(2,1)S(1)} %pad_maximum_fusion.refs_0_, ...), custom_call_target="tpu_custom_call" | custom-call | flops 1073741824 | bytes 8388608 | tf_op jit(solution)/shard_map/project/pallas_call | solution.py:184
  106.1 12.1 %all-to-all-start.1 = ((bf16[16,128,128]{2,1,0:T(8,128)(2,1)}), bf16[16,128,128]{2,1,0:T(8,128)(2,1)}, u32[]{:S(2)}, u32[]{:S(2)}) async-start(bf16[16,128,128]{2,1,0:T(8,128)(2,1)} %copy-done.6), calls=%async_computation.1 | async-start | bytes 1048576 | tf_op jit(solution)/shard_map/all_to_all | solution.py:379
  118.2 13.2 %teacher_probs.1.p_ref = f32[2,2,1024,1024]{3,2,1,0:T(8,128)} custom-call(bf16[16,2,64,256]{3,2,1,0:T(8,128)(2,1)S(1)} %bitcast.16), custom_call_target="tpu_custom_call" | custom-call | flops 1073741824 | bytes 16777216 | tf_op jit(solution)/shard_map/teacher_probs/pallas_call | solution.py:232
  131.4 16.1 %all-to-all-done.1 = bf16[16,128,128]{2,1,0:T(8,128)(2,1)} async-done(((bf16[16,128,128]{2,1,0:T(8,128)(2,1)}), bf16[16,128,128]{2,1,0:T(8,128)(2,1)}, u32[]{:S(2)}, u32[]{:S(2)}) %all-to-all-start.1) | async-done | bytes 524320 | tf_op jit(solution)/shard_map/all_to_all | solution.py:379
  147.5 11.6 %head_grads.1 = (bf16[16,2,64,128]{3,2,1,0:T(8,128)(2,1)S(1)}, f32[1,128]{1,0:T(1,128)S(1)}) custom-call(bf16[16,2,64,128]{3,2,1,0:T(8,128)(2,1)} %bitcast.7.s_ref, f32[2,2,1024,1024]{3,2,1,0:T(8,128)} %teacher_probs.1.p_ref), custom_call_target="tpu_custom_call" | custom-call | flops 3221225472 | bytes 16777216 | tf_op jit(solution)/shard_map/head_grads/pallas_call | solution.py:290
  159.9 6.5 %all-to-all-start.3 = ((bf16[16,128,128]{2,1,0:T(8,128)(2,1)}), bf16[16,128,128]{2,1,0:T(8,128)(2,1)}, u32[]{:S(2)}, u32[]{:S(2)}) async-start(bf16[16,128,128]{2,1,0:T(8,128)(2,1)} %bitcast.18), calls=%async_computation.3 | async-start | bytes 1048576 | tf_op jit(solution)/shard_map/all_to_all | solution.py:379
  171.7 3.3 %collective-permute-done.18 = f32[1,128]{1,0:T(1,128)S(1)} collective-permute-done((f32[1,128]{1,0:T(1,128)S(1)}, f32[1,128]{1,0:T(1,128)S(1)}, u32[]{:S(2)}, u32[]{:S(2)}) %collective-permute-start.18) | collective-permute-done | bytes 544 | tf_op jit(solution)/shard_map/ppermute | solution.py:373
  177.2 4.8 %collective-permute-done.19 = f32[1,128]{1,0:T(1,128)S(1)} collective-permute-done((f32[1,128]{1,0:T(1,128)S(1)}, f32[1,128]{1,0:T(1,128)S(1)}, u32[]{:S(2)}, u32[]{:S(2)}) %collective-permute-start.19) | collective-permute-done | bytes 544 | tf_op jit(solution)/shard_map/ppermute | solution.py:373
  182.0 2.7 %collective-permute-start.20 = (f32[1,128]{1,0:T(1,128)S(1)}, f32[1,128]{1,0:T(1,128)S(1)}, u32[]{:S(2)}, u32[]{:S(2)}) collective-permute-start(f32[1,128]{1,0:T(1,128)S(1)} %add.22), channel_id=1, source_target_pairs={{0,128},{16,144},{32,160},{48,176},{64,192},{80,208},{96,224},{112... | collective-permute-start | bytes 1544 | tf_op jit(solution)/shard_map/ppermute | solution.py:373
  184.7 2.7 %collective-permute-done.20 = f32[1,128]{1,0:T(1,128)S(1)} collective-permute-done((f32[1,128]{1,0:T(1,128)S(1)}, f32[1,128]{1,0:T(1,128)S(1)}, u32[]{:S(2)}, u32[]{:S(2)}) %collective-permute-start.20) | collective-permute-done | bytes 544 | tf_op jit(solution)/shard_map/ppermute | solution.py:373
  187.4 3.7 %collective-permute-start.21 = (f32[1,128]{1,0:T(1,128)S(1)}, f32[1,128]{1,0:T(1,128)S(1)}, u32[]{:S(2)}, u32[]{:S(2)}) collective-permute-start(f32[1,128]{1,0:T(1,128)S(1)} %add.23), channel_id=1, source_target_pairs={{0,256},{16,272},{32,288},{48,304},{64,320},{80,336},{96,352},{112... | collective-permute-start | bytes 1544 | tf_op jit(solution)/shard_map/ppermute | solution.py:373
  191.1 3.3 %collective-permute-done.21 = f32[1,128]{1,0:T(1,128)S(1)} collective-permute-done((f32[1,128]{1,0:T(1,128)S(1)}, f32[1,128]{1,0:T(1,128)S(1)}, u32[]{:S(2)}, u32[]{:S(2)}) %collective-permute-start.21) | collective-permute-done | bytes 544 | tf_op jit(solution)/shard_map/ppermute | solution.py:373
  195.7 6.4 %hidden_grads.1 = bf16[128,2048]{1,0:T(8,128)(2,1)} custom-call(s32[17]{0:T(128)S(1)} %dynamic-slice_bitcast_fusion.place_ref, bf16[16,128,128]{2,1,0:T(8,128)(2,1)} %all-to-all-done.3.g_ref, bf16[2,16,64,128]{3,2,1,0:T(8,128)(2,1)S(1)} %pad_maximum_fusion.refs_0_, bf16[2,16,64,128]{3,2,1,0:T(8,128)(2,1)S(1)} %pad_maximum_fusion.1.refs_1_, ...), custom_call_target="tpu_custom_call" | custom-call | flops 1073741824 | bytes 8388608 | tf_op jit(solution)/shard_map/hidden_grads/pallas_call | solution.py:345
  (62 shorter events, 43.3 us)
Async XLA Ops:
  2.8 34.6 %all-to-all-start = ((bf16[16,72,128]{2,1,0:T(8,128)(2,1)}), bf16[16,72,128]{2,1,0:T(8,128)(2,1)S(1)}, u32[]{:S(2)}, u32[]{:S(2)}) async-start(bf16[16,72,128]{2,1,0:T(8,128)(2,1)} %copies_of_piece.1), calls=%async_computation | async-start | bytes 589824 | tf_op jit(solution)/shard_map/all_to_all | solution.py:379
  37.4 68.8 %all-to-all-start.2 = ((bf16[16,128,256]{2,1,0:T(8,128)(2,1)}), bf16[16,128,256]{2,1,0:T(8,128)(2,1)S(1)}, u32[]{:S(2)}, u32[]{:S(2)}) async-start(bf16[16,128,256]{2,1,0:T(8,128)(2,1)} %split_columns.1), calls=%async_computation.2 | async-start | bytes 2097152 | tf_op jit(solution)/shard_map/all_to_all | solution.py:379
  43.6 10.8 %collective-permute-start.1 = (bf16[16,64,128]{2,1,0:T(8,128)(2,1)S(1)}, bf16[16,64,128]{2,1,0:T(8,128)(2,1)S(1)}, u32[]{:S(2)}, u32[]{:S(2)}) collective-permute-start(bf16[16,64,128]{2,1,0:T(8,128)(2,1)S(1)} %get-tuple-element.7), channel_id=1, source_target_pairs={{0,256},{16,80},{32,288},{48,112},{64,320},{80,16},{96,352},{112,4... | collective-permute-start | bytes 786440 | tf_op jit(solution)/shard_map/ppermute | solution.py:93
  48.6 8.3 %collective-permute-start.2 = (bf16[16,64,128]{2,1,0:T(8,128)(2,1)S(1)}, bf16[16,64,128]{2,1,0:T(8,128)(2,1)S(1)}, u32[]{:S(2)}, u32[]{:S(2)}) collective-permute-start(bf16[16,64,128]{2,1,0:T(8,128)(2,1)S(1)} %get-tuple-element.7), channel_id=1, source_target_pairs={{0,384},{16,112},{32,416},{48,16},{64,448},{80,48},{96,480},{112,8... | collective-permute-start | bytes 786440 | tf_op jit(solution)/shard_map/ppermute | solution.py:93
  51.6 14.3 %collective-permute-start = (bf16[16,64,128]{2,1,0:T(8,128)(2,1)S(1)}, bf16[16,64,128]{2,1,0:T(8,128)(2,1)S(1)}, u32[]{:S(2)}, u32[]{:S(2)}) collective-permute-start(bf16[16,64,128]{2,1,0:T(8,128)(2,1)S(1)} %get-tuple-element.7), channel_id=1, source_target_pairs={{0,128},{16,48},{32,160},{48,80},{64,192},{80,112},{96,224},{112,1... | collective-permute-start | bytes 786440 | tf_op jit(solution)/shard_map/ppermute | solution.py:93
  56.9 12.9 %collective-permute-start.10 = (bf16[2,16,64,128]{3,2,1,0:T(8,128)(2,1)S(1)}, bf16[2,16,64,128]{3,2,1,0:T(8,128)(2,1)S(1)}, u32[]{:S(2)}, u32[]{:S(2)}) collective-permute-start(bf16[2,16,64,128]{3,2,1,0:T(8,128)(2,1)S(1)} %pad_maximum_fusion.1.refs_1_), channel_id=1, source_target_pairs={{0,16},{16,0},{32,48},{48,32},{64,80},{80,64},{96,112},{112,96},{1... | collective-permute-start | bytes 1572872 | tf_op jit(solution)/shard_map/ppermute | solution.py:103
  58.8 14.9 %collective-permute-start.6 = (bf16[2,16,64,128]{3,2,1,0:T(8,128)(2,1)S(1)}, bf16[2,16,64,128]{3,2,1,0:T(8,128)(2,1)S(1)}, u32[]{:S(2)}, u32[]{:S(2)}) collective-permute-start(bf16[2,16,64,128]{3,2,1,0:T(8,128)(2,1)S(1)} %pad_maximum_fusion.1.refs_1_), channel_id=1, source_target_pairs={{0,96},{16,400},{32,0},{48,432},{64,32},{80,464},{96,64},{112,496}... | collective-permute-start | bytes 1572872 | tf_op jit(solution)/shard_map/ppermute | solution.py:93
  61.5 14.8 %collective-permute-start.4 = (bf16[2,16,64,128]{3,2,1,0:T(8,128)(2,1)S(1)}, bf16[2,16,64,128]{3,2,1,0:T(8,128)(2,1)}, u32[]{:S(2)}, u32[]{:S(2)}) collective-permute-start(bf16[2,16,64,128]{3,2,1,0:T(8,128)(2,1)S(1)} %pad_maximum_fusion.1.refs_1_), channel_id=1, source_target_pairs={{0,32},{16,144},{32,64},{48,176},{64,96},{80,208},{96,0},{112,240}... | collective-permute-start | bytes 1572872 | tf_op jit(solution)/shard_map/ppermute | solution.py:93
  66.0 14.2 %collective-permute-start.3 = (bf16[2,16,64,128]{3,2,1,0:T(8,128)(2,1)S(1)}, bf16[2,16,64,128]{3,2,1,0:T(8,128)(2,1)}, u32[]{:S(2)}, u32[]{:S(2)}) collective-permute-start(bf16[2,16,64,128]{3,2,1,0:T(8,128)(2,1)S(1)} %pad_maximum_fusion.refs_0_), channel_id=1, source_target_pairs={{0,32},{16,144},{32,64},{48,176},{64,96},{80,208},{96,0},{112,240}... | collective-permute-start | bytes 1572872 | tf_op jit(solution)/shard_map/ppermute | solution.py:93
  67.9 16.0 %collective-permute-start.9 = (bf16[2,16,64,128]{3,2,1,0:T(8,128)(2,1)S(1)}, bf16[2,16,64,128]{3,2,1,0:T(8,128)(2,1)S(1)}, u32[]{:S(2)}, u32[]{:S(2)}) collective-permute-start(bf16[2,16,64,128]{3,2,1,0:T(8,128)(2,1)S(1)} %pad_maximum_fusion.refs_0_), channel_id=1, source_target_pairs={{0,16},{16,0},{32,48},{48,32},{64,80},{80,64},{96,112},{112,96},{1... | collective-permute-start | bytes 1572872 | tf_op jit(solution)/shard_map/ppermute | solution.py:103
  69.8 16.8 %collective-permute-start.8 = (bf16[2,16,64,128]{3,2,1,0:T(8,128)(2,1)S(1)}, bf16[2,16,64,128]{3,2,1,0:T(8,128)(2,1)}, u32[]{:S(2)}, u32[]{:S(2)}) collective-permute-start(bf16[2,16,64,128]{3,2,1,0:T(8,128)(2,1)S(1)} %pad_maximum_fusion.refs_0_), channel_id=1, source_target_pairs={{0,96},{16,400},{32,0},{48,432},{64,32},{80,464},{96,64},{112,496}... | collective-permute-start | bytes 1572872 | tf_op jit(solution)/shard_map/ppermute | solution.py:93
  73.8 15.3 %collective-permute-start.16 = (bf16[2,16,64,128]{3,2,1,0:T(8,128)(2,1)S(1)}, bf16[2,16,64,128]{3,2,1,0:T(8,128)(2,1)S(1)}, u32[]{:S(2)}, u32[]{:S(2)}) collective-permute-start(bf16[2,16,64,128]{3,2,1,0:T(8,128)(2,1)S(1)} %collective-permute-done.6.refs_7_), channel_id=1, source_target_pairs={{0,16},{16,0},{32,48},{48,32},{64,80},{80,64},{96,112},{112,96},{1... | collective-permute-start | bytes 1572872 | tf_op jit(solution)/shard_map/ppermute | solution.py:103
  76.2 15.5 %collective-permute-start.7 = (bf16[2,16,64,128]{3,2,1,0:T(8,128)(2,1)S(1)}, bf16[2,16,64,128]{3,2,1,0:T(8,128)(2,1)}, u32[]{:S(2)}, u32[]{:S(2)}) collective-permute-start(bf16[2,16,64,128]{3,2,1,0:T(8,128)(2,1)S(1)} %collective-permute-done.6.refs_7_), channel_id=1, source_target_pairs={{0,96},{16,400},{32,0},{48,432},{64,32},{80,464},{96,64},{112,496}... | collective-permute-start | bytes 1572872 | tf_op jit(solution)/shard_map/ppermute | solution.py:93
  80.2 14.0 %collective-permute-start.5 = (bf16[2,16,64,128]{3,2,1,0:T(8,128)(2,1)}, bf16[2,16,64,128]{3,2,1,0:T(8,128)(2,1)}, u32[]{:S(2)}, u32[]{:S(2)}) collective-permute-start(bf16[2,16,64,128]{3,2,1,0:T(8,128)(2,1)} %collective-permute-done.3.refs_2_), channel_id=1, source_target_pairs={{0,32},{16,144},{32,64},{48,176},{64,96},{80,208},{96,0},{112,240}... | collective-permute-start | bytes 1572872 | tf_op jit(solution)/shard_map/ppermute | solution.py:93
  84.7 12.2 %collective-permute-start.11 = (bf16[2,16,64,128]{3,2,1,0:T(8,128)(2,1)}, bf16[2,16,64,128]{3,2,1,0:T(8,128)(2,1)}, u32[]{:S(2)}, u32[]{:S(2)}) collective-permute-start(bf16[2,16,64,128]{3,2,1,0:T(8,128)(2,1)} %collective-permute-done.3.refs_2_), channel_id=1, source_target_pairs={{0,16},{16,0},{32,48},{48,32},{64,80},{80,64},{96,112},{112,96},{1... | collective-permute-start | bytes 1572872 | tf_op jit(solution)/shard_map/ppermute | solution.py:103
  86.6 10.2 %collective-permute-start.12 = (bf16[2,16,64,128]{3,2,1,0:T(8,128)(2,1)}, bf16[2,16,64,128]{3,2,1,0:T(8,128)(2,1)}, u32[]{:S(2)}, u32[]{:S(2)}) collective-permute-start(bf16[2,16,64,128]{3,2,1,0:T(8,128)(2,1)} %collective-permute-done.4.refs_3_), channel_id=1, source_target_pairs={{0,16},{16,0},{32,48},{48,32},{64,80},{80,64},{96,112},{112,96},{1... | collective-permute-start | bytes 1572872 | tf_op jit(solution)/shard_map/ppermute | solution.py:103
  89.8 7.0 %collective-permute-start.15 = (bf16[2,16,64,128]{3,2,1,0:T(8,128)(2,1)}, bf16[2,16,64,128]{3,2,1,0:T(8,128)(2,1)}, u32[]{:S(2)}, u32[]{:S(2)}) collective-permute-start(bf16[2,16,64,128]{3,2,1,0:T(8,128)(2,1)} %collective-permute-done.8.refs_6_), channel_id=1, source_target_pairs={{0,16},{16,0},{32,48},{48,32},{64,80},{80,64},{96,112},{112,96},{1... | collective-permute-start | bytes 1572872 | tf_op jit(solution)/shard_map/ppermute | solution.py:103
  91.8 5.1 %collective-permute-start.14 = (bf16[2,16,64,128]{3,2,1,0:T(8,128)(2,1)}, bf16[2,16,64,128]{3,2,1,0:T(8,128)(2,1)}, u32[]{:S(2)}, u32[]{:S(2)}) collective-permute-start(bf16[2,16,64,128]{3,2,1,0:T(8,128)(2,1)} %collective-permute-done.7.refs_5_), channel_id=1, source_target_pairs={{0,16},{16,0},{32,48},{48,32},{64,80},{80,64},{96,112},{112,96},{1... | collective-permute-start | bytes 1572872 | tf_op jit(solution)/shard_map/ppermute | solution.py:103
  106.1 41.4 %all-to-all-start.1 = ((bf16[16,128,128]{2,1,0:T(8,128)(2,1)}), bf16[16,128,128]{2,1,0:T(8,128)(2,1)}, u32[]{:S(2)}, u32[]{:S(2)}) async-start(bf16[16,128,128]{2,1,0:T(8,128)(2,1)} %copy-done.6), calls=%async_computation.1 | async-start | bytes 1048576 | tf_op jit(solution)/shard_map/all_to_all | solution.py:379
  159.9 35.7 %all-to-all-start.3 = ((bf16[16,128,128]{2,1,0:T(8,128)(2,1)}), bf16[16,128,128]{2,1,0:T(8,128)(2,1)}, u32[]{:S(2)}, u32[]{:S(2)}) async-start(bf16[16,128,128]{2,1,0:T(8,128)(2,1)} %bitcast.18), calls=%async_computation.3 | async-start | bytes 1048576 | tf_op jit(solution)/shard_map/all_to_all | solution.py:379
  169.5 5.5 %collective-permute-start.18 = (f32[1,128]{1,0:T(1,128)S(1)}, f32[1,128]{1,0:T(1,128)S(1)}, u32[]{:S(2)}, u32[]{:S(2)}) collective-permute-start(f32[1,128]{1,0:T(1,128)S(1)} %add.20), channel_id=1, source_target_pairs={{0,32},{16,48},{32,0},{48,16},{64,96},{80,112},{96,64},{112,80},{1... | collective-permute-start | bytes 1544 | tf_op jit(solution)/shard_map/ppermute | solution.py:373
  175.0 7.0 %collective-permute-start.19 = (f32[1,128]{1,0:T(1,128)S(1)}, f32[1,128]{1,0:T(1,128)S(1)}, u32[]{:S(2)}, u32[]{:S(2)}) collective-permute-start(f32[1,128]{1,0:T(1,128)S(1)} %add.21), channel_id=1, source_target_pairs={{0,64},{16,80},{32,96},{48,112},{64,0},{80,16},{96,32},{112,48},{1... | collective-permute-start | bytes 1544 | tf_op jit(solution)/shard_map/ppermute | solution.py:373
  182.0 5.5 %collective-permute-start.20 = (f32[1,128]{1,0:T(1,128)S(1)}, f32[1,128]{1,0:T(1,128)S(1)}, u32[]{:S(2)}, u32[]{:S(2)}) collective-permute-start(f32[1,128]{1,0:T(1,128)S(1)} %add.22), channel_id=1, source_target_pairs={{0,128},{16,144},{32,160},{48,176},{64,192},{80,208},{96,224},{112... | collective-permute-start | bytes 1544 | tf_op jit(solution)/shard_map/ppermute | solution.py:373
  187.4 7.0 %collective-permute-start.21 = (f32[1,128]{1,0:T(1,128)S(1)}, f32[1,128]{1,0:T(1,128)S(1)}, u32[]{:S(2)}, u32[]{:S(2)}) collective-permute-start(f32[1,128]{1,0:T(1,128)S(1)} %add.23), channel_id=1, source_target_pairs={{0,256},{16,272},{32,288},{48,304},{64,320},{80,336},{96,352},{112... | collective-permute-start | bytes 1544 | tf_op jit(solution)/shard_map/ppermute | solution.py:373
  (11 other events, 142.1 us)

commit v5 on v4

--- a/solution.py
+++ b/solution.py
@@ -97,12 +97,12 @@
     down0, up1 = send(own[0], 1, False), send(own[1], -1, False)
     down1, up0 = send(own[1], 1, False), send(own[0], -1, False)
     far0, far1 = send(down0, 1, False), send(up1, -1, False)
+    return own + [down0, down1, far0, far1, up0, up1]
+
+
+def swap_cores(values):
     swap = [(d, d ^ 1) for d in range(2 * SIDE * SIDE)]
-    mine, theirs = [], []
-    for parts in (own, [down0, down1], [far0, far1], [up0, up1]):
-        theirs += [lax.ppermute(v, "dp", swap) for v in parts]
-        mine += parts
-    return mine + theirs
+    return [lax.ppermute(v, "dp", swap) for v in values]
 
 
 def blocks_of():
@@ -137,12 +137,11 @@
         self.core, self.take = core, take
 
     def start(self):
-        count = len(self.refs) // 2
-        blocks = self.held.shape[3]
+        sides, count, _, blocks = self.held.shape[:4]
         for n in range(blocks // self.take):
             span = pl.ds(n * self.take, self.take)
             for a, ref in enumerate(self.refs):
-                side = self.core if a < count else 1 - self.core
+                side = 0 if sides == 1 else self.core if a < count else 1 - self.core
                 pltpu.make_async_copy(
                     ref.at[:, span], self.held.at[side, a % count, :, span], self.sems.at[n]
                 ).start()
@@ -153,59 +152,79 @@
         pltpu.make_async_copy(part, part, self.sems.at[n]).wait()
 
 
-def project(hidden, weights, bias, place):
-    rows, width = hidden.shape
+def project(mine, theirs, weights, place):
+    rows, width = mine.shape
     half, blocks, depth, cols = weights[0].shape
     pair = 2
     count = len(weights)
     chips = width // LANE
 
-    def kernel(place_ref, h_ref, b_ref, *refs):
-        w_refs, o_ref, raw, h, held, ready, sems = refs[:count], *refs[count:]
-        copy = pltpu.make_async_copy(h_ref, raw, ready)
-        copy.start()
-        stream = Stream(w_refs, held, sems, place_ref[chips], TAKE)
+    def kernel(place_ref, m_ref, t_ref, *refs):
+        w_refs, a_ref, z_ref, raw, h, held, ready, sems = refs[:count], *refs[count:]
+        copies = [
+            pltpu.make_async_copy(ref, raw.at[pl.ds(n * rows, rows)], ready.at[n])
+            for n, ref in enumerate((m_ref, t_ref))
+        ]
+        for copy in copies:
+            copy.start()
+        core = place_ref[chips]
+        stream = Stream(w_refs, held, sems, core, TAKE)
         stream.start()
-        copy.wait()
-        for m in range(chips):
-            at = pl.multiple_of(place_ref[m] * LANE, LANE)
-            h[:, m * LANE : (m + 1) * LANE] = raw[:, pl.ds(at, LANE)]
+        for copy in copies:
+            copy.wait()
+
+        def line_up(c):
+            parts = []
+            for b in range(SIDE):
+                for j in range(SIDE):
+                    m = j * SIDE + b if c == 0 else b * SIDE + j
+                    at = pl.multiple_of(place_ref[m] * LANE, LANE)
+                    parts.append(raw[:, pl.ds(at, LANE)][:, c * depth : (c + 1) * depth])
+            for n in range(0, chips, 2):
+                h[:, n * depth : (n + 2) * depth] = jnp.concatenate(parts[n : n + 2], axis=1)
+
+        for c in range(2):
+            pl.when(core == c)(lambda c=c: line_up(c))
         for n in range(blocks // pair):
             if n * pair % TAKE == 0:
                 stream.wait(n * pair // TAKE)
             w = jnp.concatenate(
-                [weight_block(held, n * pair + k) for k in range(pair)], axis=1
+                [
+                    jnp.concatenate(
+                        [held[0, a, i, n * pair + k] for a in range(count) for i in range(half)],
+                        axis=0,
+                    )
+                    for k in range(pair)
+                ],
+                axis=1,
             )
             r = dot(h[...], w, NN)
             for k in range(pair):
-                v = r[:, k * cols : (k + 1) * cols] + b_ref[n * pair + k].astype(F32)
-                o_ref[n * pair + k] = v.astype(BF16)
+                v = r[:, k * cols : (k + 1) * cols]
+                a_ref[n * pair + k] = v[:rows]
+                z_ref[n * pair + k] = v[rows:]
 
     return pl.pallas_call(
         kernel,
-        in_specs=[
-            pl.BlockSpec(memory_space=pltpu.SMEM),
-            pl.BlockSpec(memory_space=pltpu.HBM),
-            pl.BlockSpec(memory_space=pltpu.VMEM),
-        ]
-        + [pl.BlockSpec(memory_space=pl.ANY)] * count,
-        out_specs=pl.BlockSpec(memory_space=pltpu.VMEM),
+        in_specs=[pl.BlockSpec(memory_space=pltpu.SMEM)]
+        + [pl.BlockSpec(memory_space=pl.ANY)] * (2 + count),
+        out_specs=[pl.BlockSpec(memory_space=pltpu.VMEM)] * 2,
         scratch_shapes=[
-            pltpu.VMEM((rows, width), BF16),
-            pltpu.VMEM((rows, width), BF16),
-            pltpu.VMEM((2, count // 2, half, blocks, depth, cols), BF16),
-            pltpu.SemaphoreType.DMA,
+            pltpu.VMEM((2 * rows, width), BF16),
+            pltpu.VMEM((2 * rows, width // 2), BF16),
+            pltpu.VMEM((1, count, half, blocks, depth, cols), BF16),
+            pltpu.SemaphoreType.DMA((2,)),
             pltpu.SemaphoreType.DMA((blocks // TAKE,)),
         ],
-        out_shape=jax.ShapeDtypeStruct((blocks, rows, cols), BF16),
+        out_shape=[jax.ShapeDtypeStruct((blocks, rows, cols), F32)] * 2,
         compiler_params=params(32),
         cost_estimate=pl.CostEstimate(
             flops=2 * rows * width * blocks * cols,
-            bytes_accessed=2 * width * blocks * cols,
+            bytes_accessed=width * blocks * cols,
             transcendentals=0,
         ),
         name="project",
-    )(place, hidden, bias, *weights)
+    )(place, mine, theirs, *weights)
 
 
 def soft(scores, scale, total):
@@ -396,8 +415,12 @@
 
     place = blocks_of()
     rows = student_hidden.reshape(seqs * toks, width)
-    values = project(rows, weights, bias, place)
+    other_rows = swap_cores([rows])[0]
+    kept, sent = project(rows, other_rows, weights, place)
+    got = swap_cores([sent])[0]
+    values = (kept + got + bias.astype(F32)).astype(BF16)
     values = exchange(values)
+    weights = weights + swap_cores(weights)
     grads, total = head_grads(values, probs)
     grads = exchange(grads)
     hidden_grad = hidden_grads(grads, weights, place).reshape(student_hidden.shape)

time: 204 us -> 224 us (1.098)
  the two profiles are of different devices: /device:TPU:24 before, /device:TPU:1 now
where the time goes in v5:
time: 224 us; the launch traced here: 221 us
  starting transfers between devices  122 us (54%)
  Pallas kernels  44.5 us (20%)
  waiting for transfers between devices  36.6 us (16%)
  local copies, waits for them, and re-layouts  15.5 us (7%)
    all_to_all x4, starting transfers between devices, exchange(): return lax.all_to_all(x, 'tok', split_axis=0, concat_axis=0, tiled=True)  51.6 us
    ppermute x10, starting transfers between devices, swap_cores(): return [lax.ppermute(v, 'dp', swap) for v in values]  29.5 us
    ppermute x9, starting transfers between devices, send(): return lax.ppermute(v, 'dp', ring_pairs(shift, first))  28.8 us
    all_to_all x4, waiting for transfers between devices, exchange(): return lax.all_to_all(x, 'tok', split_axis=0, concat_axis=0, tiled=True)  15 us
    unnamed x36, local copies, waits for them, and re-layouts  14.7 us
    pallas_call x1, Pallas kernels, teacher_probs(): pl.pallas_call(kernel, grid=(seqs, heads, length // step), in_specs=[pl.B...  13.1 us
    ppermute x5, starting transfers between devices, sum_over(): x = x + lax.ppermute(x, axis, [(i, i ^ reach) for i in range(size)])  12.3 us
    pallas_call x1, Pallas kernels, head_grads(): pl.pallas_call(kernel, grid=(seqs, length // step), in_specs=[pl.BlockSpe...  11.6 us
  transfers between devices with their start and end apart: 28, of which 11 were waited for; matrix products, arithmetic and copies ran while one was open for 1% of the time, Pallas kernels for 11%

profile of v5, /device:TPU:1, one launch (start us, length us, event | category | flops | bytes accessed | tf_op | source)
XLA Modules:
  0.0 221.4 jit_solution(449252082173746598)
XLA Ops:
  2.8 15.7 %all-to-all-start = ((bf16[16,72,128]{2,1,0:T(8,128)(2,1)}), bf16[16,72,128]{2,1,0:T(8,128)(2,1)S(1)}, u32[]{:S(2)}, u32[]{:S(2)}) async-start(bf16[16,72,128]{2,1,0:T(8,128)(2,1)} %copies_of_piece.1), calls=%async_computation | async-start | bytes 589824 | tf_op jit(solution)/shard_map/all_to_all | solution.py:398
  18.5 8.8 %split_columns.1 = bf16[16,128,256]{2,1,0:T(8,128)(2,1)} custom-call(bf16[128,4096]{1,0:T(8,128)(2,1)} %bitcast.22), custom_call_target="tpu_custom_call" | custom-call | tf_op jit(solution)/shard_map/split_columns/pallas_call | solution.py:36
  27.4 5.3 %all-to-all-done = bf16[16,72,128]{2,1,0:T(8,128)(2,1)S(1)} async-done(((bf16[16,72,128]{2,1,0:T(8,128)(2,1)}), bf16[16,72,128]{2,1,0:T(8,128)(2,1)S(1)}, u32[]{:S(2)}, u32[]{:S(2)}) %all-to-all-start) | async-done | bytes 294944 | tf_op jit(solution)/shard_map/all_to_all | solution.py:398
  32.7 11.3 %all-to-all-start.2 = ((bf16[16,128,256]{2,1,0:T(8,128)(2,1)}), bf16[16,128,256]{2,1,0:T(8,128)(2,1)S(1)}, u32[]{:S(2)}, u32[]{:S(2)}) async-start(bf16[16,128,256]{2,1,0:T(8,128)(2,1)} %split_columns.1), calls=%async_computation.2 | async-start | bytes 2097152 | tf_op jit(solution)/shard_map/all_to_all | solution.py:398
  44.1 4.8 %collective-permute-start.2 = (bf16[16,64,128]{2,1,0:T(8,128)(2,1)S(1)}, bf16[16,64,128]{2,1,0:T(8,128)(2,1)S(1)}, u32[]{:S(2)}, u32[]{:S(2)}) collective-permute-start(bf16[16,64,128]{2,1,0:T(8,128)(2,1)S(1)} %get-tuple-element.11), channel_id=1, source_target_pairs={{0,256},{16,80},{32,288},{48,112},{64,320},{80,16},{96,352},{112,4... | collective-permute-start | bytes 786440 | tf_op jit(solution)/shard_map/ppermute | solution.py:93
  48.9 2.7 %collective-permute-start.3 = (bf16[16,64,128]{2,1,0:T(8,128)(2,1)S(1)}, bf16[16,64,128]{2,1,0:T(8,128)(2,1)S(1)}, u32[]{:S(2)}, u32[]{:S(2)}) collective-permute-start(bf16[16,64,128]{2,1,0:T(8,128)(2,1)S(1)} %get-tuple-element.11), channel_id=1, source_target_pairs={{0,384},{16,112},{32,416},{48,16},{64,448},{80,48},{96,480},{112,8... | collective-permute-start | bytes 786440 | tf_op jit(solution)/shard_map/ppermute | solution.py:93
  56.4 4.4 %collective-permute-start.7 = (bf16[2,16,64,128]{3,2,1,0:T(8,128)(2,1)S(1)}, bf16[2,16,64,128]{3,2,1,0:T(8,128)(2,1)S(1)}, u32[]{:S(2)}, u32[]{:S(2)}) collective-permute-start(bf16[2,16,64,128]{3,2,1,0:T(8,128)(2,1)S(1)} %pad_maximum_fusion.1.refs_1_), channel_id=1, source_target_pairs={{0,96},{16,400},{32,0},{48,432},{64,32},{80,464},{96,64},{112,496}... | collective-permute-start | bytes 1572872 | tf_op jit(solution)/shard_map/ppermute | solution.py:93
  63.4 4.7 %collective-permute-start = (bf16[128,2048]{1,0:T(8,128)(2,1)}, bf16[128,2048]{1,0:T(8,128)(2,1)}, u32[]{:S(2)}, u32[]{:S(2)}) collective-permute-start(bf16[128,2048]{1,0:T(8,128)(2,1)} %bitcast.20), channel_id=1, source_target_pairs={{0,16},{16,0},{32,48},{48,32},{64,80},{80,64},{96,112},{112,96},{1... | collective-permute-start | bytes 1572872 | tf_op jit(solution)/shard_map/ppermute | solution.py:105
  70.0 4.6 %collective-permute-start.9 = (bf16[2,16,64,128]{3,2,1,0:T(8,128)(2,1)S(1)}, bf16[2,16,64,128]{3,2,1,0:T(8,128)(2,1)}, u32[]{:S(2)}, u32[]{:S(2)}) collective-permute-start(bf16[2,16,64,128]{3,2,1,0:T(8,128)(2,1)S(1)} %pad_maximum_fusion.refs_0_), channel_id=1, source_target_pairs={{0,96},{16,400},{32,0},{48,432},{64,32},{80,464},{96,64},{112,496}... | collective-permute-start | bytes 1572872 | tf_op jit(solution)/shard_map/ppermute | solution.py:93
  76.6 3.3 %collective-permute-start.6 = (bf16[2,16,64,128]{3,2,1,0:T(8,128)(2,1)S(1)}, bf16[2,16,64,128]{3,2,1,0:T(8,128)(2,1)}, u32[]{:S(2)}, u32[]{:S(2)}) collective-permute-start(bf16[2,16,64,128]{3,2,1,0:T(8,128)(2,1)S(1)} %collective-permute-done.4.refs_2_), channel_id=1, source_target_pairs={{0,32},{16,144},{32,64},{48,176},{64,96},{80,208},{96,0},{112,240}... | collective-permute-start | bytes 1572872 | tf_op jit(solution)/shard_map/ppermute | solution.py:93
  80.7 5.6 %collective-permute-done.8.refs_5_ = bf16[2,16,64,128]{3,2,1,0:T(8,128)(2,1)} collective-permute-done((bf16[2,16,64,128]{3,2,1,0:T(8,128)(2,1)S(1)}, bf16[2,16,64,128]{3,2,1,0:T(8,128)(2,1)}, u32[]{:S(2)}, u32[]{:S(2)}) %collective-permute-start.8) | collective-permute-done | bytes 524320 | tf_op jit(solution)/shard_map/ppermute | solution.py:93
  89.2 3.4 %project.1 = (f32[16,128,128]{2,1,0:T(8,128)S(1)}, f32[16,128,128]{2,1,0:T(8,128)S(1)}) custom-call(s32[17]{0:T(128)S(1)} %dynamic-slice_bitcast_fusion.place_ref, bf16[128,2048]{1,0:T(8,128)(2,1)S(1)} %bitcast.21, bf16[128,2048]{1,0:T(8,128)(2,1)} %collective-permute-done.t_ref, bf16[2,16,64,128]{3,2,1,0:T(8,128)(2,1)S(1)} %pad_maximum_fusion.refs_0_, ...), custom_call_target="tpu_custom_call" | custom-call | flops 1073741824 | bytes 4194304 | tf_op jit(solution)/shard_map/project/pallas_call | solution.py:207
  92.6 4.5 %collective-permute-start.10 = (f32[16,128,128]{2,1,0:T(8,128)S(1)}, f32[16,128,128]{2,1,0:T(8,128)S(1)}, u32[]{:S(2)}, u32[]{:S(2)}) collective-permute-start(f32[16,128,128]{2,1,0:T(8,128)S(1)} %get-tuple-element.7), channel_id=1, source_target_pairs={{0,16},{16,0},{32,48},{48,32},{64,80},{80,64},{96,112},{112,96},{1... | collective-permute-start | bytes 3145736 | tf_op jit(solution)/shard_map/ppermute | solution.py:105
  100.3 11.7 %all-to-all-start.1 = ((bf16[16,128,128]{2,1,0:T(8,128)(2,1)}), bf16[16,128,128]{2,1,0:T(8,128)(2,1)S(1)}, u32[]{:S(2)}, u32[]{:S(2)}) async-start(bf16[16,128,128]{2,1,0:T(8,128)(2,1)} %add_convert_fusion), calls=%async_computation.1 | async-start | bytes 1048576 | tf_op jit(solution)/shard_map/all_to_all | solution.py:398
  112.1 13.1 %teacher_probs.1.p_ref = f32[2,2,1024,1024]{3,2,1,0:T(8,128)} custom-call(bf16[16,2,64,256]{3,2,1,0:T(8,128)(2,1)S(1)} %bitcast.17), custom_call_target="tpu_custom_call" | custom-call | flops 1073741824 | bytes 16777216 | tf_op jit(solution)/shard_map/teacher_probs/pallas_call | solution.py:251
  125.2 9.6 %all-to-all-done.1 = bf16[16,128,128]{2,1,0:T(8,128)(2,1)S(1)} async-done(((bf16[16,128,128]{2,1,0:T(8,128)(2,1)}), bf16[16,128,128]{2,1,0:T(8,128)(2,1)S(1)}, u32[]{:S(2)}, u32[]{:S(2)}) %all-to-all-start.1) | async-done | bytes 524320 | tf_op jit(solution)/shard_map/all_to_all | solution.py:398
  134.8 11.6 %head_grads.1 = (bf16[16,2,64,128]{3,2,1,0:T(8,128)(2,1)S(1)}, f32[1,128]{1,0:T(1,128)S(1)}) custom-call(bf16[16,2,64,128]{3,2,1,0:T(8,128)(2,1)S(1)} %bitcast.18, f32[2,2,1024,1024]{3,2,1,0:T(8,128)} %teacher_probs.1.p_ref), custom_call_target="tpu_custom_call" | custom-call | flops 3221225472 | bytes 16777216 | tf_op jit(solution)/shard_map/head_grads/pallas_call | solution.py:309
  147.2 12.8 %all-to-all-start.3 = ((bf16[16,128,128]{2,1,0:T(8,128)(2,1)}), bf16[16,128,128]{2,1,0:T(8,128)(2,1)S(1)}, u32[]{:S(2)}, u32[]{:S(2)}) async-start(bf16[16,128,128]{2,1,0:T(8,128)(2,1)} %bitcast.19), calls=%async_computation.3 | async-start | bytes 1048576 | tf_op jit(solution)/shard_map/all_to_all | solution.py:398
  160.0 2.7 %collective-permute-start.12 = (bf16[2,16,64,128]{3,2,1,0:T(8,128)(2,1)S(1)}, bf16[2,16,64,128]{3,2,1,0:T(8,128)(2,1)S(1)}, u32[]{:S(2)}, u32[]{:S(2)}) collective-permute-start(bf16[2,16,64,128]{3,2,1,0:T(8,128)(2,1)S(1)} %pad_maximum_fusion.1.refs_1_), channel_id=1, source_target_pairs={{0,16},{16,0},{32,48},{48,32},{64,80},{80,64},{96,112},{112,96},{1... | collective-permute-start | bytes 1572872 | tf_op jit(solution)/shard_map/ppermute | solution.py:105
  172.0 2.7 %collective-permute-done.20 = f32[1,128]{1,0:T(1,128)S(1)} collective-permute-done((f32[1,128]{1,0:T(1,128)S(1)}, f32[1,128]{1,0:T(1,128)S(1)}, u32[]{:S(2)}, u32[]{:S(2)}) %collective-permute-start.20) | collective-permute-done | bytes 544 | tf_op jit(solution)/shard_map/ppermute | solution.py:392
  177.0 3.8 %collective-permute-done.21 = f32[1,128]{1,0:T(1,128)S(1)} collective-permute-done((f32[1,128]{1,0:T(1,128)S(1)}, f32[1,128]{1,0:T(1,128)S(1)}, u32[]{:S(2)}, u32[]{:S(2)}) %collective-permute-start.21) | collective-permute-done | bytes 544 | tf_op jit(solution)/shard_map/ppermute | solution.py:392
  185.4 3.7 %collective-permute-start.23 = (f32[1,128]{1,0:T(1,128)S(1)}, f32[1,128]{1,0:T(1,128)S(1)}, u32[]{:S(2)}, u32[]{:S(2)}) collective-permute-start(f32[1,128]{1,0:T(1,128)S(1)} %add.44), channel_id=1, source_target_pairs={{0,256},{16,272},{32,288},{48,304},{64,320},{80,336},{96,352},{112... | collective-permute-start | bytes 1544 | tf_op jit(solution)/shard_map/ppermute | solution.py:392
  189.1 4.6 %collective-permute-start.14 = (bf16[2,16,64,128]{3,2,1,0:T(8,128)(2,1)}, bf16[2,16,64,128]{3,2,1,0:T(8,128)(2,1)S(1)}, u32[]{:S(2)}, u32[]{:S(2)}) collective-permute-start(bf16[2,16,64,128]{3,2,1,0:T(8,128)(2,1)} %collective-permute-done.5.refs_3_), channel_id=1, source_target_pairs={{0,16},{16,0},{32,48},{48,32},{64,80},{80,64},{96,112},{112,96},{1... | collective-permute-start | bytes 1572872 | tf_op jit(solution)/shard_map/ppermute | solution.py:105
  215.9 5.5 %hidden_grads.1 = bf16[128,2048]{1,0:T(8,128)(2,1)} custom-call(s32[17]{0:T(128)S(1)} %dynamic-slice_bitcast_fusion.place_ref, bf16[16,128,128]{2,1,0:T(8,128)(2,1)S(1)} %all-to-all-done.3.g_ref, bf16[2,16,64,128]{3,2,1,0:T(8,128)(2,1)S(1)} %pad_maximum_fusion.refs_0_, bf16[2,16,64,128]{3,2,1,0:T(8,128)(2,1)S(1)} %pad_maximum_fusion.1.refs_1_, ...), custom_call_target="tpu_custom_call" | custom-call | flops 1073741824 | bytes 8388608 | tf_op jit(solution)/shard_map/hidden_grads/pallas_call | solution.py:364
  (85 shorter events, 59.3 us)
Async XLA Ops:
  2.8 29.9 %all-to-all-start = ((bf16[16,72,128]{2,1,0:T(8,128)(2,1)}), bf16[16,72,128]{2,1,0:T(8,128)(2,1)S(1)}, u32[]{:S(2)}, u32[]{:S(2)}) async-start(bf16[16,72,128]{2,1,0:T(8,128)(2,1)} %copies_of_piece.1), calls=%async_computation | async-start | bytes 589824 | tf_op jit(solution)/shard_map/all_to_all | solution.py:398
  32.7 67.6 %all-to-all-start.2 = ((bf16[16,128,256]{2,1,0:T(8,128)(2,1)}), bf16[16,128,256]{2,1,0:T(8,128)(2,1)S(1)}, u32[]{:S(2)}, u32[]{:S(2)}) async-start(bf16[16,128,256]{2,1,0:T(8,128)(2,1)} %split_columns.1), calls=%async_computation.2 | async-start | bytes 2097152 | tf_op jit(solution)/shard_map/all_to_all | solution.py:398
  44.1 10.1 %collective-permute-start.2 = (bf16[16,64,128]{2,1,0:T(8,128)(2,1)S(1)}, bf16[16,64,128]{2,1,0:T(8,128)(2,1)S(1)}, u32[]{:S(2)}, u32[]{:S(2)}) collective-permute-start(bf16[16,64,128]{2,1,0:T(8,128)(2,1)S(1)} %get-tuple-element.11), channel_id=1, source_target_pairs={{0,256},{16,80},{32,288},{48,112},{64,320},{80,16},{96,352},{112,4... | collective-permute-start | bytes 786440 | tf_op jit(solution)/shard_map/ppermute | solution.py:93
  48.9 7.4 %collective-permute-start.3 = (bf16[16,64,128]{2,1,0:T(8,128)(2,1)S(1)}, bf16[16,64,128]{2,1,0:T(8,128)(2,1)S(1)}, u32[]{:S(2)}, u32[]{:S(2)}) collective-permute-start(bf16[16,64,128]{2,1,0:T(8,128)(2,1)S(1)} %get-tuple-element.11), channel_id=1, source_target_pairs={{0,384},{16,112},{32,416},{48,16},{64,448},{80,48},{96,480},{112,8... | collective-permute-start | bytes 786440 | tf_op jit(solution)/shard_map/ppermute | solution.py:93
  51.6 9.2 %collective-permute-start.1 = (bf16[16,64,128]{2,1,0:T(8,128)(2,1)S(1)}, bf16[16,64,128]{2,1,0:T(8,128)(2,1)S(1)}, u32[]{:S(2)}, u32[]{:S(2)}) collective-permute-start(bf16[16,64,128]{2,1,0:T(8,128)(2,1)S(1)} %get-tuple-element.11), channel_id=1, source_target_pairs={{0,128},{16,48},{32,160},{48,80},{64,192},{80,112},{96,224},{112,1... | collective-permute-start | bytes 786440 | tf_op jit(solution)/shard_map/ppermute | solution.py:93
  56.4 18.2 %collective-permute-start.7 = (bf16[2,16,64,128]{3,2,1,0:T(8,128)(2,1)S(1)}, bf16[2,16,64,128]{3,2,1,0:T(8,128)(2,1)S(1)}, u32[]{:S(2)}, u32[]{:S(2)}) collective-permute-start(bf16[2,16,64,128]{3,2,1,0:T(8,128)(2,1)S(1)} %pad_maximum_fusion.1.refs_1_), channel_id=1, source_target_pairs={{0,96},{16,400},{32,0},{48,432},{64,32},{80,464},{96,64},{112,496}... | collective-permute-start | bytes 1572872 | tf_op jit(solution)/shard_map/ppermute | solution.py:93
  60.9 15.7 %collective-permute-start.4 = (bf16[2,16,64,128]{3,2,1,0:T(8,128)(2,1)S(1)}, bf16[2,16,64,128]{3,2,1,0:T(8,128)(2,1)S(1)}, u32[]{:S(2)}, u32[]{:S(2)}) collective-permute-start(bf16[2,16,64,128]{3,2,1,0:T(8,128)(2,1)S(1)} %pad_maximum_fusion.refs_0_), channel_id=1, source_target_pairs={{0,32},{16,144},{32,64},{48,176},{64,96},{80,208},{96,0},{112,240}... | collective-permute-start | bytes 1572872 | tf_op jit(solution)/shard_map/ppermute | solution.py:93
  63.4 17.2 %collective-permute-start = (bf16[128,2048]{1,0:T(8,128)(2,1)}, bf16[128,2048]{1,0:T(8,128)(2,1)}, u32[]{:S(2)}, u32[]{:S(2)}) collective-permute-start(bf16[128,2048]{1,0:T(8,128)(2,1)} %bitcast.20), channel_id=1, source_target_pairs={{0,16},{16,0},{32,48},{48,32},{64,80},{80,64},{96,112},{112,96},{1... | collective-permute-start | bytes 1572872 | tf_op jit(solution)/shard_map/ppermute | solution.py:105
  68.1 12.5 %collective-permute-start.5 = (bf16[2,16,64,128]{3,2,1,0:T(8,128)(2,1)S(1)}, bf16[2,16,64,128]{3,2,1,0:T(8,128)(2,1)}, u32[]{:S(2)}, u32[]{:S(2)}) collective-permute-start(bf16[2,16,64,128]{3,2,1,0:T(8,128)(2,1)S(1)} %pad_maximum_fusion.1.refs_1_), channel_id=1, source_target_pairs={{0,32},{16,144},{32,64},{48,176},{64,96},{80,208},{96,0},{112,240}... | collective-permute-start | bytes 1572872 | tf_op jit(solution)/shard_map/ppermute | solution.py:93
  70.0 10.7 %collective-permute-start.9 = (bf16[2,16,64,128]{3,2,1,0:T(8,128)(2,1)S(1)}, bf16[2,16,64,128]{3,2,1,0:T(8,128)(2,1)}, u32[]{:S(2)}, u32[]{:S(2)}) collective-permute-start(bf16[2,16,64,128]{3,2,1,0:T(8,128)(2,1)S(1)} %pad_maximum_fusion.refs_0_), channel_id=1, source_target_pairs={{0,96},{16,400},{32,0},{48,432},{64,32},{80,464},{96,64},{112,496}... | collective-permute-start | bytes 1572872 | tf_op jit(solution)/shard_map/ppermute | solution.py:93
  74.6 11.7 %collective-permute-start.8 = (bf16[2,16,64,128]{3,2,1,0:T(8,128)(2,1)S(1)}, bf16[2,16,64,128]{3,2,1,0:T(8,128)(2,1)}, u32[]{:S(2)}, u32[]{:S(2)}) collective-permute-start(bf16[2,16,64,128]{3,2,1,0:T(8,128)(2,1)S(1)} %collective-permute-done.7.refs_7_), channel_id=1, source_target_pairs={{0,96},{16,400},{32,0},{48,432},{64,32},{80,464},{96,64},{112,496}... | collective-permute-start | bytes 1572872 | tf_op jit(solution)/shard_map/ppermute | solution.py:93
  76.6 11.5 %collective-permute-start.6 = (bf16[2,16,64,128]{3,2,1,0:T(8,128)(2,1)S(1)}, bf16[2,16,64,128]{3,2,1,0:T(8,128)(2,1)}, u32[]{:S(2)}, u32[]{:S(2)}) collective-permute-start(bf16[2,16,64,128]{3,2,1,0:T(8,128)(2,1)S(1)} %collective-permute-done.4.refs_2_), channel_id=1, source_target_pairs={{0,32},{16,144},{32,64},{48,176},{64,96},{80,208},{96,0},{112,240}... | collective-permute-start | bytes 1572872 | tf_op jit(solution)/shard_map/ppermute | solution.py:93
  92.6 6.8 %collective-permute-start.10 = (f32[16,128,128]{2,1,0:T(8,128)S(1)}, f32[16,128,128]{2,1,0:T(8,128)S(1)}, u32[]{:S(2)}, u32[]{:S(2)}) collective-permute-start(f32[16,128,128]{2,1,0:T(8,128)S(1)} %get-tuple-element.7), channel_id=1, source_target_pairs={{0,16},{16,0},{32,48},{48,32},{64,80},{80,64},{96,112},{112,96},{1... | collective-permute-start | bytes 3145736 | tf_op jit(solution)/shard_map/ppermute | solution.py:105
  100.3 34.5 %all-to-all-start.1 = ((bf16[16,128,128]{2,1,0:T(8,128)(2,1)}), bf16[16,128,128]{2,1,0:T(8,128)(2,1)S(1)}, u32[]{:S(2)}, u32[]{:S(2)}) async-start(bf16[16,128,128]{2,1,0:T(8,128)(2,1)} %add_convert_fusion), calls=%async_computation.1 | async-start | bytes 1048576 | tf_op jit(solution)/shard_map/all_to_all | solution.py:398
  147.2 61.4 %all-to-all-start.3 = ((bf16[16,128,128]{2,1,0:T(8,128)(2,1)}), bf16[16,128,128]{2,1,0:T(8,128)(2,1)S(1)}, u32[]{:S(2)}, u32[]{:S(2)}) async-start(bf16[16,128,128]{2,1,0:T(8,128)(2,1)} %bitcast.19), calls=%async_computation.3 | async-start | bytes 1048576 | tf_op jit(solution)/shard_map/all_to_all | solution.py:398
  160.0 33.8 %collective-permute-start.12 = (bf16[2,16,64,128]{3,2,1,0:T(8,128)(2,1)S(1)}, bf16[2,16,64,128]{3,2,1,0:T(8,128)(2,1)S(1)}, u32[]{:S(2)}, u32[]{:S(2)}) collective-permute-start(bf16[2,16,64,128]{3,2,1,0:T(8,128)(2,1)S(1)} %pad_maximum_fusion.1.refs_1_), channel_id=1, source_target_pairs={{0,16},{16,0},{32,48},{48,32},{64,80},{80,64},{96,112},{112,96},{1... | collective-permute-start | bytes 1572872 | tf_op jit(solution)/shard_map/ppermute | solution.py:105
  162.7 33.0 %collective-permute-start.11 = (bf16[2,16,64,128]{3,2,1,0:T(8,128)(2,1)S(1)}, bf16[2,16,64,128]{3,2,1,0:T(8,128)(2,1)S(1)}, u32[]{:S(2)}, u32[]{:S(2)}) collective-permute-start(bf16[2,16,64,128]{3,2,1,0:T(8,128)(2,1)S(1)} %pad_maximum_fusion.refs_0_), channel_id=1, source_target_pairs={{0,16},{16,0},{32,48},{48,32},{64,80},{80,64},{96,112},{112,96},{1... | collective-permute-start | bytes 1572872 | tf_op jit(solution)/shard_map/ppermute | solution.py:105
  164.6 34.3 %collective-permute-start.18 = (bf16[2,16,64,128]{3,2,1,0:T(8,128)(2,1)S(1)}, bf16[2,16,64,128]{3,2,1,0:T(8,128)(2,1)S(1)}, u32[]{:S(2)}, u32[]{:S(2)}) collective-permute-start(bf16[2,16,64,128]{3,2,1,0:T(8,128)(2,1)S(1)} %collective-permute-done.7.refs_7_), channel_id=1, source_target_pairs={{0,16},{16,0},{32,48},{48,32},{64,80},{80,64},{96,112},{112,96},{1... | collective-permute-start | bytes 1572872 | tf_op jit(solution)/shard_map/ppermute | solution.py:105
  185.4 16.2 %collective-permute-start.23 = (f32[1,128]{1,0:T(1,128)S(1)}, f32[1,128]{1,0:T(1,128)S(1)}, u32[]{:S(2)}, u32[]{:S(2)}) collective-permute-start(f32[1,128]{1,0:T(1,128)S(1)} %add.44), channel_id=1, source_target_pairs={{0,256},{16,272},{32,288},{48,304},{64,320},{80,336},{96,352},{112... | collective-permute-start | bytes 1544 | tf_op jit(solution)/shard_map/ppermute | solution.py:392
  189.1 15.5 %collective-permute-start.14 = (bf16[2,16,64,128]{3,2,1,0:T(8,128)(2,1)}, bf16[2,16,64,128]{3,2,1,0:T(8,128)(2,1)S(1)}, u32[]{:S(2)}, u32[]{:S(2)}) collective-permute-start(bf16[2,16,64,128]{3,2,1,0:T(8,128)(2,1)} %collective-permute-done.5.refs_3_), channel_id=1, source_target_pairs={{0,16},{16,0},{32,48},{48,32},{64,80},{80,64},{96,112},{112,96},{1... | collective-permute-start | bytes 1572872 | tf_op jit(solution)/shard_map/ppermute | solution.py:105
  193.8 11.6 %collective-permute-start.13 = (bf16[2,16,64,128]{3,2,1,0:T(8,128)(2,1)S(1)}, bf16[2,16,64,128]{3,2,1,0:T(8,128)(2,1)S(1)}, u32[]{:S(2)}, u32[]{:S(2)}) collective-permute-start(bf16[2,16,64,128]{3,2,1,0:T(8,128)(2,1)S(1)} %copy-done.1), channel_id=1, source_target_pairs={{0,16},{16,0},{32,48},{48,32},{64,80},{80,64},{96,112},{112,96},{1... | collective-permute-start | bytes 1572872 | tf_op jit(solution)/shard_map/ppermute | solution.py:105
  196.5 9.7 %collective-permute-start.17 = (bf16[2,16,64,128]{3,2,1,0:T(8,128)(2,1)}, bf16[2,16,64,128]{3,2,1,0:T(8,128)(2,1)S(1)}, u32[]{:S(2)}, u32[]{:S(2)}) collective-permute-start(bf16[2,16,64,128]{3,2,1,0:T(8,128)(2,1)} %collective-permute-done.9.refs_6_), channel_id=1, source_target_pairs={{0,16},{16,0},{32,48},{48,32},{64,80},{80,64},{96,112},{112,96},{1... | collective-permute-start | bytes 1572872 | tf_op jit(solution)/shard_map/ppermute | solution.py:105
  199.7 7.3 %collective-permute-start.16 = (bf16[2,16,64,128]{3,2,1,0:T(8,128)(2,1)}, bf16[2,16,64,128]{3,2,1,0:T(8,128)(2,1)S(1)}, u32[]{:S(2)}, u32[]{:S(2)}) collective-permute-start(bf16[2,16,64,128]{3,2,1,0:T(8,128)(2,1)} %collective-permute-done.8.refs_5_), channel_id=1, source_target_pairs={{0,16},{16,0},{32,48},{48,32},{64,80},{80,64},{96,112},{112,96},{1... | collective-permute-start | bytes 1572872 | tf_op jit(solution)/shard_map/ppermute | solution.py:105
  201.6 6.2 %collective-permute-start.15 = (bf16[2,16,64,128]{3,2,1,0:T(8,128)(2,1)}, bf16[2,16,64,128]{3,2,1,0:T(8,128)(2,1)S(1)}, u32[]{:S(2)}, u32[]{:S(2)}) collective-permute-start(bf16[2,16,64,128]{3,2,1,0:T(8,128)(2,1)} %collective-permute-done.6.refs_4_), channel_id=1, source_target_pairs={{0,16},{16,0},{32,48},{48,32},{64,80},{80,64},{96,112},{112,96},{1... | collective-permute-start | bytes 1572872 | tf_op jit(solution)/shard_map/ppermute | solution.py:105
  (22 other events, 125.4 us)

commit v6 on v5

--- a/solution.py
+++ b/solution.py
@@ -73,6 +73,7 @@
 SIDE = 4
 LANE = 128
 TAKE = 8
+EARLY = 3
 
 
 def ring_pairs(shift, first):
@@ -322,7 +323,7 @@
             jax.ShapeDtypeStruct((1, cols), F32),
         ],
         scratch_shapes=[pltpu.VMEM((length, cols), F32), pltpu.VMEM((cols, length), F32)],
-        compiler_params=params(48),
+        compiler_params=params(58),
         cost_estimate=pl.CostEstimate(
             flops=6 * seqs * heads * length * length * cols,
             bytes_accessed=4 * seqs * heads * length * length,
@@ -416,11 +417,12 @@
     place = blocks_of()
     rows = student_hidden.reshape(seqs * toks, width)
     other_rows = swap_cores([rows])[0]
+    swapped = swap_cores(weights[:EARLY])
     kept, sent = project(rows, other_rows, weights, place)
     got = swap_cores([sent])[0]
     values = (kept + got + bias.astype(F32)).astype(BF16)
     values = exchange(values)
-    weights = weights + swap_cores(weights)
+    weights = weights + swapped + swap_cores(weights[EARLY:])
     grads, total = head_grads(values, probs)
     grads = exchange(grads)
     hidden_grad = hidden_grads(grads, weights, place).reshape(student_hidden.shape)

time: 224 us -> 225 us (level)
    unnamed x36 -> x30, local copies, waits for them, and re-layouts: 14.7 us -> 14 us
where the time goes in v6:
time: 225 us; the launch traced here: 222 us
  starting transfers between devices  122 us (54%)
  Pallas kernels  45.3 us (20%)
  waiting for transfers between devices  36.9 us (16%)
  local copies, waits for them, and re-layouts  14.8 us (7%)
  other arithmetic  2.27 us (1%)
    all_to_all x4, starting transfers between devices, exchange(): return lax.all_to_all(x, 'tok', split_axis=0, concat_axis=0, tiled=True)  51.6 us
    ppermute x10, starting transfers between devices, swap_cores(): return [lax.ppermute(v, 'dp', swap) for v in values]  29.4 us
    ppermute x9, starting transfers between devices, send(): return lax.ppermute(v, 'dp', ring_pairs(shift, first))  28.8 us
    all_to_all x4, waiting for transfers between devices, exchange(): return lax.all_to_all(x, 'tok', split_axis=0, concat_axis=0, tiled=True)  15.1 us
    unnamed x30, local copies, waits for them, and re-layouts  14 us
    pallas_call x1, Pallas kernels, teacher_probs(): pl.pallas_call(kernel, grid=(seqs, heads, length // step), in_specs=[pl.B...  13.1 us
    pallas_call x1, Pallas kernels, head_grads(): pl.pallas_call(kernel, grid=(seqs, length // step), in_specs=[pl.BlockSpe...  12.4 us
    ppermute x5, starting transfers between devices, sum_over(): x = x + lax.ppermute(x, axis, [(i, i ^ reach) for i in range(size)])  12.3 us
  transfers between devices with their start and end apart: 28, of which 11 were waited for; matrix products, arithmetic and copies ran while one was open for 1% of the time, Pallas kernels for 11%

profile of v6, /device:TPU:1, one launch (start us, length us, event | category | flops | bytes accessed | tf_op | source)
XLA Modules:
  0.0 222.4 jit_solution(17620041819776130729)
XLA Ops:
  2.8 15.7 %all-to-all-start = ((bf16[16,72,128]{2,1,0:T(8,128)(2,1)}), bf16[16,72,128]{2,1,0:T(8,128)(2,1)S(1)}, u32[]{:S(2)}, u32[]{:S(2)}) async-start(bf16[16,72,128]{2,1,0:T(8,128)(2,1)} %copies_of_piece.1), calls=%async_computation | async-start | bytes 589824 | tf_op jit(solution)/shard_map/all_to_all | solution.py:399
  18.5 8.8 %split_columns.1 = bf16[16,128,256]{2,1,0:T(8,128)(2,1)} custom-call(bf16[128,4096]{1,0:T(8,128)(2,1)} %bitcast.20), custom_call_target="tpu_custom_call" | custom-call | tf_op jit(solution)/shard_map/split_columns/pallas_call | solution.py:36
  27.3 5.4 %all-to-all-done = bf16[16,72,128]{2,1,0:T(8,128)(2,1)S(1)} async-done(((bf16[16,72,128]{2,1,0:T(8,128)(2,1)}), bf16[16,72,128]{2,1,0:T(8,128)(2,1)S(1)}, u32[]{:S(2)}, u32[]{:S(2)}) %all-to-all-start) | async-done | bytes 294944 | tf_op jit(solution)/shard_map/all_to_all | solution.py:399
  32.7 11.3 %all-to-all-start.2 = ((bf16[16,128,256]{2,1,0:T(8,128)(2,1)}), bf16[16,128,256]{2,1,0:T(8,128)(2,1)S(1)}, u32[]{:S(2)}, u32[]{:S(2)}) async-start(bf16[16,128,256]{2,1,0:T(8,128)(2,1)} %split_columns.1), calls=%async_computation.2 | async-start | bytes 2097152 | tf_op jit(solution)/shard_map/all_to_all | solution.py:399
  44.1 4.8 %collective-permute-start.2 = (bf16[16,64,128]{2,1,0:T(8,128)(2,1)S(1)}, bf16[16,64,128]{2,1,0:T(8,128)(2,1)S(1)}, u32[]{:S(2)}, u32[]{:S(2)}) collective-permute-start(bf16[16,64,128]{2,1,0:T(8,128)(2,1)S(1)} %get-tuple-element.11), channel_id=1, source_target_pairs={{0,256},{16,80},{32,288},{48,112},{64,320},{80,16},{96,352},{112,4... | collective-permute-start | bytes 786440 | tf_op jit(solution)/shard_map/ppermute | solution.py:94
  48.9 2.7 %collective-permute-start.3 = (bf16[16,64,128]{2,1,0:T(8,128)(2,1)S(1)}, bf16[16,64,128]{2,1,0:T(8,128)(2,1)S(1)}, u32[]{:S(2)}, u32[]{:S(2)}) collective-permute-start(bf16[16,64,128]{2,1,0:T(8,128)(2,1)S(1)} %get-tuple-element.11), channel_id=1, source_target_pairs={{0,384},{16,112},{32,416},{48,16},{64,448},{80,48},{96,480},{112,8... | collective-permute-start | bytes 786440 | tf_op jit(solution)/shard_map/ppermute | solution.py:94
  56.4 4.4 %collective-permute-start.7 = (bf16[2,16,64,128]{3,2,1,0:T(8,128)(2,1)S(1)}, bf16[2,16,64,128]{3,2,1,0:T(8,128)(2,1)S(1)}, u32[]{:S(2)}, u32[]{:S(2)}) collective-permute-start(bf16[2,16,64,128]{3,2,1,0:T(8,128)(2,1)S(1)} %pad_maximum_fusion.1.refs_1_), channel_id=1, source_target_pairs={{0,96},{16,400},{32,0},{48,432},{64,32},{80,464},{96,64},{112,496}... | collective-permute-start | bytes 1572872 | tf_op jit(solution)/shard_map/ppermute | solution.py:94
  63.4 4.7 %collective-permute-start = (bf16[128,2048]{1,0:T(8,128)(2,1)}, bf16[128,2048]{1,0:T(8,128)(2,1)}, u32[]{:S(2)}, u32[]{:S(2)}) collective-permute-start(bf16[128,2048]{1,0:T(8,128)(2,1)} %bitcast.18), channel_id=1, source_target_pairs={{0,16},{16,0},{32,48},{48,32},{64,80},{80,64},{96,112},{112,96},{1... | collective-permute-start | bytes 1572872 | tf_op jit(solution)/shard_map/ppermute | solution.py:106
  70.0 4.6 %collective-permute-start.9 = (bf16[2,16,64,128]{3,2,1,0:T(8,128)(2,1)S(1)}, bf16[2,16,64,128]{3,2,1,0:T(8,128)(2,1)}, u32[]{:S(2)}, u32[]{:S(2)}) collective-permute-start(bf16[2,16,64,128]{3,2,1,0:T(8,128)(2,1)S(1)} %pad_maximum_fusion.refs_0_), channel_id=1, source_target_pairs={{0,96},{16,400},{32,0},{48,432},{64,32},{80,464},{96,64},{112,496}... | collective-permute-start | bytes 1572872 | tf_op jit(solution)/shard_map/ppermute | solution.py:94
  76.6 3.3 %collective-permute-start.6 = (bf16[2,16,64,128]{3,2,1,0:T(8,128)(2,1)S(1)}, bf16[2,16,64,128]{3,2,1,0:T(8,128)(2,1)}, u32[]{:S(2)}, u32[]{:S(2)}) collective-permute-start(bf16[2,16,64,128]{3,2,1,0:T(8,128)(2,1)S(1)} %collective-permute-done.4.refs_2_), channel_id=1, source_target_pairs={{0,32},{16,144},{32,64},{48,176},{64,96},{80,208},{96,0},{112,240}... | collective-permute-start | bytes 1572872 | tf_op jit(solution)/shard_map/ppermute | solution.py:94
  80.7 5.6 %collective-permute-done.8.refs_5_ = bf16[2,16,64,128]{3,2,1,0:T(8,128)(2,1)} collective-permute-done((bf16[2,16,64,128]{3,2,1,0:T(8,128)(2,1)S(1)}, bf16[2,16,64,128]{3,2,1,0:T(8,128)(2,1)}, u32[]{:S(2)}, u32[]{:S(2)}) %collective-permute-start.8) | collective-permute-done | bytes 524320 | tf_op jit(solution)/shard_map/ppermute | solution.py:94
  89.2 3.4 %project.1 = (f32[16,128,128]{2,1,0:T(8,128)S(1)}, f32[16,128,128]{2,1,0:T(8,128)S(1)}) custom-call(s32[17]{0:T(128)S(1)} %dynamic-slice_bitcast_fusion.place_ref, bf16[128,2048]{1,0:T(8,128)(2,1)S(1)} %bitcast.19, bf16[128,2048]{1,0:T(8,128)(2,1)} %collective-permute-done.t_ref, bf16[2,16,64,128]{3,2,1,0:T(8,128)(2,1)S(1)} %pad_maximum_fusion.refs_0_, ...), custom_call_target="tpu_custom_call" | custom-call | flops 1073741824 | bytes 4194304 | tf_op jit(solution)/shard_map/project/pallas_call | solution.py:208
  92.6 4.5 %collective-permute-start.10 = (f32[16,128,128]{2,1,0:T(8,128)S(1)}, f32[16,128,128]{2,1,0:T(8,128)S(1)}, u32[]{:S(2)}, u32[]{:S(2)}) collective-permute-start(f32[16,128,128]{2,1,0:T(8,128)S(1)} %get-tuple-element.7), channel_id=1, source_target_pairs={{0,16},{16,0},{32,48},{48,32},{64,80},{80,64},{96,112},{112,96},{1... | collective-permute-start | bytes 3145736 | tf_op jit(solution)/shard_map/ppermute | solution.py:106
  100.3 11.8 %all-to-all-start.1 = ((bf16[16,128,128]{2,1,0:T(8,128)(2,1)}), bf16[16,128,128]{2,1,0:T(8,128)(2,1)}, u32[]{:S(2)}, u32[]{:S(2)}) async-start(bf16[16,128,128]{2,1,0:T(8,128)(2,1)} %add_convert_fusion), calls=%async_computation.1 | async-start | bytes 1048576 | tf_op jit(solution)/shard_map/all_to_all | solution.py:399
  112.1 13.1 %teacher_probs.1.p_ref = f32[2,2,1024,1024]{3,2,1,0:T(8,128)} custom-call(bf16[16,2,64,256]{3,2,1,0:T(8,128)(2,1)S(1)} %bitcast.17), custom_call_target="tpu_custom_call" | custom-call | flops 1073741824 | bytes 16777216 | tf_op jit(solution)/shard_map/teacher_probs/pallas_call | solution.py:252
  125.2 9.7 %all-to-all-done.1 = bf16[16,128,128]{2,1,0:T(8,128)(2,1)} async-done(((bf16[16,128,128]{2,1,0:T(8,128)(2,1)}), bf16[16,128,128]{2,1,0:T(8,128)(2,1)}, u32[]{:S(2)}, u32[]{:S(2)}) %all-to-all-start.1) | async-done | bytes 524320 | tf_op jit(solution)/shard_map/all_to_all | solution.py:399
  134.9 12.4 %head_grads.1 = (bf16[16,2,64,128]{3,2,1,0:T(8,128)(2,1)}, f32[1,128]{1,0:T(1,128)}) custom-call(bf16[16,2,64,128]{3,2,1,0:T(8,128)(2,1)} %bitcast.8.s_ref, f32[2,2,1024,1024]{3,2,1,0:T(8,128)} %teacher_probs.1.p_ref), custom_call_target="tpu_custom_call" | custom-call | flops 3221225472 | bytes 16777216 | tf_op jit(solution)/shard_map/head_grads/pallas_call | solution.py:310
  147.3 12.8 %all-to-all-start.3 = ((bf16[16,128,128]{2,1,0:T(8,128)(2,1)}), bf16[16,128,128]{2,1,0:T(8,128)(2,1)S(1)}, u32[]{:S(2)}, u32[]{:S(2)}) async-start(bf16[16,128,128]{2,1,0:T(8,128)(2,1)} %bitcast.22), calls=%async_computation.3 | async-start | bytes 1048576 | tf_op jit(solution)/shard_map/all_to_all | solution.py:399
  160.2 2.7 %collective-permute-start.12 = (bf16[2,16,64,128]{3,2,1,0:T(8,128)(2,1)S(1)}, bf16[2,16,64,128]{3,2,1,0:T(8,128)(2,1)S(1)}, u32[]{:S(2)}, u32[]{:S(2)}) collective-permute-start(bf16[2,16,64,128]{3,2,1,0:T(8,128)(2,1)S(1)} %pad_maximum_fusion.1.refs_1_), channel_id=1, source_target_pairs={{0,16},{16,0},{32,48},{48,32},{64,80},{80,64},{96,112},{112,96},{1... | collective-permute-start | bytes 1572872 | tf_op jit(solution)/shard_map/ppermute | solution.py:106
  173.0 2.7 %collective-permute-done.20 = f32[1,128]{1,0:T(1,128)S(1)} collective-permute-done((f32[1,128]{1,0:T(1,128)S(1)}, f32[1,128]{1,0:T(1,128)S(1)}, u32[]{:S(2)}, u32[]{:S(2)}) %collective-permute-start.20) | collective-permute-done | bytes 544 | tf_op jit(solution)/shard_map/ppermute | solution.py:393
  177.9 3.8 %collective-permute-done.21 = f32[1,128]{1,0:T(1,128)S(1)} collective-permute-done((f32[1,128]{1,0:T(1,128)S(1)}, f32[1,128]{1,0:T(1,128)S(1)}, u32[]{:S(2)}, u32[]{:S(2)}) %collective-permute-start.21) | collective-permute-done | bytes 544 | tf_op jit(solution)/shard_map/ppermute | solution.py:393
  186.4 3.7 %collective-permute-start.23 = (f32[1,128]{1,0:T(1,128)S(1)}, f32[1,128]{1,0:T(1,128)S(1)}, u32[]{:S(2)}, u32[]{:S(2)}) collective-permute-start(f32[1,128]{1,0:T(1,128)S(1)} %add.44), channel_id=1, source_target_pairs={{0,256},{16,272},{32,288},{48,304},{64,320},{80,336},{96,352},{112... | collective-permute-start | bytes 1544 | tf_op jit(solution)/shard_map/ppermute | solution.py:393
  190.0 4.6 %collective-permute-start.14 = (bf16[2,16,64,128]{3,2,1,0:T(8,128)(2,1)}, bf16[2,16,64,128]{3,2,1,0:T(8,128)(2,1)S(1)}, u32[]{:S(2)}, u32[]{:S(2)}) collective-permute-start(bf16[2,16,64,128]{3,2,1,0:T(8,128)(2,1)} %collective-permute-done.5.refs_3_), channel_id=1, source_target_pairs={{0,16},{16,0},{32,48},{48,32},{64,80},{80,64},{96,112},{112,96},{1... | collective-permute-start | bytes 1572872 | tf_op jit(solution)/shard_map/ppermute | solution.py:106
  216.9 5.5 %hidden_grads.1 = bf16[128,2048]{1,0:T(8,128)(2,1)} custom-call(s32[17]{0:T(128)S(1)} %dynamic-slice_bitcast_fusion.place_ref, bf16[16,128,128]{2,1,0:T(8,128)(2,1)S(1)} %all-to-all-done.3.g_ref, bf16[2,16,64,128]{3,2,1,0:T(8,128)(2,1)S(1)} %pad_maximum_fusion.refs_0_, bf16[2,16,64,128]{3,2,1,0:T(8,128)(2,1)S(1)} %pad_maximum_fusion.1.refs_1_, ...), custom_call_target="tpu_custom_call" | custom-call | flops 1073741824 | bytes 8388608 | tf_op jit(solution)/shard_map/hidden_grads/pallas_call | solution.py:365
  (79 shorter events, 59.3 us)
Async XLA Ops:
  2.8 29.9 %all-to-all-start = ((bf16[16,72,128]{2,1,0:T(8,128)(2,1)}), bf16[16,72,128]{2,1,0:T(8,128)(2,1)S(1)}, u32[]{:S(2)}, u32[]{:S(2)}) async-start(bf16[16,72,128]{2,1,0:T(8,128)(2,1)} %copies_of_piece.1), calls=%async_computation | async-start | bytes 589824 | tf_op jit(solution)/shard_map/all_to_all | solution.py:399
  32.7 67.6 %all-to-all-start.2 = ((bf16[16,128,256]{2,1,0:T(8,128)(2,1)}), bf16[16,128,256]{2,1,0:T(8,128)(2,1)S(1)}, u32[]{:S(2)}, u32[]{:S(2)}) async-start(bf16[16,128,256]{2,1,0:T(8,128)(2,1)} %split_columns.1), calls=%async_computation.2 | async-start | bytes 2097152 | tf_op jit(solution)/shard_map/all_to_all | solution.py:399
  44.1 10.1 %collective-permute-start.2 = (bf16[16,64,128]{2,1,0:T(8,128)(2,1)S(1)}, bf16[16,64,128]{2,1,0:T(8,128)(2,1)S(1)}, u32[]{:S(2)}, u32[]{:S(2)}) collective-permute-start(bf16[16,64,128]{2,1,0:T(8,128)(2,1)S(1)} %get-tuple-element.11), channel_id=1, source_target_pairs={{0,256},{16,80},{32,288},{48,112},{64,320},{80,16},{96,352},{112,4... | collective-permute-start | bytes 786440 | tf_op jit(solution)/shard_map/ppermute | solution.py:94
  48.9 7.4 %collective-permute-start.3 = (bf16[16,64,128]{2,1,0:T(8,128)(2,1)S(1)}, bf16[16,64,128]{2,1,0:T(8,128)(2,1)S(1)}, u32[]{:S(2)}, u32[]{:S(2)}) collective-permute-start(bf16[16,64,128]{2,1,0:T(8,128)(2,1)S(1)} %get-tuple-element.11), channel_id=1, source_target_pairs={{0,384},{16,112},{32,416},{48,16},{64,448},{80,48},{96,480},{112,8... | collective-permute-start | bytes 786440 | tf_op jit(solution)/shard_map/ppermute | solution.py:94
  51.6 9.2 %collective-permute-start.1 = (bf16[16,64,128]{2,1,0:T(8,128)(2,1)S(1)}, bf16[16,64,128]{2,1,0:T(8,128)(2,1)S(1)}, u32[]{:S(2)}, u32[]{:S(2)}) collective-permute-start(bf16[16,64,128]{2,1,0:T(8,128)(2,1)S(1)} %get-tuple-element.11), channel_id=1, source_target_pairs={{0,128},{16,48},{32,160},{48,80},{64,192},{80,112},{96,224},{112,1... | collective-permute-start | bytes 786440 | tf_op jit(solution)/shard_map/ppermute | solution.py:94
  56.4 18.2 %collective-permute-start.7 = (bf16[2,16,64,128]{3,2,1,0:T(8,128)(2,1)S(1)}, bf16[2,16,64,128]{3,2,1,0:T(8,128)(2,1)S(1)}, u32[]{:S(2)}, u32[]{:S(2)}) collective-permute-start(bf16[2,16,64,128]{3,2,1,0:T(8,128)(2,1)S(1)} %pad_maximum_fusion.1.refs_1_), channel_id=1, source_target_pairs={{0,96},{16,400},{32,0},{48,432},{64,32},{80,464},{96,64},{112,496}... | collective-permute-start | bytes 1572872 | tf_op jit(solution)/shard_map/ppermute | solution.py:94
  60.9 15.7 %collective-permute-start.4 = (bf16[2,16,64,128]{3,2,1,0:T(8,128)(2,1)S(1)}, bf16[2,16,64,128]{3,2,1,0:T(8,128)(2,1)S(1)}, u32[]{:S(2)}, u32[]{:S(2)}) collective-permute-start(bf16[2,16,64,128]{3,2,1,0:T(8,128)(2,1)S(1)} %pad_maximum_fusion.refs_0_), channel_id=1, source_target_pairs={{0,32},{16,144},{32,64},{48,176},{64,96},{80,208},{96,0},{112,240}... | collective-permute-start | bytes 1572872 | tf_op jit(solution)/shard_map/ppermute | solution.py:94
  63.4 17.2 %collective-permute-start = (bf16[128,2048]{1,0:T(8,128)(2,1)}, bf16[128,2048]{1,0:T(8,128)(2,1)}, u32[]{:S(2)}, u32[]{:S(2)}) collective-permute-start(bf16[128,2048]{1,0:T(8,128)(2,1)} %bitcast.18), channel_id=1, source_target_pairs={{0,16},{16,0},{32,48},{48,32},{64,80},{80,64},{96,112},{112,96},{1... | collective-permute-start | bytes 1572872 | tf_op jit(solution)/shard_map/ppermute | solution.py:106
  68.1 12.5 %collective-permute-start.5 = (bf16[2,16,64,128]{3,2,1,0:T(8,128)(2,1)S(1)}, bf16[2,16,64,128]{3,2,1,0:T(8,128)(2,1)}, u32[]{:S(2)}, u32[]{:S(2)}) collective-permute-start(bf16[2,16,64,128]{3,2,1,0:T(8,128)(2,1)S(1)} %pad_maximum_fusion.1.refs_1_), channel_id=1, source_target_pairs={{0,32},{16,144},{32,64},{48,176},{64,96},{80,208},{96,0},{112,240}... | collective-permute-start | bytes 1572872 | tf_op jit(solution)/shard_map/ppermute | solution.py:94
  70.0 10.7 %collective-permute-start.9 = (bf16[2,16,64,128]{3,2,1,0:T(8,128)(2,1)S(1)}, bf16[2,16,64,128]{3,2,1,0:T(8,128)(2,1)}, u32[]{:S(2)}, u32[]{:S(2)}) collective-permute-start(bf16[2,16,64,128]{3,2,1,0:T(8,128)(2,1)S(1)} %pad_maximum_fusion.refs_0_), channel_id=1, source_target_pairs={{0,96},{16,400},{32,0},{48,432},{64,32},{80,464},{96,64},{112,496}... | collective-permute-start | bytes 1572872 | tf_op jit(solution)/shard_map/ppermute | solution.py:94
  74.6 11.7 %collective-permute-start.8 = (bf16[2,16,64,128]{3,2,1,0:T(8,128)(2,1)S(1)}, bf16[2,16,64,128]{3,2,1,0:T(8,128)(2,1)}, u32[]{:S(2)}, u32[]{:S(2)}) collective-permute-start(bf16[2,16,64,128]{3,2,1,0:T(8,128)(2,1)S(1)} %collective-permute-done.7.refs_7_), channel_id=1, source_target_pairs={{0,96},{16,400},{32,0},{48,432},{64,32},{80,464},{96,64},{112,496}... | collective-permute-start | bytes 1572872 | tf_op jit(solution)/shard_map/ppermute | solution.py:94
  76.6 11.5 %collective-permute-start.6 = (bf16[2,16,64,128]{3,2,1,0:T(8,128)(2,1)S(1)}, bf16[2,16,64,128]{3,2,1,0:T(8,128)(2,1)}, u32[]{:S(2)}, u32[]{:S(2)}) collective-permute-start(bf16[2,16,64,128]{3,2,1,0:T(8,128)(2,1)S(1)} %collective-permute-done.4.refs_2_), channel_id=1, source_target_pairs={{0,32},{16,144},{32,64},{48,176},{64,96},{80,208},{96,0},{112,240}... | collective-permute-start | bytes 1572872 | tf_op jit(solution)/shard_map/ppermute | solution.py:94
  92.6 6.8 %collective-permute-start.10 = (f32[16,128,128]{2,1,0:T(8,128)S(1)}, f32[16,128,128]{2,1,0:T(8,128)S(1)}, u32[]{:S(2)}, u32[]{:S(2)}) collective-permute-start(f32[16,128,128]{2,1,0:T(8,128)S(1)} %get-tuple-element.7), channel_id=1, source_target_pairs={{0,16},{16,0},{32,48},{48,32},{64,80},{80,64},{96,112},{112,96},{1... | collective-permute-start | bytes 3145736 | tf_op jit(solution)/shard_map/ppermute | solution.py:106
  100.3 34.6 %all-to-all-start.1 = ((bf16[16,128,128]{2,1,0:T(8,128)(2,1)}), bf16[16,128,128]{2,1,0:T(8,128)(2,1)}, u32[]{:S(2)}, u32[]{:S(2)}) async-start(bf16[16,128,128]{2,1,0:T(8,128)(2,1)} %add_convert_fusion), calls=%async_computation.1 | async-start | bytes 1048576 | tf_op jit(solution)/shard_map/all_to_all | solution.py:399
  147.3 62.3 %all-to-all-start.3 = ((bf16[16,128,128]{2,1,0:T(8,128)(2,1)}), bf16[16,128,128]{2,1,0:T(8,128)(2,1)S(1)}, u32[]{:S(2)}, u32[]{:S(2)}) async-start(bf16[16,128,128]{2,1,0:T(8,128)(2,1)} %bitcast.22), calls=%async_computation.3 | async-start | bytes 1048576 | tf_op jit(solution)/shard_map/all_to_all | solution.py:399
  160.2 34.5 %collective-permute-start.12 = (bf16[2,16,64,128]{3,2,1,0:T(8,128)(2,1)S(1)}, bf16[2,16,64,128]{3,2,1,0:T(8,128)(2,1)S(1)}, u32[]{:S(2)}, u32[]{:S(2)}) collective-permute-start(bf16[2,16,64,128]{3,2,1,0:T(8,128)(2,1)S(1)} %pad_maximum_fusion.1.refs_1_), channel_id=1, source_target_pairs={{0,16},{16,0},{32,48},{48,32},{64,80},{80,64},{96,112},{112,96},{1... | collective-permute-start | bytes 1572872 | tf_op jit(solution)/shard_map/ppermute | solution.py:106
  162.9 33.8 %collective-permute-start.11 = (bf16[2,16,64,128]{3,2,1,0:T(8,128)(2,1)S(1)}, bf16[2,16,64,128]{3,2,1,0:T(8,128)(2,1)S(1)}, u32[]{:S(2)}, u32[]{:S(2)}) collective-permute-start(bf16[2,16,64,128]{3,2,1,0:T(8,128)(2,1)S(1)} %pad_maximum_fusion.refs_0_), channel_id=1, source_target_pairs={{0,16},{16,0},{32,48},{48,32},{64,80},{80,64},{96,112},{112,96},{1... | collective-permute-start | bytes 1572872 | tf_op jit(solution)/shard_map/ppermute | solution.py:106
  164.8 35.1 %collective-permute-start.18 = (bf16[2,16,64,128]{3,2,1,0:T(8,128)(2,1)S(1)}, bf16[2,16,64,128]{3,2,1,0:T(8,128)(2,1)S(1)}, u32[]{:S(2)}, u32[]{:S(2)}) collective-permute-start(bf16[2,16,64,128]{3,2,1,0:T(8,128)(2,1)S(1)} %collective-permute-done.7.refs_7_), channel_id=1, source_target_pairs={{0,16},{16,0},{32,48},{48,32},{64,80},{80,64},{96,112},{112,96},{1... | collective-permute-start | bytes 1572872 | tf_op jit(solution)/shard_map/ppermute | solution.py:106
  186.4 16.2 %collective-permute-start.23 = (f32[1,128]{1,0:T(1,128)S(1)}, f32[1,128]{1,0:T(1,128)S(1)}, u32[]{:S(2)}, u32[]{:S(2)}) collective-permute-start(f32[1,128]{1,0:T(1,128)S(1)} %add.44), channel_id=1, source_target_pairs={{0,256},{16,272},{32,288},{48,304},{64,320},{80,336},{96,352},{112... | collective-permute-start | bytes 1544 | tf_op jit(solution)/shard_map/ppermute | solution.py:393
  190.0 15.5 %collective-permute-start.14 = (bf16[2,16,64,128]{3,2,1,0:T(8,128)(2,1)}, bf16[2,16,64,128]{3,2,1,0:T(8,128)(2,1)S(1)}, u32[]{:S(2)}, u32[]{:S(2)}) collective-permute-start(bf16[2,16,64,128]{3,2,1,0:T(8,128)(2,1)} %collective-permute-done.5.refs_3_), channel_id=1, source_target_pairs={{0,16},{16,0},{32,48},{48,32},{64,80},{80,64},{96,112},{112,96},{1... | collective-permute-start | bytes 1572872 | tf_op jit(solution)/shard_map/ppermute | solution.py:106
  194.7 11.6 %collective-permute-start.13 = (bf16[2,16,64,128]{3,2,1,0:T(8,128)(2,1)S(1)}, bf16[2,16,64,128]{3,2,1,0:T(8,128)(2,1)S(1)}, u32[]{:S(2)}, u32[]{:S(2)}) collective-permute-start(bf16[2,16,64,128]{3,2,1,0:T(8,128)(2,1)S(1)} %collective-permute-done.4.refs_2_), channel_id=1, source_target_pairs={{0,16},{16,0},{32,48},{48,32},{64,80},{80,64},{96,112},{112,96},{1... | collective-permute-start | bytes 1572872 | tf_op jit(solution)/shard_map/ppermute | solution.py:106
  197.5 9.7 %collective-permute-start.17 = (bf16[2,16,64,128]{3,2,1,0:T(8,128)(2,1)}, bf16[2,16,64,128]{3,2,1,0:T(8,128)(2,1)S(1)}, u32[]{:S(2)}, u32[]{:S(2)}) collective-permute-start(bf16[2,16,64,128]{3,2,1,0:T(8,128)(2,1)} %collective-permute-done.9.refs_6_), channel_id=1, source_target_pairs={{0,16},{16,0},{32,48},{48,32},{64,80},{80,64},{96,112},{112,96},{1... | collective-permute-start | bytes 1572872 | tf_op jit(solution)/shard_map/ppermute | solution.py:106
  200.7 7.3 %collective-permute-start.16 = (bf16[2,16,64,128]{3,2,1,0:T(8,128)(2,1)}, bf16[2,16,64,128]{3,2,1,0:T(8,128)(2,1)S(1)}, u32[]{:S(2)}, u32[]{:S(2)}) collective-permute-start(bf16[2,16,64,128]{3,2,1,0:T(8,128)(2,1)} %collective-permute-done.8.refs_5_), channel_id=1, source_target_pairs={{0,16},{16,0},{32,48},{48,32},{64,80},{80,64},{96,112},{112,96},{1... | collective-permute-start | bytes 1572872 | tf_op jit(solution)/shard_map/ppermute | solution.py:106
  202.6 6.2 %collective-permute-start.15 = (bf16[2,16,64,128]{3,2,1,0:T(8,128)(2,1)}, bf16[2,16,64,128]{3,2,1,0:T(8,128)(2,1)S(1)}, u32[]{:S(2)}, u32[]{:S(2)}) collective-permute-start(bf16[2,16,64,128]{3,2,1,0:T(8,128)(2,1)} %collective-permute-done.6.refs_4_), channel_id=1, source_target_pairs={{0,16},{16,0},{32,48},{48,32},{64,80},{80,64},{96,112},{112,96},{1... | collective-permute-start | bytes 1572872 | tf_op jit(solution)/shard_map/ppermute | solution.py:106
  (19 other events, 32.5 us)

commit v7 on v6

--- a/solution.py
+++ b/solution.py
@@ -73,7 +73,7 @@
 SIDE = 4
 LANE = 128
 TAKE = 8
-EARLY = 3
+EARLY = 4
 
 
 def ring_pairs(shift, first):
@@ -418,11 +418,12 @@
     rows = student_hidden.reshape(seqs * toks, width)
     other_rows = swap_cores([rows])[0]
     swapped = swap_cores(weights[:EARLY])
+    swapped += swap_cores(weights[EARLY : EARLY + 1])
     kept, sent = project(rows, other_rows, weights, place)
     got = swap_cores([sent])[0]
     values = (kept + got + bias.astype(F32)).astype(BF16)
     values = exchange(values)
-    weights = weights + swapped + swap_cores(weights[EARLY:])
+    weights = weights + swapped + swap_cores(weights[EARLY + 1 :])
     grads, total = head_grads(values, probs)
     grads = exchange(grads)
     hidden_grad = hidden_grads(grads, weights, place).reshape(student_hidden.shape)

time: 225 us -> 225 us (level)
  no operation moved by 1% of the time
where the time goes in v7:
time: 225 us; the launch traced here: 222 us
  starting transfers between devices  122 us (54%)
  Pallas kernels  45.3 us (20%)
  waiting for transfers between devices  36.9 us (16%)
  local copies, waits for them, and re-layouts  14.8 us (7%)
  other arithmetic  2.27 us (1%)
    all_to_all x4, starting transfers between devices, exchange(): return lax.all_to_all(x, 'tok', split_axis=0, concat_axis=0, tiled=True)  51.6 us
    ppermute x10, starting transfers between devices, swap_cores(): return [lax.ppermute(v, 'dp', swap) for v in values]  29.4 us
    ppermute x9, starting transfers between devices, send(): return lax.ppermute(v, 'dp', ring_pairs(shift, first))  28.8 us
    all_to_all x4, waiting for transfers between devices, exchange(): return lax.all_to_all(x, 'tok', split_axis=0, concat_axis=0, tiled=True)  15.1 us
    unnamed x30, local copies, waits for them, and re-layouts  14 us
    pallas_call x1, Pallas kernels, teacher_probs(): pl.pallas_call(kernel, grid=(seqs, heads, length // step), in_specs=[pl.B...  13.1 us
    pallas_call x1, Pallas kernels, head_grads(): pl.pallas_call(kernel, grid=(seqs, length // step), in_specs=[pl.BlockSpe...  12.4 us
    ppermute x5, starting transfers between devices, sum_over(): x = x + lax.ppermute(x, axis, [(i, i ^ reach) for i in range(size)])  12.3 us
  transfers between devices with their start and end apart: 28, of which 11 were waited for; matrix products, arithmetic and copies ran while one was open for 1% of the time, Pallas kernels for 11%

profile of v7, /device:TPU:1, one launch (start us, length us, event | category | flops | bytes accessed | tf_op | source)
XLA Modules:
  0.0 222.4 jit_solution(17620041819776130729)
XLA Ops:
  2.8 15.7 %all-to-all-start = ((bf16[16,72,128]{2,1,0:T(8,128)(2,1)}), bf16[16,72,128]{2,1,0:T(8,128)(2,1)S(1)}, u32[]{:S(2)}, u32[]{:S(2)}) async-start(bf16[16,72,128]{2,1,0:T(8,128)(2,1)} %copies_of_piece.1), calls=%async_computation | async-start | bytes 589824 | tf_op jit(solution)/shard_map/all_to_all | solution.py:399
  18.5 8.8 %split_columns.1 = bf16[16,128,256]{2,1,0:T(8,128)(2,1)} custom-call(bf16[128,4096]{1,0:T(8,128)(2,1)} %bitcast.20), custom_call_target="tpu_custom_call" | custom-call | tf_op jit(solution)/shard_map/split_columns/pallas_call | solution.py:36
  27.3 5.4 %all-to-all-done = bf16[16,72,128]{2,1,0:T(8,128)(2,1)S(1)} async-done(((bf16[16,72,128]{2,1,0:T(8,128)(2,1)}), bf16[16,72,128]{2,1,0:T(8,128)(2,1)S(1)}, u32[]{:S(2)}, u32[]{:S(2)}) %all-to-all-start) | async-done | bytes 294944 | tf_op jit(solution)/shard_map/all_to_all | solution.py:399
  32.7 11.3 %all-to-all-start.2 = ((bf16[16,128,256]{2,1,0:T(8,128)(2,1)}), bf16[16,128,256]{2,1,0:T(8,128)(2,1)S(1)}, u32[]{:S(2)}, u32[]{:S(2)}) async-start(bf16[16,128,256]{2,1,0:T(8,128)(2,1)} %split_columns.1), calls=%async_computation.2 | async-start | bytes 2097152 | tf_op jit(solution)/shard_map/all_to_all | solution.py:399
  44.1 4.8 %collective-permute-start.2 = (bf16[16,64,128]{2,1,0:T(8,128)(2,1)S(1)}, bf16[16,64,128]{2,1,0:T(8,128)(2,1)S(1)}, u32[]{:S(2)}, u32[]{:S(2)}) collective-permute-start(bf16[16,64,128]{2,1,0:T(8,128)(2,1)S(1)} %get-tuple-element.11), channel_id=1, source_target_pairs={{0,256},{16,80},{32,288},{48,112},{64,320},{80,16},{96,352},{112,4... | collective-permute-start | bytes 786440 | tf_op jit(solution)/shard_map/ppermute | solution.py:94
  48.9 2.7 %collective-permute-start.3 = (bf16[16,64,128]{2,1,0:T(8,128)(2,1)S(1)}, bf16[16,64,128]{2,1,0:T(8,128)(2,1)S(1)}, u32[]{:S(2)}, u32[]{:S(2)}) collective-permute-start(bf16[16,64,128]{2,1,0:T(8,128)(2,1)S(1)} %get-tuple-element.11), channel_id=1, source_target_pairs={{0,384},{16,112},{32,416},{48,16},{64,448},{80,48},{96,480},{112,8... | collective-permute-start | bytes 786440 | tf_op jit(solution)/shard_map/ppermute | solution.py:94
  56.4 4.4 %collective-permute-start.7 = (bf16[2,16,64,128]{3,2,1,0:T(8,128)(2,1)S(1)}, bf16[2,16,64,128]{3,2,1,0:T(8,128)(2,1)S(1)}, u32[]{:S(2)}, u32[]{:S(2)}) collective-permute-start(bf16[2,16,64,128]{3,2,1,0:T(8,128)(2,1)S(1)} %pad_maximum_fusion.1.refs_1_), channel_id=1, source_target_pairs={{0,96},{16,400},{32,0},{48,432},{64,32},{80,464},{96,64},{112,496}... | collective-permute-start | bytes 1572872 | tf_op jit(solution)/shard_map/ppermute | solution.py:94
  63.4 4.7 %collective-permute-start = (bf16[128,2048]{1,0:T(8,128)(2,1)}, bf16[128,2048]{1,0:T(8,128)(2,1)}, u32[]{:S(2)}, u32[]{:S(2)}) collective-permute-start(bf16[128,2048]{1,0:T(8,128)(2,1)} %bitcast.18), channel_id=1, source_target_pairs={{0,16},{16,0},{32,48},{48,32},{64,80},{80,64},{96,112},{112,96},{1... | collective-permute-start | bytes 1572872 | tf_op jit(solution)/shard_map/ppermute | solution.py:106
  70.0 4.6 %collective-permute-start.9 = (bf16[2,16,64,128]{3,2,1,0:T(8,128)(2,1)S(1)}, bf16[2,16,64,128]{3,2,1,0:T(8,128)(2,1)}, u32[]{:S(2)}, u32[]{:S(2)}) collective-permute-start(bf16[2,16,64,128]{3,2,1,0:T(8,128)(2,1)S(1)} %pad_maximum_fusion.refs_0_), channel_id=1, source_target_pairs={{0,96},{16,400},{32,0},{48,432},{64,32},{80,464},{96,64},{112,496}... | collective-permute-start | bytes 1572872 | tf_op jit(solution)/shard_map/ppermute | solution.py:94
  76.6 3.3 %collective-permute-start.6 = (bf16[2,16,64,128]{3,2,1,0:T(8,128)(2,1)S(1)}, bf16[2,16,64,128]{3,2,1,0:T(8,128)(2,1)}, u32[]{:S(2)}, u32[]{:S(2)}) collective-permute-start(bf16[2,16,64,128]{3,2,1,0:T(8,128)(2,1)S(1)} %collective-permute-done.4.refs_2_), channel_id=1, source_target_pairs={{0,32},{16,144},{32,64},{48,176},{64,96},{80,208},{96,0},{112,240}... | collective-permute-start | bytes 1572872 | tf_op jit(solution)/shard_map/ppermute | solution.py:94
  80.7 5.6 %collective-permute-done.8.refs_5_ = bf16[2,16,64,128]{3,2,1,0:T(8,128)(2,1)} collective-permute-done((bf16[2,16,64,128]{3,2,1,0:T(8,128)(2,1)S(1)}, bf16[2,16,64,128]{3,2,1,0:T(8,128)(2,1)}, u32[]{:S(2)}, u32[]{:S(2)}) %collective-permute-start.8) | collective-permute-done | bytes 524320 | tf_op jit(solution)/shard_map/ppermute | solution.py:94
  89.2 3.4 %project.1 = (f32[16,128,128]{2,1,0:T(8,128)S(1)}, f32[16,128,128]{2,1,0:T(8,128)S(1)}) custom-call(s32[17]{0:T(128)S(1)} %dynamic-slice_bitcast_fusion.place_ref, bf16[128,2048]{1,0:T(8,128)(2,1)S(1)} %bitcast.19, bf16[128,2048]{1,0:T(8,128)(2,1)} %collective-permute-done.t_ref, bf16[2,16,64,128]{3,2,1,0:T(8,128)(2,1)S(1)} %pad_maximum_fusion.refs_0_, ...), custom_call_target="tpu_custom_call" | custom-call | flops 1073741824 | bytes 4194304 | tf_op jit(solution)/shard_map/project/pallas_call | solution.py:208
  92.6 4.5 %collective-permute-start.10 = (f32[16,128,128]{2,1,0:T(8,128)S(1)}, f32[16,128,128]{2,1,0:T(8,128)S(1)}, u32[]{:S(2)}, u32[]{:S(2)}) collective-permute-start(f32[16,128,128]{2,1,0:T(8,128)S(1)} %get-tuple-element.7), channel_id=1, source_target_pairs={{0,16},{16,0},{32,48},{48,32},{64,80},{80,64},{96,112},{112,96},{1... | collective-permute-start | bytes 3145736 | tf_op jit(solution)/shard_map/ppermute | solution.py:106
  100.3 11.8 %all-to-all-start.1 = ((bf16[16,128,128]{2,1,0:T(8,128)(2,1)}), bf16[16,128,128]{2,1,0:T(8,128)(2,1)}, u32[]{:S(2)}, u32[]{:S(2)}) async-start(bf16[16,128,128]{2,1,0:T(8,128)(2,1)} %add_convert_fusion), calls=%async_computation.1 | async-start | bytes 1048576 | tf_op jit(solution)/shard_map/all_to_all | solution.py:399
  112.1 13.1 %teacher_probs.1.p_ref = f32[2,2,1024,1024]{3,2,1,0:T(8,128)} custom-call(bf16[16,2,64,256]{3,2,1,0:T(8,128)(2,1)S(1)} %bitcast.17), custom_call_target="tpu_custom_call" | custom-call | flops 1073741824 | bytes 16777216 | tf_op jit(solution)/shard_map/teacher_probs/pallas_call | solution.py:252
  125.2 9.7 %all-to-all-done.1 = bf16[16,128,128]{2,1,0:T(8,128)(2,1)} async-done(((bf16[16,128,128]{2,1,0:T(8,128)(2,1)}), bf16[16,128,128]{2,1,0:T(8,128)(2,1)}, u32[]{:S(2)}, u32[]{:S(2)}) %all-to-all-start.1) | async-done | bytes 524320 | tf_op jit(solution)/shard_map/all_to_all | solution.py:399
  134.9 12.4 %head_grads.1 = (bf16[16,2,64,128]{3,2,1,0:T(8,128)(2,1)}, f32[1,128]{1,0:T(1,128)}) custom-call(bf16[16,2,64,128]{3,2,1,0:T(8,128)(2,1)} %bitcast.8.s_ref, f32[2,2,1024,1024]{3,2,1,0:T(8,128)} %teacher_probs.1.p_ref), custom_call_target="tpu_custom_call" | custom-call | flops 3221225472 | bytes 16777216 | tf_op jit(solution)/shard_map/head_grads/pallas_call | solution.py:310
  147.3 12.8 %all-to-all-start.3 = ((bf16[16,128,128]{2,1,0:T(8,128)(2,1)}), bf16[16,128,128]{2,1,0:T(8,128)(2,1)S(1)}, u32[]{:S(2)}, u32[]{:S(2)}) async-start(bf16[16,128,128]{2,1,0:T(8,128)(2,1)} %bitcast.22), calls=%async_computation.3 | async-start | bytes 1048576 | tf_op jit(solution)/shard_map/all_to_all | solution.py:399
  160.2 2.7 %collective-permute-start.12 = (bf16[2,16,64,128]{3,2,1,0:T(8,128)(2,1)S(1)}, bf16[2,16,64,128]{3,2,1,0:T(8,128)(2,1)S(1)}, u32[]{:S(2)}, u32[]{:S(2)}) collective-permute-start(bf16[2,16,64,128]{3,2,1,0:T(8,128)(2,1)S(1)} %pad_maximum_fusion.1.refs_1_), channel_id=1, source_target_pairs={{0,16},{16,0},{32,48},{48,32},{64,80},{80,64},{96,112},{112,96},{1... | collective-permute-start | bytes 1572872 | tf_op jit(solution)/shard_map/ppermute | solution.py:106
  173.0 2.7 %collective-permute-done.20 = f32[1,128]{1,0:T(1,128)S(1)} collective-permute-done((f32[1,128]{1,0:T(1,128)S(1)}, f32[1,128]{1,0:T(1,128)S(1)}, u32[]{:S(2)}, u32[]{:S(2)}) %collective-permute-start.20) | collective-permute-done | bytes 544 | tf_op jit(solution)/shard_map/ppermute | solution.py:393
  177.9 3.8 %collective-permute-done.21 = f32[1,128]{1,0:T(1,128)S(1)} collective-permute-done((f32[1,128]{1,0:T(1,128)S(1)}, f32[1,128]{1,0:T(1,128)S(1)}, u32[]{:S(2)}, u32[]{:S(2)}) %collective-permute-start.21) | collective-permute-done | bytes 544 | tf_op jit(solution)/shard_map/ppermute | solution.py:393
  186.4 3.7 %collective-permute-start.23 = (f32[1,128]{1,0:T(1,128)S(1)}, f32[1,128]{1,0:T(1,128)S(1)}, u32[]{:S(2)}, u32[]{:S(2)}) collective-permute-start(f32[1,128]{1,0:T(1,128)S(1)} %add.44), channel_id=1, source_target_pairs={{0,256},{16,272},{32,288},{48,304},{64,320},{80,336},{96,352},{112... | collective-permute-start | bytes 1544 | tf_op jit(solution)/shard_map/ppermute | solution.py:393
  190.0 4.6 %collective-permute-start.14 = (bf16[2,16,64,128]{3,2,1,0:T(8,128)(2,1)}, bf16[2,16,64,128]{3,2,1,0:T(8,128)(2,1)S(1)}, u32[]{:S(2)}, u32[]{:S(2)}) collective-permute-start(bf16[2,16,64,128]{3,2,1,0:T(8,128)(2,1)} %collective-permute-done.5.refs_3_), channel_id=1, source_target_pairs={{0,16},{16,0},{32,48},{48,32},{64,80},{80,64},{96,112},{112,96},{1... | collective-permute-start | bytes 1572872 | tf_op jit(solution)/shard_map/ppermute | solution.py:106
  216.9 5.5 %hidden_grads.1 = bf16[128,2048]{1,0:T(8,128)(2,1)} custom-call(s32[17]{0:T(128)S(1)} %dynamic-slice_bitcast_fusion.place_ref, bf16[16,128,128]{2,1,0:T(8,128)(2,1)S(1)} %all-to-all-done.3.g_ref, bf16[2,16,64,128]{3,2,1,0:T(8,128)(2,1)S(1)} %pad_maximum_fusion.refs_0_, bf16[2,16,64,128]{3,2,1,0:T(8,128)(2,1)S(1)} %pad_maximum_fusion.1.refs_1_, ...), custom_call_target="tpu_custom_call" | custom-call | flops 1073741824 | bytes 8388608 | tf_op jit(solution)/shard_map/hidden_grads/pallas_call | solution.py:365
  (79 shorter events, 59.3 us)
Async XLA Ops:
  2.8 29.9 %all-to-all-start = ((bf16[16,72,128]{2,1,0:T(8,128)(2,1)}), bf16[16,72,128]{2,1,0:T(8,128)(2,1)S(1)}, u32[]{:S(2)}, u32[]{:S(2)}) async-start(bf16[16,72,128]{2,1,0:T(8,128)(2,1)} %copies_of_piece.1), calls=%async_computation | async-start | bytes 589824 | tf_op jit(solution)/shard_map/all_to_all | solution.py:399
  32.7 67.6 %all-to-all-start.2 = ((bf16[16,128,256]{2,1,0:T(8,128)(2,1)}), bf16[16,128,256]{2,1,0:T(8,128)(2,1)S(1)}, u32[]{:S(2)}, u32[]{:S(2)}) async-start(bf16[16,128,256]{2,1,0:T(8,128)(2,1)} %split_columns.1), calls=%async_computation.2 | async-start | bytes 2097152 | tf_op jit(solution)/shard_map/all_to_all | solution.py:399
  44.1 10.1 %collective-permute-start.2 = (bf16[16,64,128]{2,1,0:T(8,128)(2,1)S(1)}, bf16[16,64,128]{2,1,0:T(8,128)(2,1)S(1)}, u32[]{:S(2)}, u32[]{:S(2)}) collective-permute-start(bf16[16,64,128]{2,1,0:T(8,128)(2,1)S(1)} %get-tuple-element.11), channel_id=1, source_target_pairs={{0,256},{16,80},{32,288},{48,112},{64,320},{80,16},{96,352},{112,4... | collective-permute-start | bytes 786440 | tf_op jit(solution)/shard_map/ppermute | solution.py:94
  48.9 7.4 %collective-permute-start.3 = (bf16[16,64,128]{2,1,0:T(8,128)(2,1)S(1)}, bf16[16,64,128]{2,1,0:T(8,128)(2,1)S(1)}, u32[]{:S(2)}, u32[]{:S(2)}) collective-permute-start(bf16[16,64,128]{2,1,0:T(8,128)(2,1)S(1)} %get-tuple-element.11), channel_id=1, source_target_pairs={{0,384},{16,112},{32,416},{48,16},{64,448},{80,48},{96,480},{112,8... | collective-permute-start | bytes 786440 | tf_op jit(solution)/shard_map/ppermute | solution.py:94
  51.6 9.2 %collective-permute-start.1 = (bf16[16,64,128]{2,1,0:T(8,128)(2,1)S(1)}, bf16[16,64,128]{2,1,0:T(8,128)(2,1)S(1)}, u32[]{:S(2)}, u32[]{:S(2)}) collective-permute-start(bf16[16,64,128]{2,1,0:T(8,128)(2,1)S(1)} %get-tuple-element.11), channel_id=1, source_target_pairs={{0,128},{16,48},{32,160},{48,80},{64,192},{80,112},{96,224},{112,1... | collective-permute-start | bytes 786440 | tf_op jit(solution)/shard_map/ppermute | solution.py:94
  56.4 18.2 %collective-permute-start.7 = (bf16[2,16,64,128]{3,2,1,0:T(8,128)(2,1)S(1)}, bf16[2,16,64,128]{3,2,1,0:T(8,128)(2,1)S(1)}, u32[]{:S(2)}, u32[]{:S(2)}) collective-permute-start(bf16[2,16,64,128]{3,2,1,0:T(8,128)(2,1)S(1)} %pad_maximum_fusion.1.refs_1_), channel_id=1, source_target_pairs={{0,96},{16,400},{32,0},{48,432},{64,32},{80,464},{96,64},{112,496}... | collective-permute-start | bytes 1572872 | tf_op jit(solution)/shard_map/ppermute | solution.py:94
  60.9 15.7 %collective-permute-start.4 = (bf16[2,16,64,128]{3,2,1,0:T(8,128)(2,1)S(1)}, bf16[2,16,64,128]{3,2,1,0:T(8,128)(2,1)S(1)}, u32[]{:S(2)}, u32[]{:S(2)}) collective-permute-start(bf16[2,16,64,128]{3,2,1,0:T(8,128)(2,1)S(1)} %pad_maximum_fusion.refs_0_), channel_id=1, source_target_pairs={{0,32},{16,144},{32,64},{48,176},{64,96},{80,208},{96,0},{112,240}... | collective-permute-start | bytes 1572872 | tf_op jit(solution)/shard_map/ppermute | solution.py:94
  63.4 17.2 %collective-permute-start = (bf16[128,2048]{1,0:T(8,128)(2,1)}, bf16[128,2048]{1,0:T(8,128)(2,1)}, u32[]{:S(2)}, u32[]{:S(2)}) collective-permute-start(bf16[128,2048]{1,0:T(8,128)(2,1)} %bitcast.18), channel_id=1, source_target_pairs={{0,16},{16,0},{32,48},{48,32},{64,80},{80,64},{96,112},{112,96},{1... | collective-permute-start | bytes 1572872 | tf_op jit(solution)/shard_map/ppermute | solution.py:106
  68.1 12.5 %collective-permute-start.5 = (bf16[2,16,64,128]{3,2,1,0:T(8,128)(2,1)S(1)}, bf16[2,16,64,128]{3,2,1,0:T(8,128)(2,1)}, u32[]{:S(2)}, u32[]{:S(2)}) collective-permute-start(bf16[2,16,64,128]{3,2,1,0:T(8,128)(2,1)S(1)} %pad_maximum_fusion.1.refs_1_), channel_id=1, source_target_pairs={{0,32},{16,144},{32,64},{48,176},{64,96},{80,208},{96,0},{112,240}... | collective-permute-start | bytes 1572872 | tf_op jit(solution)/shard_map/ppermute | solution.py:94
  70.0 10.7 %collective-permute-start.9 = (bf16[2,16,64,128]{3,2,1,0:T(8,128)(2,1)S(1)}, bf16[2,16,64,128]{3,2,1,0:T(8,128)(2,1)}, u32[]{:S(2)}, u32[]{:S(2)}) collective-permute-start(bf16[2,16,64,128]{3,2,1,0:T(8,128)(2,1)S(1)} %pad_maximum_fusion.refs_0_), channel_id=1, source_target_pairs={{0,96},{16,400},{32,0},{48,432},{64,32},{80,464},{96,64},{112,496}... | collective-permute-start | bytes 1572872 | tf_op jit(solution)/shard_map/ppermute | solution.py:94
  74.6 11.7 %collective-permute-start.8 = (bf16[2,16,64,128]{3,2,1,0:T(8,128)(2,1)S(1)}, bf16[2,16,64,128]{3,2,1,0:T(8,128)(2,1)}, u32[]{:S(2)}, u32[]{:S(2)}) collective-permute-start(bf16[2,16,64,128]{3,2,1,0:T(8,128)(2,1)S(1)} %collective-permute-done.7.refs_7_), channel_id=1, source_target_pairs={{0,96},{16,400},{32,0},{48,432},{64,32},{80,464},{96,64},{112,496}... | collective-permute-start | bytes 1572872 | tf_op jit(solution)/shard_map/ppermute | solution.py:94
  76.6 11.5 %collective-permute-start.6 = (bf16[2,16,64,128]{3,2,1,0:T(8,128)(2,1)S(1)}, bf16[2,16,64,128]{3,2,1,0:T(8,128)(2,1)}, u32[]{:S(2)}, u32[]{:S(2)}) collective-permute-start(bf16[2,16,64,128]{3,2,1,0:T(8,128)(2,1)S(1)} %collective-permute-done.4.refs_2_), channel_id=1, source_target_pairs={{0,32},{16,144},{32,64},{48,176},{64,96},{80,208},{96,0},{112,240}... | collective-permute-start | bytes 1572872 | tf_op jit(solution)/shard_map/ppermute | solution.py:94
  92.6 6.8 %collective-permute-start.10 = (f32[16,128,128]{2,1,0:T(8,128)S(1)}, f32[16,128,128]{2,1,0:T(8,128)S(1)}, u32[]{:S(2)}, u32[]{:S(2)}) collective-permute-start(f32[16,128,128]{2,1,0:T(8,128)S(1)} %get-tuple-element.7), channel_id=1, source_target_pairs={{0,16},{16,0},{32,48},{48,32},{64,80},{80,64},{96,112},{112,96},{1... | collective-permute-start | bytes 3145736 | tf_op jit(solution)/shard_map/ppermute | solution.py:106
  100.3 34.6 %all-to-all-start.1 = ((bf16[16,128,128]{2,1,0:T(8,128)(2,1)}), bf16[16,128,128]{2,1,0:T(8,128)(2,1)}, u32[]{:S(2)}, u32[]{:S(2)}) async-start(bf16[16,128,128]{2,1,0:T(8,128)(2,1)} %add_convert_fusion), calls=%async_computation.1 | async-start | bytes 1048576 | tf_op jit(solution)/shard_map/all_to_all | solution.py:399
  147.3 62.3 %all-to-all-start.3 = ((bf16[16,128,128]{2,1,0:T(8,128)(2,1)}), bf16[16,128,128]{2,1,0:T(8,128)(2,1)S(1)}, u32[]{:S(2)}, u32[]{:S(2)}) async-start(bf16[16,128,128]{2,1,0:T(8,128)(2,1)} %bitcast.22), calls=%async_computation.3 | async-start | bytes 1048576 | tf_op jit(solution)/shard_map/all_to_all | solution.py:399
  160.2 34.5 %collective-permute-start.12 = (bf16[2,16,64,128]{3,2,1,0:T(8,128)(2,1)S(1)}, bf16[2,16,64,128]{3,2,1,0:T(8,128)(2,1)S(1)}, u32[]{:S(2)}, u32[]{:S(2)}) collective-permute-start(bf16[2,16,64,128]{3,2,1,0:T(8,128)(2,1)S(1)} %pad_maximum_fusion.1.refs_1_), channel_id=1, source_target_pairs={{0,16},{16,0},{32,48},{48,32},{64,80},{80,64},{96,112},{112,96},{1... | collective-permute-start | bytes 1572872 | tf_op jit(solution)/shard_map/ppermute | solution.py:106
  162.9 33.8 %collective-permute-start.11 = (bf16[2,16,64,128]{3,2,1,0:T(8,128)(2,1)S(1)}, bf16[2,16,64,128]{3,2,1,0:T(8,128)(2,1)S(1)}, u32[]{:S(2)}, u32[]{:S(2)}) collective-permute-start(bf16[2,16,64,128]{3,2,1,0:T(8,128)(2,1)S(1)} %pad_maximum_fusion.refs_0_), channel_id=1, source_target_pairs={{0,16},{16,0},{32,48},{48,32},{64,80},{80,64},{96,112},{112,96},{1... | collective-permute-start | bytes 1572872 | tf_op jit(solution)/shard_map/ppermute | solution.py:106
  164.8 35.1 %collective-permute-start.18 = (bf16[2,16,64,128]{3,2,1,0:T(8,128)(2,1)S(1)}, bf16[2,16,64,128]{3,2,1,0:T(8,128)(2,1)S(1)}, u32[]{:S(2)}, u32[]{:S(2)}) collective-permute-start(bf16[2,16,64,128]{3,2,1,0:T(8,128)(2,1)S(1)} %collective-permute-done.7.refs_7_), channel_id=1, source_target_pairs={{0,16},{16,0},{32,48},{48,32},{64,80},{80,64},{96,112},{112,96},{1... | collective-permute-start | bytes 1572872 | tf_op jit(solution)/shard_map/ppermute | solution.py:106
  186.4 16.2 %collective-permute-start.23 = (f32[1,128]{1,0:T(1,128)S(1)}, f32[1,128]{1,0:T(1,128)S(1)}, u32[]{:S(2)}, u32[]{:S(2)}) collective-permute-start(f32[1,128]{1,0:T(1,128)S(1)} %add.44), channel_id=1, source_target_pairs={{0,256},{16,272},{32,288},{48,304},{64,320},{80,336},{96,352},{112... | collective-permute-start | bytes 1544 | tf_op jit(solution)/shard_map/ppermute | solution.py:393
  190.0 15.5 %collective-permute-start.14 = (bf16[2,16,64,128]{3,2,1,0:T(8,128)(2,1)}, bf16[2,16,64,128]{3,2,1,0:T(8,128)(2,1)S(1)}, u32[]{:S(2)}, u32[]{:S(2)}) collective-permute-start(bf16[2,16,64,128]{3,2,1,0:T(8,128)(2,1)} %collective-permute-done.5.refs_3_), channel_id=1, source_target_pairs={{0,16},{16,0},{32,48},{48,32},{64,80},{80,64},{96,112},{112,96},{1... | collective-permute-start | bytes 1572872 | tf_op jit(solution)/shard_map/ppermute | solution.py:106
  194.7 11.6 %collective-permute-start.13 = (bf16[2,16,64,128]{3,2,1,0:T(8,128)(2,1)S(1)}, bf16[2,16,64,128]{3,2,1,0:T(8,128)(2,1)S(1)}, u32[]{:S(2)}, u32[]{:S(2)}) collective-permute-start(bf16[2,16,64,128]{3,2,1,0:T(8,128)(2,1)S(1)} %collective-permute-done.4.refs_2_), channel_id=1, source_target_pairs={{0,16},{16,0},{32,48},{48,32},{64,80},{80,64},{96,112},{112,96},{1... | collective-permute-start | bytes 1572872 | tf_op jit(solution)/shard_map/ppermute | solution.py:106
  197.5 9.7 %collective-permute-start.17 = (bf16[2,16,64,128]{3,2,1,0:T(8,128)(2,1)}, bf16[2,16,64,128]{3,2,1,0:T(8,128)(2,1)S(1)}, u32[]{:S(2)}, u32[]{:S(2)}) collective-permute-start(bf16[2,16,64,128]{3,2,1,0:T(8,128)(2,1)} %collective-permute-done.9.refs_6_), channel_id=1, source_target_pairs={{0,16},{16,0},{32,48},{48,32},{64,80},{80,64},{96,112},{112,96},{1... | collective-permute-start | bytes 1572872 | tf_op jit(solution)/shard_map/ppermute | solution.py:106
  200.7 7.3 %collective-permute-start.16 = (bf16[2,16,64,128]{3,2,1,0:T(8,128)(2,1)}, bf16[2,16,64,128]{3,2,1,0:T(8,128)(2,1)S(1)}, u32[]{:S(2)}, u32[]{:S(2)}) collective-permute-start(bf16[2,16,64,128]{3,2,1,0:T(8,128)(2,1)} %collective-permute-done.8.refs_5_), channel_id=1, source_target_pairs={{0,16},{16,0},{32,48},{48,32},{64,80},{80,64},{96,112},{112,96},{1... | collective-permute-start | bytes 1572872 | tf_op jit(solution)/shard_map/ppermute | solution.py:106
  202.6 6.2 %collective-permute-start.15 = (bf16[2,16,64,128]{3,2,1,0:T(8,128)(2,1)}, bf16[2,16,64,128]{3,2,1,0:T(8,128)(2,1)S(1)}, u32[]{:S(2)}, u32[]{:S(2)}) collective-permute-start(bf16[2,16,64,128]{3,2,1,0:T(8,128)(2,1)} %collective-permute-done.6.refs_4_), channel_id=1, source_target_pairs={{0,16},{16,0},{32,48},{48,32},{64,80},{80,64},{96,112},{112,96},{1... | collective-permute-start | bytes 1572872 | tf_op jit(solution)/shard_map/ppermute | solution.py:106
  (19 other events, 32.5 us)
